TPU v7x, 256 devices: a whole 4x4x8 slice. The times are simulated.
256 devices in a mesh: row: 16 (over z, core), col: 16 (over x, y).
Axes of the slice: x: 4, y: 4, z: 8, core: 2. Of those that a mesh axis runs over, the one named last changes fastest.
Arguments:
- panel: float32 [16384, 128], P(('row', 'col')), as said below
- mobility: float32 [16384, 16384], P('row', 'col'), as said below
Outputs:
- updated: float32 [16384, 16384], P('row', 'col')
- panel_factor: float32 [128, 128], replicated
Inputs may be any that keep to these rules, and one draw needn't show every extreme that they name: Each row and each column of the panel has its own scale. `mobility`: Symmetric.
All inputs are finite; a program needn't handle non-finite values.
Results may differ from a plain program's by a relative error of at most 0.000076.
Values sent between devices are 32-bit elements; how exact they have to be, the bound alone decides.
No kernel may reach another device: no remote copies, remote signals or barrier semaphores. Data moves between devices by JAX's collectives and lax.ppermute only.
A program may use at most 64 MiB of HBM per device.

v0:
```python
import jax
import jax.numpy as jnp
from jax import lax
from jax.sharding import PartitionSpec as P


def spread(shard, axis, root):
    mine = lax.axis_index(axis) == root
    return lax.psum(jnp.where(mine, shard, jnp.zeros_like(shard)), axis)


def product(first_op, second_op):
    return jnp.dot(
        first_op, second_op, precision=lax.Precision.HIGHEST, preferred_element_type=jnp.float32
    )


def product_tn(first_op, second_op):
    return lax.dot_general(
        first_op,
        second_op,
        (((0,), (0,)), ((), ())),
        precision=lax.Precision.HIGHEST,
        preferred_element_type=jnp.float32,
    )


def product_nt(first_op, second_op):
    return lax.dot_general(
        first_op,
        second_op,
        (((1,), (1,)), ((), ())),
        precision=lax.Precision.HIGHEST,
        preferred_element_type=jnp.float32,
    )


def invert_core(core_matrix):
    identity = jnp.eye(core_matrix.shape[0], dtype=jnp.float32)

    def newton_step(index, approx):
        return product(approx, 2.0 * identity - product(core_matrix, approx))

    return lax.fori_loop(0, 12, newton_step, identity)


def correction_columns(block_rows_arr, block_ratio):
    root_index = lax.axis_index("col") * block_ratio + 0
    copies = spread(block_rows_arr, "row", root_index)
    return copies


def on_device(panel, mobility):
    piece_rows = panel.shape[0]
    width_cols = panel.shape[1]
    count_col = lax.axis_size("col")
    count_row = lax.axis_size("row")
    block_ratio = count_row // count_col
    row_index = lax.axis_index("row")
    col_index = lax.axis_index("col")
    block_rows = mobility.shape[0]
    block_cols = mobility.shape[1]
    first_row = (row_index * count_col + col_index) * piece_rows
    positions = first_row + jnp.arange(piece_rows, dtype=jnp.int32)
    selector = (jnp.arange(width_cols, dtype=jnp.int32)[:, None] == positions[None, :]).astype(
        jnp.float32
    )
    gram_term = product_tn(panel, panel)
    top_term = product(selector, panel)
    gram_sum, top_rows = lax.psum((gram_term, top_term), ("row", "col"))
    lower_factor = jnp.linalg.cholesky(gram_sum)
    panel_factor = lower_factor.T
    ortho_piece = jax.scipy.linalg.solve_triangular(lower_factor, panel.T, lower=True).T
    basis_piece = ortho_piece + selector.T
    top_ortho = jax.scipy.linalg.solve_triangular(lower_factor, top_rows.T, lower=True)
    core_matrix = jnp.eye(width_cols, dtype=jnp.float32) + top_ortho
    kernel = invert_core(core_matrix)
    everything = lax.all_gather(basis_piece, ("row", "col"), axis=0, tiled=True)
    basis_rows = lax.dynamic_slice_in_dim(everything, row_index * block_rows, block_rows, 0)
    basis_cols = lax.dynamic_slice_in_dim(everything, col_index * block_cols, block_cols, 0)
    partial_rows = product(mobility, basis_cols)
    spread_rows = product(lax.psum(partial_rows, "col"), kernel)
    inner_sum = lax.psum(product_tn(basis_rows, spread_rows), "row")
    inner = product_tn(kernel, inner_sum)
    correction_rows = spread_rows - 0.5 * product(basis_rows, inner)
    correction_cols = correction_columns(correction_rows, block_ratio)
    left_side = jnp.concatenate([basis_rows, correction_rows], axis=1)
    right_side = jnp.concatenate([correction_cols, basis_cols], axis=1)
    updated = mobility - product_nt(left_side, right_side)
    return (updated, panel_factor)


def solution(mesh):
    in_specs = (P(("row", "col"), None), P("row", "col"))
    out_specs = (P("row", "col"), P())
    return jax.shard_map(
        on_device, mesh=mesh, in_specs=in_specs, out_specs=out_specs, check_vma=False
    )
```

profile of v0, /device:TPU:1, one launch (start us, length us, event | category | flops | bytes accessed | tf_op | source)
XLA Modules:
  0.0 727.7 jit_solution(3753922273948830282)
XLA Ops:
  7.2 0.0 copy-start
  7.2 0.0 all-reduce.12.cloned.1.call-start
  7.2 0.7 copy-done
  7.9 0.9 fusion.18
  8.8 0.8 fusion.14
  9.6 0.0 all-reduce.12.cloned.1.call-update
  9.7 0.0 all-gather.2.cloned.1.call-start
  9.7 249.4 %all-reduce.12.cloned.1.call-done = (f32[128,128]{0,1:T(8,128)}, f32[128,128]{1,0:T(8,128)}) async-done(((f32[128,128]{0,1:T(8,128)}, f32[128,128]{1,0:T(8,128)}), (f32[128,128]{0,1:T(8,128)}, f32[128,128]{1,0:T(8,128)})) %all-reduce.12.cloned.1.call-update) | async-done | bytes 131088 | tf_op jit(solution)/shard_map/psum | solution.py:70
  259.1 0.9 copy.5
  260.0 0.9 fusion.12
  260.9 11.7 %cholesky.19 = f32[128,128]{1,0:T(8,128)S(1)} custom-call(f32[128,128]{1,0:T(8,128)S(1)} %fusion.12), custom_call_target="Cholesky" | custom-call | tf_op jit(solution)/shard_map/jit(cholesky)/cholesky | solution.py:71
  272.6 0.6 compare_reduce_fusion
  273.3 0.7 fusion.15
  273.9 9.8 %custom-call.10 = f32[1,128,128]{1,2,0:T(8,128)S(1)} custom-call(f32[1,128,128]{2,1,0:T(8,128)S(1)} %get-tuple-element.49), custom_call_target="InvertDiagBlocksLowerTriangular" | custom-call | tf_op jit(solution)/shard_map/jit(_solve_triangular)/triangular_solve | solution.py:73
  283.8 0.8 fusion.3
  284.6 0.0 all-gather.2.cloned.1.call-update
  284.6 0.0 all-reduce.6.cloned.1.call-start
  284.7 0.1 copy.6
  284.7 1.1 convolution_add_fusion
  285.9 115.3 %all-gather.2.cloned.1.call-done = f32[16384,128]{1,0:T(8,128)} async-done(((f32[64,128]{1,0:T(8,128)}), f32[16384,128]{1,0:T(8,128)}) %all-gather.2.cloned.1.call-update) | async-done | bytes 8388624 | tf_op jit(solution)/shard_map/all_gather | solution.py:78
  401.2 1.3 constant_dynamic-slice_fusion.1
  402.5 7.5 %convolution_bitcast_fusion.1 = f32[1024,128]{0,1:T(8,128)} fusion(f32[1024,128]{1,0:T(8,128)S(1)} %get-tuple-element.47, f32[1024,1024]{1,0:T(8,128)} %param.5), kind=kOutput, calls=%fused_computation.7 | convolution fusion | flops 1610612736 | bytes 5242880 | tf_op jit(solution)/shard_map/dot_general | solution.py:13
  409.9 0.0 all-reduce.6.cloned.1.call-update
  410.0 0.2 all-reduce.8.cloned.1.call-start
  410.2 7.1 while.11
  410.2 0.3 convolution_subtract_fusion.3
  410.5 0.3 convolution_bitcast_fusion.4
  410.8 0.3 convolution_subtract_fusion.3
  411.1 0.3 convolution_bitcast_fusion.4
  411.4 0.3 convolution_subtract_fusion.3
  411.7 0.3 convolution_bitcast_fusion.4
  412.0 0.3 convolution_subtract_fusion.3
  412.3 0.3 convolution_bitcast_fusion.4
  412.6 0.3 convolution_subtract_fusion.3
  412.9 0.3 convolution_bitcast_fusion.4
  413.2 0.3 convolution_subtract_fusion.3
  413.5 0.3 convolution_bitcast_fusion.4
  413.8 0.3 convolution_subtract_fusion.3
  414.0 0.3 convolution_bitcast_fusion.4
  414.4 0.3 convolution_subtract_fusion.3
  414.6 0.3 convolution_bitcast_fusion.4
  415.0 0.3 convolution_subtract_fusion.3
  415.2 0.3 convolution_bitcast_fusion.4
  415.6 0.3 convolution_subtract_fusion.3
  415.8 0.3 convolution_bitcast_fusion.4
  416.1 0.3 convolution_subtract_fusion.3
  416.4 0.3 convolution_bitcast_fusion.4
  416.7 0.3 convolution_subtract_fusion.3
  417.0 0.3 convolution_bitcast_fusion.4
  417.3 83.1 %all-reduce.6.cloned.1.call-done = f32[1024,128]{0,1:T(8,128)} async-done(((f32[1024,128]{0,1:T(8,128)}), f32[1024,128]{0,1:T(8,128)}) %all-reduce.6.cloned.1.call-update) | async-done | bytes 524304 | tf_op jit(solution)/shard_map/psum | solution.py:82
  500.4 1.6 fusion.19
  502.1 1.6 fusion.20
  503.7 0.0 all-reduce.8.cloned.1.call-update
  503.7 0.0 all-reduce.10.cloned.1.call-start
  503.8 0.2 copy.8
  504.0 99.9 %all-reduce.8.cloned.1.call-done = f32[128,128]{1,0:T(8,128)} async-done(((f32[128,128]{1,0:T(8,128)}), f32[128,128]{1,0:T(8,128)}) %all-reduce.8.cloned.1.call-update) | async-done | bytes 65552 | tf_op jit(solution)/shard_map/psum | solution.py:83
  603.9 1.0 fusion.21
  604.9 1.4 broadcast_select_fusion
  606.3 0.0 all-reduce.10.cloned.1.call-update
  606.3 0.7 copy.9
  607.1 107.4 %all-reduce.10.cloned.1.call-done = f32[1024,128]{1,0:T(8,128)} async-done(((f32[1024,128]{1,0:T(8,128)}), f32[1024,128]{1,0:T(8,128)}) %all-reduce.10.cloned.1.call-update) | async-done | bytes 524304 | tf_op jit(solution)/shard_map/psum | solution.py:9
  714.4 6.7 convolution_subtract_fusion.1
  (15 shorter events, 0.1 us)
Async XLA Ops:
  7.2 0.8 copy-start
  7.2 251.9 %all-reduce.12.cloned.1.call-start = ((), (), s32[]{:S(2)}) async-start(), calls=%async_computation.4 | async-start | bytes 262144 | tf_op jit(solution)/shard_map/psum | solution.py:70
  9.7 391.5 %all-gather.2.cloned.1.call-start = ((), (), s32[]{:S(2)}) async-start(), calls=%async_computation | async-start | bytes 8421376 | tf_op jit(solution)/shard_map/all_gather | solution.py:78
  284.6 215.8 %all-reduce.6.cloned.1.call-start = ((), (), s32[]{:S(2)}) async-start(), calls=%async_computation.1 | async-start | bytes 1048576 | tf_op jit(solution)/shard_map/psum | solution.py:82
  410.0 193.9 %all-reduce.8.cloned.1.call-start = ((), (), s32[]{:S(2)}) async-start(), calls=%async_computation.2 | async-start | bytes 131072 | tf_op jit(solution)/shard_map/psum | solution.py:83
  503.7 210.7 %all-reduce.10.cloned.1.call-start = ((), (), s32[]{:S(2)}) async-start(), calls=%async_computation.3 | async-start | bytes 1048576 | tf_op jit(solution)/shard_map/psum | solution.py:9
Sparse Core Ops, SparseCore 0:
  14.2 244.8 all-reduce.11
  284.7 116.4 all-gather.1
  410.1 90.2 all-reduce.5
  503.8 99.9 all-reduce.7
  606.6 107.7 all-reduce.9
where the time goes:
time: 728 us
  waiting for transfers between devices  655 us (90%)
  matrix products  30.2 us (4%)
  other arithmetic  23.7 us (3%)
  between operations  13.9 us (2%)
    psum x1, waiting for transfers between devices, on_device(): gram_sum, top_rows = lax.psum((gram_term, top_term), ('row', 'col'))  249 us
    all_gather x1, waiting for transfers between devices, on_device(): everything = lax.all_gather(basis_piece, ('row', 'col'), axis=0, tiled=True)  115 us
    psum x1, waiting for transfers between devices, spread(): return lax.psum(jnp.where(mine, shard, jnp.zeros_like(shard)), axis)  107 us
    psum x1, waiting for transfers between devices, on_device(): inner_sum = lax.psum(product_tn(basis_rows, spread_rows), 'row')  99.9 us
    psum x1, waiting for transfers between devices, on_device(): spread_rows = product(lax.psum(partial_rows, 'col'), kernel)  83.1 us
    dot_general x28, matrix products, product(): jnp.dot(first_op, second_op, precision=lax.Precision.HIGHEST, preferred_e...  17.9 us
  transfers between devices with their start and end apart: 5, of which 5 were waited for; matrix products, arithmetic and copies ran while one was open for 1% of the time, Pallas kernels for 0%

commit v1 on v0

v1 whole, which is shorter than its diff:
```python
import jax
import jax.numpy as jnp
from jax import lax
from jax.sharding import PartitionSpec as P

BOTH = ("row", "col")


def product(first_op, second_op):
    return jnp.dot(
        first_op, second_op, precision=lax.Precision.HIGHEST, preferred_element_type=jnp.float32
    )


def product_tn(first_op, second_op):
    return lax.dot_general(
        first_op,
        second_op,
        (((0,), (0,)), ((), ())),
        precision=lax.Precision.HIGHEST,
        preferred_element_type=jnp.float32,
    )


def product_nt(first_op, second_op):
    return lax.dot_general(
        first_op,
        second_op,
        (((1,), (1,)), ((), ())),
        precision=lax.Precision.HIGHEST,
        preferred_element_type=jnp.float32,
    )


def invert_core(core_matrix):
    identity = jnp.eye(core_matrix.shape[0], dtype=jnp.float32)

    def newton_step(index, approx):
        return product(approx, 2.0 * identity - product(core_matrix, approx))

    return lax.fori_loop(0, 12, newton_step, identity)


def on_device(panel, mobility):
    piece, width = panel.shape
    n_row, n_col = lax.axis_size("row"), lax.axis_size("col")
    block_rows, block_cols = mobility.shape
    row, col = lax.axis_index("row"), lax.axis_index("col")
    half = row % 2
    n_z = n_row // 2
    share = width // n_col
    z_groups = [[2 * z + h for z in range(n_z)] for h in range(2)]
    pairs = [[2 * z, 2 * z + 1] for z in range(n_z)]
    transposing = [(i * n_col + j, j * n_col + i) for i in range(n_row) for j in range(n_col)]
    swap = [(i, i ^ 1) for i in range(n_row)]

    def gather_col(rows):
        return lax.all_to_all(jnp.broadcast_to(rows[None], (n_col,) + rows.shape), "col", 0, 0)

    def gather_z(rows):
        copies = jnp.broadcast_to(rows[None], (n_z,) + rows.shape)
        return lax.all_to_all(copies, "row", 0, 0, axis_index_groups=z_groups)

    def gather_pair(rows):
        return lax.all_gather(rows, "row", axis=0, axis_index_groups=pairs)

    def in_order(parts):
        return parts.reshape(2, n_z, piece, width).transpose(1, 0, 2, 3).reshape(block_rows, width)

    turned_panel = lax.ppermute(panel, BOTH, transposing)
    panel_rows = gather_col(panel).reshape(block_rows, width)
    gram_part = product_tn(panel_rows, panel_rows).reshape(2, width // 2, width)
    keep = lax.dynamic_index_in_dim(gram_part, half, 0, False)
    give = lax.dynamic_index_in_dim(gram_part, 1 - half, 0, False)
    gram_part = keep + lax.ppermute(give, "row", swap)
    top_part = lax.dynamic_slice_in_dim(panel_rows, col * share, share, 0)
    z_parts = gather_z(jnp.concatenate([turned_panel, gram_part, top_part], 0))
    gram_part = jnp.sum(z_parts[:, piece : piece + width // 2], 0)
    both = gather_pair(
        jnp.concatenate(
            [z_parts[:, :piece].reshape(n_z * piece, width), gram_part, z_parts[0, -share:]], 0
        )
    )
    panel_cols = in_order(both[:, : n_z * piece])
    gram = both[:, n_z * piece : n_z * piece + width // 2].reshape(width, width)
    top_part = both[0, -share:]

    identity = jnp.eye(width, dtype=jnp.float32)
    lower_factor = jnp.linalg.cholesky(gram)
    panel_factor = lower_factor.T
    inverse_factor = jax.scipy.linalg.solve_triangular(lower_factor, identity, lower=True)

    def unit_rows(index):
        place = index * block_rows + jnp.arange(block_rows, dtype=jnp.int32)
        return (place[:, None] == jnp.arange(width, dtype=jnp.int32)[None, :]).astype(jnp.float32)

    basis_rows = product_nt(panel_rows, inverse_factor) + unit_rows(row)
    basis_cols = product_nt(panel_cols, inverse_factor) + unit_rows(col)
    partial = product(mobility, basis_cols)
    small = product_tn(basis_rows, partial)
    sent = jnp.concatenate(
        [
            partial.reshape(n_col, piece, width),
            small.reshape(n_col, share, width),
            jnp.broadcast_to(top_part[None], (n_col, share, width)),
        ],
        1,
    )
    got = lax.all_to_all(sent, "col", 0, 0)
    image = jnp.sum(got[:, : piece + share], 0)
    turned_image = lax.ppermute(image[:piece], BOTH, transposing)
    top_rows = got[:, piece + share :].reshape(width, width)
    kernel = invert_core(identity + product_nt(inverse_factor, top_rows))
    z_parts = gather_z(jnp.concatenate([turned_image, image[piece:]], 0))
    both = gather_pair(
        jnp.concatenate(
            [z_parts[:, :piece].reshape(n_z * piece, width), jnp.sum(z_parts[:, piece:], 0)], 0
        )
    )
    image_cols = in_order(both[:, : n_z * piece])
    small = both[0, n_z * piece :] + both[1, n_z * piece :]
    col_parts = gather_col(jnp.concatenate([image[:piece], small], 0))
    image_rows = col_parts[:, :piece].reshape(block_rows, width)
    small = col_parts[:, piece:].reshape(width, width)

    half_inner = 0.5 * product_tn(kernel, product(small, kernel))
    correction_rows = product(image_rows, kernel) - product(basis_rows, half_inner)
    correction_cols = product(image_cols, kernel) - product(basis_cols, half_inner)
    left_side = jnp.concatenate([basis_rows, correction_rows], axis=1)
    right_side = jnp.concatenate([correction_cols, basis_cols], axis=1)
    updated = mobility - product_nt(left_side, right_side)
    return (updated, panel_factor)


def solution(mesh):
    in_specs = (P(("row", "col"), None), P("row", "col"))
    out_specs = (P("row", "col"), P())
    return jax.shard_map(
        on_device, mesh=mesh, in_specs=in_specs, out_specs=out_specs, check_vma=False
    )
```

time: 728 us -> 158 us (0.22)
  waiting for transfers between devices: 655 us -> 39 us
  starting transfers between devices: 0.39 us -> 40.4 us
  blocking collectives: 0 us -> 23.9 us
  between operations: 13.9 us -> 0.97 us
    psum x4 -> x0, waiting for transfers between devices: 540 us -> none  [the longest x1 249 us: on_device(): gram_sum, top_rows = lax.psum((gram_term, top_term), ('row', 'col'))]
    all_gather x1 -> x0, waiting for transfers between devices: 115 us -> none  [on_device(): everything = lax.all_gather(basis_piece, ('row', 'col'), axis=0, tiled=True)]
    all_to_all x0 -> x4, waiting for transfers between devices: none -> 36.2 us  [the longest x2 27.3 us: gather_z(): return lax.all_to_all(copies, 'row', 0, 0, axis_index_groups=z_groups)]
    all_to_all x0 -> x4, starting transfers between devices: none -> 30.1 us  [the longest x2 17.3 us: gather_z(): return lax.all_to_all(copies, 'row', 0, 0, axis_index_groups=z_groups)]
    all_to_all x0 -> x1, blocking collectives: none -> 15.8 us  [on_device(): got = lax.all_to_all(sent, 'col', 0, 0)]
    ppermute x0 -> x3, starting transfers between devices: none -> 10.3 us  [the longest x1 4.38 us: on_device(): turned_panel = lax.ppermute(panel, BOTH, transposing)]
    all_gather x0 -> x2, blocking collectives: none -> 8.07 us  [gather_pair(): return lax.all_gather(rows, 'row', axis=0, axis_index_groups=pairs)]
    dot_general x28 -> x30, matrix products: 17.9 us -> 15.9 us  [product(): jnp.dot(first_op, second_op, precision=lax.Precision.HIGHEST, preferred_e...]
  transfers between devices with their start and end apart: 5 -> 7, of which waited for: 5 -> 6; matrix products, arithmetic and copies ran while one was open for 1% -> 6% of each run, Pallas kernels for 0% -> 0%
where the time goes in v1:
time: 158 us
  starting transfers between devices  40.4 us (26%)
  waiting for transfers between devices  39 us (25%)
  matrix products  24.3 us (15%)
  blocking collectives  23.9 us (15%)
  other arithmetic  23.1 us (15%)
  local copies, waits for them, and re-layouts  5.66 us (4%)
    all_to_all x2, waiting for transfers between devices, gather_z(): return lax.all_to_all(copies, 'row', 0, 0, axis_index_groups=z_groups)  27.3 us
    all_to_all x2, starting transfers between devices, gather_z(): return lax.all_to_all(copies, 'row', 0, 0, axis_index_groups=z_groups)  17.3 us
    dot_general x30, matrix products, product(): jnp.dot(first_op, second_op, precision=lax.Precision.HIGHEST, preferred_e...  15.9 us
    all_to_all x1, blocking collectives, on_device(): got = lax.all_to_all(sent, 'col', 0, 0)  15.8 us
    all_to_all x2, starting transfers between devices, gather_col(): lax.all_to_all(jnp.broadcast_to(rows[None], (n_col,) + rows.shape), 'col'...  12.8 us
    another operation x3, other arithmetic, on_device(): lower_factor = jnp.linalg.cholesky(gram)  12.4 us
    another operation x1, other arithmetic, on_device(): jax.scipy.linalg.solve_triangular(lower_factor, identity, lower=True)  9.81 us
    all_to_all x2, waiting for transfers between devices, gather_col(): lax.all_to_all(jnp.broadcast_to(rows[None], (n_col,) + rows.shape), 'col'...  8.94 us
  transfers between devices with their start and end apart: 7, of which 6 were waited for; matrix products, arithmetic and copies ran while one was open for 6% of the time, Pallas kernels for 0%

profile of v1, /device:TPU:1, one launch (start us, length us, event | category | flops | bytes accessed | tf_op | source)
XLA Modules:
  0.0 157.7 jit_solution(17031147397252486435)
XLA Ops:
  0.6 1.6 %broadcast_in_dim.14 = f32[16,64,128]{2,1,0:T(8,128)} broadcast(f32[64,128]{1,0:T(8,128)} %param.4), dimensions={1,2} | broadcast | bytes 557056 | tf_op jit(solution)/shard_map/broadcast_in_dim | solution.py:58
  2.2 7.6 %all-to-all-start = ((f32[16,64,128]{2,1,0:T(8,128)}), f32[16,64,128]{2,1,0:T(8,128)S(1)}, u32[]{:S(2)}, u32[]{:S(2)}) async-start(f32[16,64,128]{2,1,0:T(8,128)} %broadcast_in_dim.14), calls=%async_computation | async-start | bytes 1048576 | tf_op jit(solution)/shard_map/all_to_all | solution.py:58
  9.8 4.4 %collective-permute-start = (f32[64,128]{1,0:T(8,128)}, f32[64,128]{1,0:T(8,128)S(1)}, u32[]{:S(2)}, u32[]{:S(2)}) collective-permute-start(f32[64,128]{1,0:T(8,128)} %param.4), channel_id=1, source_target_pairs={{0,0},{1,16},{2,32},{3,48},{4,64},{5,80},{6,96},{7,112},{8,128},{9... | collective-permute-start | bytes 98312 | tf_op jit(solution)/shard_map/ppermute | solution.py:70
  14.2 5.9 %all-to-all-done = f32[16,64,128]{2,1,0:T(8,128)S(1)} async-done(((f32[16,64,128]{2,1,0:T(8,128)}), f32[16,64,128]{2,1,0:T(8,128)S(1)}, u32[]{:S(2)}, u32[]{:S(2)}) %all-to-all-start) | async-done | bytes 524320 | tf_op jit(solution)/shard_map/all_to_all | solution.py:58
  20.3 0.6 fusion.18
  21.0 2.2 %collective-permute-start.1 = (f32[64,128]{1,0:T(8,128)S(1)}, f32[64,128]{1,0:T(8,128)S(1)}, u32[]{:S(2)}, u32[]{:S(2)}) collective-permute-start(f32[64,128]{1,0:T(8,128)S(1)} %dynamic-slice_bitcast_fusion), channel_id=1, source_target_pairs={{0,16},{16,0},{32,48},{48,32},{64,80},{80,64},{96,112},{112,96},{1... | collective-permute-start | bytes 98312 | tf_op jit(solution)/shard_map/ppermute | solution.py:75
  23.2 0.9 collective-permute-done.1
  24.1 0.8 broadcast_in_dim.15
  25.0 8.4 %all-to-all-start.1 = ((f32[8,136,128]{2,1,0:T(8,128)}), f32[8,136,128]{2,1,0:T(8,128)S(1)}, u32[]{:S(2)}, u32[]{:S(2)}) async-start(f32[8,136,128]{2,1,0:T(8,128)} %broadcast_in_dim.15), calls=%async_computation.1 | async-start | bytes 1114112 | tf_op jit(solution)/shard_map/all_to_all | solution.py:62
  33.4 18.6 %all-to-all-done.1 = f32[8,136,128]{2,1,0:T(8,128)S(1)} async-done(((f32[8,136,128]{2,1,0:T(8,128)}), f32[8,136,128]{2,1,0:T(8,128)S(1)}, u32[]{:S(2)}, u32[]{:S(2)}) %all-to-all-start.1) | async-done | bytes 557088 | tf_op jit(solution)/shard_map/all_to_all | solution.py:62
  52.1 2.4 %all-gather = f32[1168,128]{1,0:T(8,128)S(1)} all-gather(f32[584,128]{1,0:T(8,128)S(1)} %pad_maximum_fusion.1), channel_id=2, replica_groups={{0,16},{32,48},{64,80},{96,112},{128,144},{160,176},{192,208},{224,240}..., dimensions={0}, use_global_device_ids=true | all-gather | bytes 897024 | tf_op jit(solution)/shard_map/all_gather | solution.py:65
  54.7 11.7 %cholesky.20 = f32[128,128]{1,0:T(8,128)S(1)} custom-call(f32[128,128]{1,0:T(8,128)S(1)} %fusion.12), custom_call_target="Cholesky" | custom-call | tf_op jit(solution)/shard_map/jit(cholesky)/cholesky | solution.py:89
  66.4 0.6 compare_reduce_fusion
  67.1 0.7 fusion.14
  67.7 9.8 %custom-call.7 = f32[1,128,128]{1,2,0:T(8,128)S(1)} custom-call(f32[1,128,128]{2,1,0:T(8,128)S(1)} %get-tuple-element.57), custom_call_target="InvertDiagBlocksLowerTriangular" | custom-call | tf_op jit(solution)/shard_map/jit(_solve_triangular)/triangular_solve | solution.py:91
  77.6 0.2 fusion.10
  77.8 0.6 fusion.2
  78.4 0.6 convolution_add_fusion
  79.1 6.5 %fusion.19 = f32[128,1024]{1,0:T(8,128)S(1)} fusion(f32[1024,128]{0,1:T(8,128)S(1)} %convolution_add_fusion, f32[1024,1024]{1,0:T(8,128)} %param.5), kind=kOutput, calls=%fused_computation.57 | convolution fusion | flops 1610612736 | bytes 5242880 | tf_op jit(solution)/shard_map/dot_general | solution.py:10
  85.6 0.6 convolution_bitcast_fusion.2
  86.5 15.8 %all_to_all.25 = f32[16,80,128]{2,1,0:T(8,128)S(1)} all-to-all(f32[16,80,128]{2,1,0:T(8,128)S(1)} %pad_maximum_fusion), channel_id=1, replica_groups=mesh['row'=16,'col'=16] {'col'}, dimensions={0} | all-to-all | bytes 1310720 | tf_op jit(solution)/shard_map/all_to_all | solution.py:109
  102.3 3.7 %collective-permute-start.2 = (f32[64,128]{1,0:T(8,128)S(1)}, f32[64,128]{1,0:T(8,128)S(1)}, u32[]{:S(2)}, u32[]{:S(2)}) collective-permute-start(f32[64,128]{1,0:T(8,128)S(1)} %slice.88), channel_id=1, source_target_pairs={{0,0},{1,16},{2,32},{3,48},{4,64},{5,80},{6,96},{7,112},{8,128},{9... | collective-permute-start | bytes 98312 | tf_op jit(solution)/shard_map/ppermute | solution.py:111
  106.1 1.9 %collective-permute-done.2 = f32[64,128]{1,0:T(8,128)S(1)} collective-permute-done((f32[64,128]{1,0:T(8,128)S(1)}, f32[64,128]{1,0:T(8,128)S(1)}, u32[]{:S(2)}, u32[]{:S(2)}) %collective-permute-start.2) | collective-permute-done | bytes 32800 | tf_op jit(solution)/shard_map/ppermute | solution.py:111
  108.0 0.7 broadcast_in_dim.18
  108.8 8.8 %all-to-all-start.3 = ((f32[8,72,128]{2,1,0:T(8,128)}), f32[8,72,128]{2,1,0:T(8,128)S(1)}, u32[]{:S(2)}, u32[]{:S(2)}) async-start(f32[8,72,128]{2,1,0:T(8,128)} %broadcast_in_dim.18), calls=%async_computation.3 | async-start | bytes 589824 | tf_op jit(solution)/shard_map/all_to_all | solution.py:62
  117.7 0.7 copy.22
  118.4 0.3 convolution_add_fusion.1
  118.7 8.7 %all-to-all-done.3 = f32[8,72,128]{2,1,0:T(8,128)S(1)} async-done(((f32[8,72,128]{2,1,0:T(8,128)}), f32[8,72,128]{2,1,0:T(8,128)S(1)}, u32[]{:S(2)}, u32[]{:S(2)}) %all-to-all-start.3) | async-done | bytes 294944 | tf_op jit(solution)/shard_map/all_to_all | solution.py:62
  127.4 5.7 %all-gather.1 = f32[1040,128]{1,0:T(8,128)S(1)} all-gather(f32[520,128]{1,0:T(8,128)S(1)} %pad_maximum_fusion.2), channel_id=3, replica_groups={{0,16},{32,48},{64,80},{96,112},{128,144},{160,176},{192,208},{224,240}..., dimensions={0}, use_global_device_ids=true | all-gather | bytes 798720 | tf_op jit(solution)/shard_map/all_gather | solution.py:65
  133.2 0.9 broadcast_in_dim.19
  134.0 5.2 %all-to-all-start.4 = ((f32[16,72,128]{2,1,0:T(8,128)}), f32[16,72,128]{2,1,0:T(8,128)S(1)}, u32[]{:S(2)}, u32[]{:S(2)}) async-start(f32[16,72,128]{2,1,0:T(8,128)} %broadcast_in_dim.19), calls=%async_computation.4 | async-start | bytes 1179648 | tf_op jit(solution)/shard_map/all_to_all | solution.py:58
  139.2 7.1 %while.11 = (s32[]{:T(128)}, f32[128,128]{0,1:T(8,128)S(1)}, f32[128,128]{1,0:T(8,128)S(1)}, s32[]{:T(128)}) while((s32[]{:T(128)}, f32[128,128]{0,1:T(8,128)S(1)}, f32[128,128]{1,0:T(8,128)S(1)}, s32[]{:T(128)}) %tuple.33), condition=%wide.region_6.7_spmd.clone, body=%wide.region_5.6_spmd.clone.sunk | while | flops 50380800 | bytes 524341 | solution.py:41
  139.2 0.3 convolution_subtract_fusion.5
  139.5 0.3 convolution_bitcast_fusion.4
  139.8 0.3 convolution_subtract_fusion.5
  140.1 0.3 convolution_bitcast_fusion.4
  140.4 0.3 convolution_subtract_fusion.5
  140.7 0.3 convolution_bitcast_fusion.4
  141.0 0.3 convolution_subtract_fusion.5
  141.3 0.3 convolution_bitcast_fusion.4
  141.6 0.3 convolution_subtract_fusion.5
  141.9 0.3 convolution_bitcast_fusion.4
  142.2 0.3 convolution_subtract_fusion.5
  142.5 0.3 convolution_bitcast_fusion.4
  142.8 0.3 convolution_subtract_fusion.5
  143.1 0.3 convolution_bitcast_fusion.4
  143.4 0.3 convolution_subtract_fusion.5
  143.6 0.3 convolution_bitcast_fusion.4
  144.0 0.3 convolution_subtract_fusion.5
  144.2 0.3 convolution_bitcast_fusion.4
  144.6 0.3 convolution_subtract_fusion.5
  144.8 0.3 convolution_bitcast_fusion.4
  145.2 0.3 convolution_subtract_fusion.5
  145.4 0.3 convolution_bitcast_fusion.4
  145.8 0.3 convolution_subtract_fusion.5
  146.0 0.3 convolution_bitcast_fusion.4
  146.4 0.6 fusion.21
  147.0 3.1 %all-to-all-done.4 = f32[16,72,128]{2,1,0:T(8,128)S(1)} async-done(((f32[16,72,128]{2,1,0:T(8,128)}), f32[16,72,128]{2,1,0:T(8,128)S(1)}, u32[]{:S(2)}, u32[]{:S(2)}) %all-to-all-start.4) | async-done | bytes 589856 | tf_op jit(solution)/shard_map/all_to_all | solution.py:58
  150.1 0.3 fusion.9
  150.4 0.2 convolution_multiply_fusion
  150.6 0.6 fusion.20
  151.2 0.6 convolution_subtract_fusion.2
  151.9 0.6 convolution_subtract_fusion.3
  152.5 5.2 %convolution_subtract_fusion.1 = f32[1024,1024]{1,0:T(8,128)} fusion(f32[1024,1024]{1,0:T(8,128)S(1)} %copy-done, f32[1024,128]{0,1:T(8,128)S(1)} %convolution_subtract_fusion.3, f32[1024,128]{0,1:T(8,128)S(1)} %fusion.2, f32[1024,128]{0,1:T(8,128)S(1)} %convolution_add_fusion, f32[1024,128]{0,1:T(8,128)S(1)} %convolution_subtract_fusion.2), kind=kOutput, calls=%fused_computation.4 | convolution fusion | flops 3222798336 | bytes 10485760 | tf_op jit(solution)/shard_map/dot_general | solution.py:26
  (49 shorter events, 1.2 us)
Async XLA Ops:
  2.2 17.9 %all-to-all-start = ((f32[16,64,128]{2,1,0:T(8,128)}), f32[16,64,128]{2,1,0:T(8,128)S(1)}, u32[]{:S(2)}, u32[]{:S(2)}) async-start(f32[16,64,128]{2,1,0:T(8,128)} %broadcast_in_dim.14), calls=%async_computation | async-start | bytes 1048576 | tf_op jit(solution)/shard_map/all_to_all | solution.py:58
  9.8 14.3 %collective-permute-start = (f32[64,128]{1,0:T(8,128)}, f32[64,128]{1,0:T(8,128)S(1)}, u32[]{:S(2)}, u32[]{:S(2)}) collective-permute-start(f32[64,128]{1,0:T(8,128)} %param.4), channel_id=1, source_target_pairs={{0,0},{1,16},{2,32},{3,48},{4,64},{5,80},{6,96},{7,112},{8,128},{9... | collective-permute-start | bytes 98312 | tf_op jit(solution)/shard_map/ppermute | solution.py:70
  21.0 3.1 %collective-permute-start.1 = (f32[64,128]{1,0:T(8,128)S(1)}, f32[64,128]{1,0:T(8,128)S(1)}, u32[]{:S(2)}, u32[]{:S(2)}) collective-permute-start(f32[64,128]{1,0:T(8,128)S(1)} %dynamic-slice_bitcast_fusion), channel_id=1, source_target_pairs={{0,16},{16,0},{32,48},{48,32},{64,80},{80,64},{96,112},{112,96},{1... | collective-permute-start | bytes 98312 | tf_op jit(solution)/shard_map/ppermute | solution.py:75
  25.0 27.1 %all-to-all-start.1 = ((f32[8,136,128]{2,1,0:T(8,128)}), f32[8,136,128]{2,1,0:T(8,128)S(1)}, u32[]{:S(2)}, u32[]{:S(2)}) async-start(f32[8,136,128]{2,1,0:T(8,128)} %broadcast_in_dim.15), calls=%async_computation.1 | async-start | bytes 1114112 | tf_op jit(solution)/shard_map/all_to_all | solution.py:62
  102.3 5.7 %collective-permute-start.2 = (f32[64,128]{1,0:T(8,128)S(1)}, f32[64,128]{1,0:T(8,128)S(1)}, u32[]{:S(2)}, u32[]{:S(2)}) collective-permute-start(f32[64,128]{1,0:T(8,128)S(1)} %slice.88), channel_id=1, source_target_pairs={{0,0},{1,16},{2,32},{3,48},{4,64},{5,80},{6,96},{7,112},{8,128},{9... | collective-permute-start | bytes 98312 | tf_op jit(solution)/shard_map/ppermute | solution.py:111
  108.8 18.6 %all-to-all-start.3 = ((f32[8,72,128]{2,1,0:T(8,128)}), f32[8,72,128]{2,1,0:T(8,128)S(1)}, u32[]{:S(2)}, u32[]{:S(2)}) async-start(f32[8,72,128]{2,1,0:T(8,128)} %broadcast_in_dim.18), calls=%async_computation.3 | async-start | bytes 589824 | tf_op jit(solution)/shard_map/all_to_all | solution.py:62
  134.0 16.1 %all-to-all-start.4 = ((f32[16,72,128]{2,1,0:T(8,128)}), f32[16,72,128]{2,1,0:T(8,128)S(1)}, u32[]{:S(2)}, u32[]{:S(2)}) async-start(f32[16,72,128]{2,1,0:T(8,128)} %broadcast_in_dim.19), calls=%async_computation.4 | async-start | bytes 1179648 | tf_op jit(solution)/shard_map/all_to_all | solution.py:58
  150.1 2.4 %copy-start = (f32[1024,1024]{1,0:T(8,128)S(1)}, f32[1024,1024]{1,0:T(8,128)}, u32[]{:S(2)}) copy-start(f32[1024,1024]{1,0:T(8,128)} %param.5) | copy-start | bytes 12582916

commit v2 on v0

v2 whole, which is shorter than its diff:
```python
import jax
import jax.numpy as jnp
from jax import lax
from jax.experimental import pallas as pl
from jax.experimental.pallas import tpu as pltpu
from jax.sharding import PartitionSpec as P

BOTH = ("row", "col")
STEP = 8
NN = (((1,), (0,)), ((), ()))
TN = (((0,), (0,)), ((), ()))
NT = (((1,), (1,)), ((), ()))


def product(first_op, second_op, dims=NN):
    return lax.dot_general(
        first_op,
        second_op,
        dims,
        precision=lax.Precision.HIGHEST,
        preferred_element_type=jnp.float32,
    )


def split(value):
    high = value.astype(jnp.bfloat16)
    return high, (value - high.astype(jnp.float32)).astype(jnp.bfloat16)


def left_terms(value):
    high, low = split(value)
    return jnp.concatenate([high, low, high], 1)


def right_terms(value):
    high, low = split(value)
    return jnp.concatenate([high, high, low], 1)


def exact_dot(first_op, second_op, dims):
    return lax.dot_general(first_op, second_op, dims, preferred_element_type=jnp.float32)


def unit_rows(index, shape):
    rows = lax.broadcasted_iota(jnp.int32, shape, 0) + index * shape[0]
    return jnp.where(rows == lax.broadcasted_iota(jnp.int32, shape, 1), 1.0, 0.0)


def eye(width):
    return unit_rows(0, (width, width))


def pieces_of(pairs_ref, n_z, piece):
    return jnp.concatenate(
        [pairs_ref[h, z * piece : (z + 1) * piece, :] for z in range(n_z) for h in range(2)], 0
    )


def factor_kernel(gram_ref, upper_ref, inverse_ref, work, other):
    width = gram_ref.shape[0]
    full = (STEP, width)
    lane = lax.broadcasted_iota(jnp.int32, full, 1)
    work[...] = gram_ref[...]
    other[...] = eye(width)
    for first in range(0, width, STEP):
        a_rows = [jnp.broadcast_to(work[first + k : first + k + 1, :], full) for k in range(STEP)]
        x_rows = [jnp.broadcast_to(other[first + k : first + k + 1, :], full) for k in range(STEP)]
        entry, mult, inv = {}, {}, {}
        for i in range(STEP):
            for k in range(i + 1):
                column = a_rows[i][:, first + k : first + k + 1]
                entry[i, k] = jnp.broadcast_to(column, full)
        for k in range(STEP):
            inv[k] = 1.0 / entry[k, k]
            for i in range(k + 1, STEP):
                mult[i, k] = entry[i, k] * inv[k]
            for i in range(k + 1, STEP):
                for l in range(k + 1, i + 1):
                    entry[i, l] = entry[i, l] - mult[i, k] * entry[l, k]
        for i in range(STEP):
            for k in range(i):
                a_rows[i] = a_rows[i] - mult[i, k] * a_rows[k]
                x_rows[i] = x_rows[i] - mult[i, k] * x_rows[k]
        for k in range(STEP):
            root = lax.rsqrt(entry[k, k])
            root = root * (1.5 - 0.5 * entry[k, k] * root * root)
            row = slice(first + k, first + k + 1)
            upper_ref[row, :] = jnp.where(lane >= first + k, a_rows[k] * root, 0.0)[:1]
            inverse_ref[row, :] = (x_rows[k] * root)[:1]
        if first + STEP == width:
            break
        a_back = [a_rows[k] * inv[k] for k in range(STEP)]
        x_back = [x_rows[k] * inv[k] for k in range(STEP)]
        for k in range(STEP - 2, -1, -1):
            for l in range(k + 1, STEP):
                a_back[k] = a_back[k] - mult[l, k] * a_back[l]
                x_back[k] = x_back[k] - mult[l, k] * x_back[l]
        for g in range(first + STEP, width, STEP):
            block = work[g : g + STEP, :]
            a_new, x_new = block, other[g : g + STEP, :]
            for k in range(STEP):
                column = jnp.broadcast_to(block[:, first + k : first + k + 1], full)
                a_new = a_new - column * a_back[k]
                x_new = x_new - column * x_back[k]
            work[g : g + STEP, :] = a_new
            other[g : g + STEP, :] = x_new


def factor(gram):
    width = gram.shape[0]
    shape = jax.ShapeDtypeStruct((width, width), jnp.float32)
    return pl.pallas_call(
        factor_kernel,
        out_shape=(shape, shape),
        scratch_shapes=[pltpu.VMEM((width, width), jnp.float32)] * 2,
        cost_estimate=pl.CostEstimate(
            flops=400_000_000, bytes_accessed=20_000_000, transcendentals=0
        ),
        name="factor",
    )(gram)


def partial_kernel(n_z, piece, share, place_ref, pairs_ref, mob_ref, out_ref, rhs):
    width = pairs_ref.shape[2]
    rows = mob_ref.shape[0]

    @pl.when(pl.program_id(0) == 0)
    def _():
        high, low = split(pieces_of(pairs_ref, n_z, piece))
        rhs[:, :width] = high
        rhs[:, width:] = low

    high, low = split(mob_ref[...])
    wide = exact_dot(high, rhs[...], NN)
    found = wide[:, :width] + wide[:, width:] + exact_dot(low, rhs[:, :width], NN)
    count = rows // piece
    out_ref[:, :piece, :] = found.reshape(count, piece, width)
    first = jnp.where(place_ref[1] == 0, mob_ref[:, :width], 0.0)
    out_ref[:, piece : 2 * piece, :] = first.reshape(count, piece, width)
    out_ref[:, 2 * piece :, :] = jnp.broadcast_to(
        pairs_ref[0, pairs_ref.shape[1] - share :, :][None], (count, share, width)
    )


def partial_sums(place, pairs, mobility, n_z, piece, share):
    n_rows, n_cols = mobility.shape
    width = pairs.shape[2]
    per = 2 * piece + share
    tile = 256
    return pl.pallas_call(
        lambda *refs: partial_kernel(n_z, piece, share, *refs),
        grid_spec=pltpu.PrefetchScalarGridSpec(
            num_scalar_prefetch=1,
            grid=(n_rows // tile,),
            in_specs=[
                pl.BlockSpec(pairs.shape, lambda i, p: (0, 0, 0)),
                pl.BlockSpec((tile, n_cols), lambda i, p: (i, 0)),
            ],
            out_specs=pl.BlockSpec((tile // piece, per, width), lambda i, p: (i, 0, 0)),
            scratch_shapes=[pltpu.VMEM((n_cols, 2 * width), jnp.bfloat16)],
        ),
        out_shape=jax.ShapeDtypeStruct((n_rows // piece, per, width), jnp.float32),
        cost_estimate=pl.CostEstimate(
            flops=6 * n_rows * n_cols * width, bytes_accessed=6_000_000, transcendentals=0
        ),
        name="partial_sums",
    )(place, pairs, mobility)


def image_kernel(piece, got_ref, inverse_ref, image_ref, copies_ref, top_ref):
    total = got_ref[0, : 2 * piece, :]
    for k in range(1, got_ref.shape[0]):
        total = total + got_ref[k, : 2 * piece, :]
    image = product(total[:piece], inverse_ref[...], NT) + total[piece:]
    image_ref[...] = image
    copies_ref[...] = jnp.broadcast_to(image[None], copies_ref.shape)
    top_ref[...] = got_ref[:, 2 * piece :, :].reshape(top_ref.shape)


def image_piece(got, inverse, piece):
    count, _, width = got.shape
    share = width // count
    return pl.pallas_call(
        lambda *refs: image_kernel(piece, *refs),
        out_shape=(
            jax.ShapeDtypeStruct((piece, width), jnp.float32),
            jax.ShapeDtypeStruct((count, piece, width), jnp.float32),
            jax.ShapeDtypeStruct((width, width), jnp.float32),
        ),
        cost_estimate=pl.CostEstimate(
            flops=10_000_000, bytes_accessed=2_000_000, transcendentals=0
        ),
        name="image_piece",
    )(got, inverse)


def basis_kernel(n_z, piece, place, rows_ref, pairs_ref, inverse_ref, top_ref, *outs):
    basis_rows, basis_cols, twisted, turned, kernel_ref, state_ref = outs
    width = inverse_ref.shape[0]
    inverse = inverse_ref[...]
    identity = eye(width)
    ratio = -product(inverse, top_ref[...], NT)

    state_ref[:width, :] = ratio
    state_ref[width:, :] = identity

    def go_on(state):
        return jnp.logical_and(state[0] < 40, state[1] > 1e-10)

    def double(state):
        power = state_ref[:width, :]
        both = product(state_ref[...], power)
        state_ref[:width, :] = both[:width]
        state_ref[width:, :] = state_ref[width:, :] + both[width:]
        return state[0] + 1, jnp.max(jnp.abs(both[:width]))

    lax.while_loop(go_on, double, (0, jnp.max(jnp.abs(ratio))))
    total = state_ref[width:, :]
    kernel = total + product(total, identity - product(identity - ratio, total))
    kernel_ref[...] = kernel
    inverse_terms = right_terms(inverse)
    rows = exact_dot(left_terms(rows_ref[...]), inverse_terms, NT)
    rows = rows + unit_rows(place[0], rows_ref.shape)
    basis_rows[...] = rows
    cols = exact_dot(left_terms(pieces_of(pairs_ref, n_z, piece)), inverse_terms, NT)
    basis_cols[...] = cols + unit_rows(place[1], cols.shape)
    terms = left_terms(rows)
    twisted[...] = exact_dot(terms, right_terms(kernel.T), NT)
    turned[...] = exact_dot(terms, right_terms(kernel), NT)


def bases(place, panel_rows, pairs, inverse, top_rows, n_z, piece):
    width = inverse.shape[0]
    long = jax.ShapeDtypeStruct(panel_rows.shape, jnp.float32)
    vmem = pl.BlockSpec(memory_space=pltpu.VMEM)
    return pl.pallas_call(
        lambda *refs: basis_kernel(n_z, piece, *refs),
        in_specs=[pl.BlockSpec(memory_space=pltpu.SMEM)] + [vmem] * 4,
        out_specs=[vmem] * 5,
        out_shape=(long, long, long, long, jax.ShapeDtypeStruct((width, width), jnp.float32)),
        scratch_shapes=[pltpu.VMEM((2 * width, width), jnp.float32)],
        cost_estimate=pl.CostEstimate(
            flops=300_000_000, bytes_accessed=10_000_000, transcendentals=0
        ),
        name="bases",
    )(place, panel_rows, pairs, inverse, top_rows)


def first_update_kernel(image_ref, kernel_ref, cols_ref, mob_ref, out_ref, rhs):
    @pl.when(pl.program_id(0) == 0)
    def _():
        rhs[...] = right_terms(cols_ref[...])

    spread = product(image_ref[...], kernel_ref[...])
    out_ref[...] = mob_ref[...] - exact_dot(left_terms(spread), rhs[...], NT)


def first_update(image_rows, kernel, basis_cols, mobility):
    n_rows, n_cols = mobility.shape
    width = kernel.shape[0]
    tile = 256
    return pl.pallas_call(
        first_update_kernel,
        grid=(n_rows // tile,),
        in_specs=[
            pl.BlockSpec((tile, width), lambda i: (i, 0)),
            pl.BlockSpec((width, width), lambda i: (0, 0)),
            pl.BlockSpec((n_cols, width), lambda i: (0, 0)),
            pl.BlockSpec((tile, n_cols), lambda i: (i, 0)),
        ],
        out_specs=pl.BlockSpec((tile, n_cols), lambda i: (i, 0)),
        out_shape=jax.ShapeDtypeStruct(mobility.shape, jnp.float32),
        scratch_shapes=[pltpu.VMEM((n_cols, 3 * width), jnp.bfloat16)],
        cost_estimate=pl.CostEstimate(
            flops=6 * n_rows * n_cols * width, bytes_accessed=9_000_000, transcendentals=0
        ),
        name="first_update",
    )(image_rows, kernel, basis_cols, mobility)


def last_update_kernel(n_z, piece, pairs_ref, cols_ref, turned_ref, half_ref, out_ref, rhs):
    width = cols_ref.shape[1]

    @pl.when(pl.program_id(0) == 0)
    def _():
        start = n_z * piece
        small = pairs_ref[:, start : start + width // 2, :].reshape(width, width)
        image_cols = pieces_of(pairs_ref, n_z, piece)
        rhs[...] = right_terms(image_cols - product(cols_ref[...], small))

    out_ref[...] = half_ref[...] - exact_dot(left_terms(turned_ref[...]), rhs[...], NT)


def last_update(pairs, basis_cols, turned, halfway, n_z, piece):
    n_rows, n_cols = halfway.shape
    width = basis_cols.shape[1]
    tile = 256
    return pl.pallas_call(
        lambda *refs: last_update_kernel(n_z, piece, *refs),
        grid=(n_rows // tile,),
        in_specs=[
            pl.BlockSpec(pairs.shape, lambda i: (0, 0, 0)),
            pl.BlockSpec((n_cols, width), lambda i: (0, 0)),
            pl.BlockSpec((tile, width), lambda i: (i, 0)),
            pl.BlockSpec((tile, n_cols), lambda i: (i, 0)),
        ],
        out_specs=pl.BlockSpec((tile, n_cols), lambda i: (i, 0)),
        out_shape=jax.ShapeDtypeStruct(halfway.shape, jnp.float32),
        scratch_shapes=[pltpu.VMEM((n_cols, 3 * width), jnp.bfloat16)],
        cost_estimate=pl.CostEstimate(
            flops=6 * n_rows * n_cols * width, bytes_accessed=9_000_000, transcendentals=0
        ),
        name="last_update",
    )(pairs, basis_cols, turned, halfway)


def on_device(panel, mobility):
    piece, width = panel.shape
    n_row, n_col = lax.axis_size("row"), lax.axis_size("col")
    block_rows, block_cols = mobility.shape
    row, col = lax.axis_index("row"), lax.axis_index("col")
    place = jnp.stack([row, col]).astype(jnp.int32)
    half = row % 2
    n_z = n_row // 2
    share = width // n_col
    z_groups = [[2 * z + h for z in range(n_z)] for h in range(2)]
    pairs = [[2 * z, 2 * z + 1] for z in range(n_z)]
    transposing = [(i * n_col + j, j * n_col + i) for i in range(n_row) for j in range(n_col)]
    swap = [(i, i ^ 1) for i in range(n_row)]

    def copies(rows, count):
        return jnp.broadcast_to(rows[None], (count,) + rows.shape)

    def gather_row(lone, summed, extra):
        summed = summed.reshape(2, width // 2, width)
        keep = lax.dynamic_index_in_dim(summed, half, 0, False)
        give = lax.dynamic_index_in_dim(summed, 1 - half, 0, False)
        summed = keep + lax.ppermute(give, "row", swap)
        sent = jnp.concatenate([lone, summed] + extra, 0)
        parts = lax.all_to_all(copies(sent, n_z), "row", 0, 0, axis_index_groups=z_groups)
        lone = parts[:, :piece].reshape(n_z * piece, width)
        summed = jnp.sum(parts[:, piece : piece + width // 2], 0)
        extra = [parts[0, piece + width // 2 :]] if extra else []
        sent = jnp.concatenate([lone, summed] + extra, 0)
        return lax.all_gather(sent, "row", axis=0, axis_index_groups=pairs)

    turned_panel = lax.ppermute(panel, BOTH, transposing)
    panel_rows = lax.all_to_all(copies(panel, n_col), "col", 0, 0).reshape(block_rows, width)
    gram_part = product(panel_rows, panel_rows, TN)
    top_part = lax.dynamic_slice_in_dim(panel_rows, col * share, share, 0)
    panel_pairs = gather_row(turned_panel, gram_part, [top_part])
    start = n_z * piece
    gram = panel_pairs[:, start : start + width // 2].reshape(width, width)

    sent = partial_sums(place, panel_pairs, mobility, n_z, piece, share)
    got = lax.all_to_all(sent, "col", 0, 0)
    panel_factor, inverse = factor(gram)
    image, image_copies, top_rows = image_piece(got, inverse, piece)
    turned_image = lax.ppermute(image, BOTH, transposing)
    image_rows = lax.all_to_all(image_copies, "col", 0, 0).reshape(block_rows, width)
    basis_rows, basis_cols, twisted, turned, kernel = bases(
        place, panel_rows, panel_pairs, inverse, top_rows, n_z, piece
    )
    inner_part = product(twisted, image_rows, TN)
    image_pairs = gather_row(turned_image, inner_part, [])
    halfway = first_update(image_rows, kernel, basis_cols, mobility)
    updated = last_update(image_pairs, basis_cols, turned, halfway, n_z, piece)
    return (updated, panel_factor)


def solution(mesh):
    in_specs = (P(("row", "col"), None), P("row", "col"))
    out_specs = (P("row", "col"), P())
    return jax.shard_map(
        on_device, mesh=mesh, in_specs=in_specs, out_specs=out_specs, check_vma=False
    )
```

time: 728 us -> 146 us (0.20)
  waiting for transfers between devices: 655 us -> 50.3 us
  starting transfers between devices: 0.39 us -> 46.1 us
  Pallas kernels: 0 us -> 33.3 us
  matrix products: 30.2 us -> 1.28 us
  other arithmetic: 23.7 us -> 0.79 us
  between operations: 13.9 us -> 0.8 us
    psum x4 -> x0, waiting for transfers between devices: 540 us -> none  [the longest x1 249 us: on_device(): gram_sum, top_rows = lax.psum((gram_term, top_term), ('row', 'col'))]
    all_gather x1 -> x0, waiting for transfers between devices: 115 us -> none  [on_device(): everything = lax.all_gather(basis_piece, ('row', 'col'), axis=0, tiled=True)]
    all_to_all x0 -> x5, waiting for transfers between devices: none -> 46.2 us  [the longest x2 29.3 us: gather_row(): lax.all_to_all(copies(sent, n_z), 'row', 0, 0, axis_index_groups=z_groups)]
    all_to_all x0 -> x5, starting transfers between devices: none -> 34.1 us  [the longest x2 17.7 us: gather_row(): lax.all_to_all(copies(sent, n_z), 'row', 0, 0, axis_index_groups=z_groups)]
    pallas_call x0 -> x6, Pallas kernels: none -> 33.3 us  [the longest x1 6.69 us: first_update(): pl.pallas_call(first_update_kernel, grid=(n_rows // tile,), in_specs=[pl....]
    dot_general x32 -> x2, matrix products: 28.3 us -> 1.28 us  [product(): lax.dot_general(first_op, second_op, dims, precision=lax.Precision.HIGHES...]
    another operation x4 -> x1, other arithmetic: 22.2 us -> 0.65 us  [on_device(): place = jnp.stack([row, col]).astype(jnp.int32)]
    ppermute x0 -> x4, starting transfers between devices: none -> 12 us  [the longest x2 5.55 us: gather_row(): summed = keep + lax.ppermute(give, 'row', swap)]
  transfers between devices with their start and end apart: 5 -> 9, of which waited for: 5 -> 7; matrix products, arithmetic and copies ran while one was open for 1% -> 3% of each run, Pallas kernels for 0% -> 13%
where the time goes in v2:
time: 146 us; the launch traced here: 145 us
  waiting for transfers between devices  50.3 us (34%)
  starting transfers between devices  46.1 us (32%)
  Pallas kernels  33.3 us (23%)
  local copies, waits for them, and re-layouts  7.21 us (5%)
  blocking collectives  4.97 us (3%)
    all_to_all x2, waiting for transfers between devices, gather_row(): lax.all_to_all(copies(sent, n_z), 'row', 0, 0, axis_index_groups=z_groups)  29.3 us
    all_to_all x2, starting transfers between devices, gather_row(): lax.all_to_all(copies(sent, n_z), 'row', 0, 0, axis_index_groups=z_groups)  17.7 us
    all_to_all x1, waiting for transfers between devices, on_device(): got = lax.all_to_all(sent, 'col', 0, 0)  8.25 us
    all_to_all x1, starting transfers between devices, on_device(): lax.all_to_all(copies(panel, n_col), 'col', 0, 0).reshape(block_rows, width)  7.58 us
    pallas_call x1, Pallas kernels, first_update(): pl.pallas_call(first_update_kernel, grid=(n_rows // tile,), in_specs=[pl....  6.69 us
    pallas_call x1, Pallas kernels, last_update(): pl.pallas_call(lambda *refs: last_update_kernel(n_z, piece, *refs), grid=...  6.67 us
    pallas_call x1, Pallas kernels, factor(): pl.pallas_call(factor_kernel, out_shape=(shape, shape), scratch_shapes=[p...  6.61 us
    all_to_all x1, waiting for transfers between devices, on_device(): lax.all_to_all(copies(panel, n_col), 'col', 0, 0).reshape(block_rows, width)  5.89 us
  transfers between devices with their start and end apart: 9, of which 7 were waited for; matrix products, arithmetic and copies ran while one was open for 3% of the time, Pallas kernels for 13%

profile of v2, /device:TPU:1, one launch (start us, length us, event | category | flops | bytes accessed | tf_op | source)
XLA Modules:
  0.0 144.7 jit_solution(1401885292313934889)
XLA Ops:
  0.6 1.6 %broadcast_in_dim.6 = f32[16,64,128]{2,1,0:T(8,128)} broadcast(f32[64,128]{1,0:T(8,128)} %param.2), dimensions={1,2} | broadcast | bytes 557056 | tf_op jit(solution)/shard_map/broadcast_in_dim | solution.py:332
  2.2 7.6 %all-to-all-start = ((f32[16,64,128]{2,1,0:T(8,128)}), f32[16,64,128]{2,1,0:T(8,128)S(1)}, u32[]{:S(2)}, u32[]{:S(2)}) async-start(f32[16,64,128]{2,1,0:T(8,128)} %broadcast_in_dim.6), calls=%async_computation | async-start | bytes 1048576 | tf_op jit(solution)/shard_map/all_to_all | solution.py:348
  9.8 4.4 %collective-permute-start = (f32[64,128]{1,0:T(8,128)}, f32[64,128]{1,0:T(8,128)S(1)}, u32[]{:S(2)}, u32[]{:S(2)}) collective-permute-start(f32[64,128]{1,0:T(8,128)} %param.2), channel_id=1, source_target_pairs={{0,0},{1,16},{2,32},{3,48},{4,64},{5,80},{6,96},{7,112},{8,128},{9... | collective-permute-start | bytes 98312 | tf_op jit(solution)/shard_map/ppermute | solution.py:347
  14.2 5.9 %all-to-all-done = f32[16,64,128]{2,1,0:T(8,128)S(1)} async-done(((f32[16,64,128]{2,1,0:T(8,128)}), f32[16,64,128]{2,1,0:T(8,128)S(1)}, u32[]{:S(2)}, u32[]{:S(2)}) %all-to-all-start) | async-done | bytes 524320 | tf_op jit(solution)/shard_map/all_to_all | solution.py:348
  20.1 0.0 copy-start
  20.1 0.2 copy.6
  20.3 0.6 fusion.2
  21.0 2.2 %collective-permute-start.1 = (f32[64,128]{1,0:T(8,128)S(1)}, f32[64,128]{1,0:T(8,128)S(1)}, u32[]{:S(2)}, u32[]{:S(2)}) collective-permute-start(f32[64,128]{1,0:T(8,128)S(1)} %dynamic-slice_bitcast_fusion.1), channel_id=1, source_target_pairs={{0,16},{16,0},{32,48},{48,32},{64,80},{80,64},{96,112},{112,96},{1... | collective-permute-start | bytes 98312 | tf_op jit(solution)/shard_map/ppermute | solution.py:338
  23.2 0.9 collective-permute-done.1
  24.1 0.0 collective-permute-done
  24.1 0.8 broadcast_in_dim.7
  25.0 8.4 %all-to-all-start.1 = ((f32[8,136,128]{2,1,0:T(8,128)}), f32[8,136,128]{2,1,0:T(8,128)S(1)}, u32[]{:S(2)}, u32[]{:S(2)}) async-start(f32[8,136,128]{2,1,0:T(8,128)} %broadcast_in_dim.7), calls=%async_computation.1 | async-start | bytes 1114112 | tf_op jit(solution)/shard_map/all_to_all | solution.py:340
  33.4 0.7 pad_add_fusion.refs_0_
  34.0 18.0 %all-to-all-done.1 = f32[8,136,128]{2,1,0:T(8,128)S(1)} async-done(((f32[8,136,128]{2,1,0:T(8,128)}), f32[8,136,128]{2,1,0:T(8,128)S(1)}, u32[]{:S(2)}, u32[]{:S(2)}) %all-to-all-start.1) | async-done | bytes 557088 | tf_op jit(solution)/shard_map/all_to_all | solution.py:340
  52.1 2.5 %all-gather = f32[1168,128]{1,0:T(8,128)} all-gather(f32[584,128]{1,0:T(8,128)S(1)} %pad_maximum_fusion), channel_id=2, replica_groups={{0,16},{32,48},{64,80},{96,112},{128,144},{160,176},{192,208},{224,240}..., dimensions={0}, use_global_device_ids=true | all-gather | bytes 897024 | tf_op jit(solution)/shard_map/all_gather | solution.py:345
  54.6 5.8 %partial_sums.1 = f32[16,136,128]{2,1,0:T(8,128)} custom-call(s32[2]{0:T(128)} %pad_add_fusion.refs_0_, f32[2,584,128]{2,1,0:T(8,128)} %bitcast.36, f32[1024,1024]{1,0:T(8,128)} %mob_ref.1), custom_call_target="tpu_custom_call" | custom-call | flops 805306368 | bytes 6000000 | tf_op jit(solution)/shard_map/partial_sums/pallas_call | solution.py:150
  60.4 0.0 copy-done
  60.4 4.1 %all-to-all-start.2 = ((f32[16,136,128]{2,1,0:T(8,128)}), f32[16,136,128]{2,1,0:T(8,128)S(1)}, u32[]{:S(2)}, u32[]{:S(2)}) async-start(f32[16,136,128]{2,1,0:T(8,128)} %partial_sums.1), calls=%async_computation.2 | async-start | bytes 2228224 | tf_op jit(solution)/shard_map/all_to_all | solution.py:356
  64.4 1.5 %slice.27 = f32[2,64,128]{2,1,0:T(8,128)} slice(f32[2,584,128]{2,1,0:T(8,128)} %bitcast.37), slice={[0:2], [512:576], [0:128]} | slice | bytes 131072 | tf_op jit(solution)/shard_map/slice | solution.py:353
  65.9 6.6 %factor.1 = (f32[128,128]{1,0:T(8,128)}, f32[128,128]{1,0:T(8,128)}) custom-call(f32[128,128]{1,0:T(8,128)} %bitcast.47), custom_call_target="tpu_custom_call" | custom-call | flops 400000000 | bytes 20000000 | tf_op jit(solution)/shard_map/factor/pallas_call | solution.py:112
  72.5 8.3 %all-to-all-done.2.refs_0_ = f32[16,136,128]{2,1,0:T(8,128)S(1)} async-done(((f32[16,136,128]{2,1,0:T(8,128)}), f32[16,136,128]{2,1,0:T(8,128)S(1)}, u32[]{:S(2)}, u32[]{:S(2)}) %all-to-all-start.2) | async-done | bytes 1114144 | tf_op jit(solution)/shard_map/all_to_all | solution.py:356
  80.8 0.0 copy-start.2
  80.8 1.0 copy-done.2
  81.8 2.4 %image_piece.1 = (f32[64,128]{1,0:T(8,128)}, f32[16,64,128]{2,1,0:T(8,128)}, f32[128,128]{1,0:T(8,128)}) custom-call(f32[16,136,128]{2,1,0:T(8,128)} %copy-done.2, f32[128,128]{1,0:T(8,128)} %get-tuple-element.11.refs_1_.refs_3_), custom_call_target="tpu_custom_call" | custom-call | flops 10000000 | bytes 2000000 | tf_op jit(solution)/shard_map/image_piece/pallas_call | solution.py:183
  84.2 0.0 copy-start.3
  84.2 4.7 %all-to-all-start.3 = ((f32[16,64,128]{2,1,0:T(8,128)}), f32[16,64,128]{2,1,0:T(8,128)S(1)}, u32[]{:S(2)}, u32[]{:S(2)}) async-start(f32[16,64,128]{2,1,0:T(8,128)} %get-tuple-element.15), calls=%async_computation.3 | async-start | bytes 1048576 | tf_op jit(solution)/shard_map/all_to_all | solution.py:360
  88.9 5.2 %bases.1 = (f32[1024,128]{1,0:T(8,128)}, f32[1024,128]{1,0:T(8,128)}, f32[1024,128]{1,0:T(8,128)}, f32[1024,128]{1,0:T(8,128)}, f32[128,128]{1,0:T(8,128)}) custom-call(s32[2]{0:T(128)} %pad_add_fusion.refs_0_, f32[1024,128]{1,0:T(8,128)} %bitcast.35, f32[2,584,128]{2,1,0:T(8,128)} %bitcast.38, f32[128,128]{1,0:T(8,128)} %get-tuple-element.11.refs_1_.refs_3_, ...), custom_call_target="tpu_custom_call" | custom-call | flops 300000000 | bytes 10000000 | tf_op jit(solution)/shard_map/bases/pallas_call | solution.py:236
  94.1 1.2 copy.7
  95.3 2.8 %all-to-all-done.3 = f32[16,64,128]{2,1,0:T(8,128)S(1)} async-done(((f32[16,64,128]{2,1,0:T(8,128)}), f32[16,64,128]{2,1,0:T(8,128)S(1)}, u32[]{:S(2)}, u32[]{:S(2)}) %all-to-all-start.3) | async-done | bytes 524320 | tf_op jit(solution)/shard_map/all_to_all | solution.py:360
  98.1 0.0 copy-start.1
  98.1 0.6 fusion.3
  98.7 3.3 %collective-permute-start.3 = (f32[64,128]{1,0:T(8,128)S(1)}, f32[64,128]{1,0:T(8,128)S(1)}, u32[]{:S(2)}, u32[]{:S(2)}) collective-permute-start(f32[64,128]{1,0:T(8,128)S(1)} %dynamic-slice_bitcast_fusion), channel_id=1, source_target_pairs={{0,16},{16,0},{32,48},{48,32},{64,80},{80,64},{96,112},{112,96},{1... | collective-permute-start | bytes 98312 | tf_op jit(solution)/shard_map/ppermute | solution.py:338
  102.1 0.0 copy-done.3
  102.1 2.1 %collective-permute-start.2 = (f32[64,128]{1,0:T(8,128)S(1)}, f32[64,128]{1,0:T(8,128)S(1)}, u32[]{:S(2)}, u32[]{:S(2)}) collective-permute-start(f32[64,128]{1,0:T(8,128)S(1)} %copy-done.3), channel_id=1, source_target_pairs={{0,0},{1,16},{2,32},{3,48},{4,64},{5,80},{6,96},{7,112},{8,128},{9... | collective-permute-start | bytes 98312 | tf_op jit(solution)/shard_map/ppermute | solution.py:359
  104.2 0.0 collective-permute-done.3
  104.2 3.2 %collective-permute-done.2 = f32[64,128]{1,0:T(8,128)S(1)} collective-permute-done((f32[64,128]{1,0:T(8,128)S(1)}, f32[64,128]{1,0:T(8,128)S(1)}, u32[]{:S(2)}, u32[]{:S(2)}) %collective-permute-start.2) | collective-permute-done | bytes 32800 | tf_op jit(solution)/shard_map/ppermute | solution.py:359
  107.4 0.8 broadcast_in_dim.8
  108.3 9.3 %all-to-all-start.4 = ((f32[8,128,128]{2,1,0:T(8,128)}), f32[8,128,128]{2,1,0:T(8,128)S(1)}, u32[]{:S(2)}, u32[]{:S(2)}) async-start(f32[8,128,128]{2,1,0:T(8,128)} %broadcast_in_dim.8), calls=%async_computation.4 | async-start | bytes 1048576 | tf_op jit(solution)/shard_map/all_to_all | solution.py:340
  117.6 0.0 copy-done.1
  117.6 6.7 %first_update.1.refs_3_ = f32[1024,1024]{1,0:T(8,128)} custom-call(f32[1024,128]{1,0:T(8,128)} %bitcast.40, f32[128,128]{1,0:T(8,128)} %get-tuple-element.18.kernel_ref, f32[1024,128]{1,0:T(8,128)} %get-tuple-element.16.cols_ref.refs_1_, f32[1024,1024]{1,0:T(8,128)} %mob_ref.1), custom_call_target="tpu_custom_call" | custom-call | flops 805306368 | bytes 9000000 | tf_op jit(solution)/shard_map/first_update/pallas_call | solution.py:262
  124.3 11.3 %all-to-all-done.4 = f32[8,128,128]{2,1,0:T(8,128)S(1)} async-done(((f32[8,128,128]{2,1,0:T(8,128)}), f32[8,128,128]{2,1,0:T(8,128)S(1)}, u32[]{:S(2)}, u32[]{:S(2)}) %all-to-all-start.4) | async-done | bytes 524320 | tf_op jit(solution)/shard_map/all_to_all | solution.py:340
  135.6 2.5 %all-gather.1 = f32[1152,128]{1,0:T(8,128)} all-gather(f32[576,128]{1,0:T(8,128)S(1)} %pad_maximum_fusion.1), channel_id=3, replica_groups={{0,16},{32,48},{64,80},{96,112},{128,144},{160,176},{192,208},{224,240}..., dimensions={0}, use_global_device_ids=true | all-gather | bytes 884736 | tf_op jit(solution)/shard_map/all_gather | solution.py:345
  138.1 6.7 %last_update.1 = f32[1024,1024]{1,0:T(8,128)} custom-call(f32[2,576,128]{2,1,0:T(8,128)} %bitcast.41, f32[1024,128]{1,0:T(8,128)} %get-tuple-element.16.cols_ref.refs_1_, f32[1024,128]{1,0:T(8,128)} %get-tuple-element.17.refs_2_, f32[1024,1024]{1,0:T(8,128)} %first_update.1.refs_3_), custom_call_target="tpu_custom_call" | custom-call | flops 805306368 | bytes 9000000 | tf_op jit(solution)/shard_map/last_update/pallas_call | solution.py:298
  (12 shorter events, 0.2 us)
Async XLA Ops:
  2.2 17.9 %all-to-all-start = ((f32[16,64,128]{2,1,0:T(8,128)}), f32[16,64,128]{2,1,0:T(8,128)S(1)}, u32[]{:S(2)}, u32[]{:S(2)}) async-start(f32[16,64,128]{2,1,0:T(8,128)} %broadcast_in_dim.6), calls=%async_computation | async-start | bytes 1048576 | tf_op jit(solution)/shard_map/all_to_all | solution.py:348
  9.8 14.3 %collective-permute-start = (f32[64,128]{1,0:T(8,128)}, f32[64,128]{1,0:T(8,128)S(1)}, u32[]{:S(2)}, u32[]{:S(2)}) collective-permute-start(f32[64,128]{1,0:T(8,128)} %param.2), channel_id=1, source_target_pairs={{0,0},{1,16},{2,32},{3,48},{4,64},{5,80},{6,96},{7,112},{8,128},{9... | collective-permute-start | bytes 98312 | tf_op jit(solution)/shard_map/ppermute | solution.py:347
  20.1 40.2 %copy-start = (f32[16,64,128]{2,1,0:T(8,128)}, f32[16,64,128]{2,1,0:T(8,128)S(1)}, u32[]{:S(2)}) copy-start(f32[16,64,128]{2,1,0:T(8,128)S(1)} %all-to-all-done) | copy-start | bytes 1572868
  21.0 3.1 %collective-permute-start.1 = (f32[64,128]{1,0:T(8,128)S(1)}, f32[64,128]{1,0:T(8,128)S(1)}, u32[]{:S(2)}, u32[]{:S(2)}) collective-permute-start(f32[64,128]{1,0:T(8,128)S(1)} %dynamic-slice_bitcast_fusion.1), channel_id=1, source_target_pairs={{0,16},{16,0},{32,48},{48,32},{64,80},{80,64},{96,112},{112,96},{1... | collective-permute-start | bytes 98312 | tf_op jit(solution)/shard_map/ppermute | solution.py:338
  25.0 27.1 %all-to-all-start.1 = ((f32[8,136,128]{2,1,0:T(8,128)}), f32[8,136,128]{2,1,0:T(8,128)S(1)}, u32[]{:S(2)}, u32[]{:S(2)}) async-start(f32[8,136,128]{2,1,0:T(8,128)} %broadcast_in_dim.7), calls=%async_computation.1 | async-start | bytes 1114112 | tf_op jit(solution)/shard_map/all_to_all | solution.py:340
  60.4 20.4 %all-to-all-start.2 = ((f32[16,136,128]{2,1,0:T(8,128)}), f32[16,136,128]{2,1,0:T(8,128)S(1)}, u32[]{:S(2)}, u32[]{:S(2)}) async-start(f32[16,136,128]{2,1,0:T(8,128)} %partial_sums.1), calls=%async_computation.2 | async-start | bytes 2228224 | tf_op jit(solution)/shard_map/all_to_all | solution.py:356
  80.8 1.0 copy-start.2
  84.2 17.9 %copy-start.3 = (f32[64,128]{1,0:T(8,128)S(1)}, f32[64,128]{1,0:T(8,128)}, u32[]{:S(2)}) copy-start(f32[64,128]{1,0:T(8,128)} %get-tuple-element.12) | copy-start | bytes 98308
  84.2 13.9 %all-to-all-start.3 = ((f32[16,64,128]{2,1,0:T(8,128)}), f32[16,64,128]{2,1,0:T(8,128)S(1)}, u32[]{:S(2)}, u32[]{:S(2)}) async-start(f32[16,64,128]{2,1,0:T(8,128)} %get-tuple-element.15), calls=%async_computation.3 | async-start | bytes 1048576 | tf_op jit(solution)/shard_map/all_to_all | solution.py:360
  98.1 19.5 %copy-start.1 = (f32[16,64,128]{2,1,0:T(8,128)}, f32[16,64,128]{2,1,0:T(8,128)S(1)}, u32[]{:S(2)}) copy-start(f32[16,64,128]{2,1,0:T(8,128)S(1)} %all-to-all-done.3) | copy-start | bytes 1572868
  98.7 5.4 %collective-permute-start.3 = (f32[64,128]{1,0:T(8,128)S(1)}, f32[64,128]{1,0:T(8,128)S(1)}, u32[]{:S(2)}, u32[]{:S(2)}) collective-permute-start(f32[64,128]{1,0:T(8,128)S(1)} %dynamic-slice_bitcast_fusion), channel_id=1, source_target_pairs={{0,16},{16,0},{32,48},{48,32},{64,80},{80,64},{96,112},{112,96},{1... | collective-permute-start | bytes 98312 | tf_op jit(solution)/shard_map/ppermute | solution.py:338
  102.1 5.4 %collective-permute-start.2 = (f32[64,128]{1,0:T(8,128)S(1)}, f32[64,128]{1,0:T(8,128)S(1)}, u32[]{:S(2)}, u32[]{:S(2)}) collective-permute-start(f32[64,128]{1,0:T(8,128)S(1)} %copy-done.3), channel_id=1, source_target_pairs={{0,0},{1,16},{2,32},{3,48},{4,64},{5,80},{6,96},{7,112},{8,128},{9... | collective-permute-start | bytes 98312 | tf_op jit(solution)/shard_map/ppermute | solution.py:359
  108.3 27.3 %all-to-all-start.4 = ((f32[8,128,128]{2,1,0:T(8,128)}), f32[8,128,128]{2,1,0:T(8,128)S(1)}, u32[]{:S(2)}, u32[]{:S(2)}) async-start(f32[8,128,128]{2,1,0:T(8,128)} %broadcast_in_dim.8), calls=%async_computation.4 | async-start | bytes 1048576 | tf_op jit(solution)/shard_map/all_to_all | solution.py:340

commit v3 on v2

v3 whole, which is shorter than its diff:
```python
import jax
import jax.numpy as jnp
from jax import lax
from jax.experimental import pallas as pl
from jax.experimental.pallas import tpu as pltpu
from jax.sharding import PartitionSpec as P

BOTH = ("row", "col")
STEP = 8
MIB = 1 << 20
NN = (((1,), (0,)), ((), ()))
TN = (((0,), (0,)), ((), ()))
NT = (((1,), (1,)), ((), ()))


def product(first_op, second_op, dims=NN):
    return lax.dot_general(
        first_op,
        second_op,
        dims,
        precision=lax.Precision.HIGHEST,
        preferred_element_type=jnp.float32,
    )


def split(value):
    high = value.astype(jnp.bfloat16)
    return high, (value - high.astype(jnp.float32)).astype(jnp.bfloat16)


def left_terms(value):
    high, low = split(value)
    return jnp.concatenate([high, low, high], 1)


def right_terms(value):
    high, low = split(value)
    return jnp.concatenate([high, high, low], 1)


def exact_dot(first_op, second_op, dims):
    return lax.dot_general(first_op, second_op, dims, preferred_element_type=jnp.float32)


def unit_rows(index, shape):
    rows = lax.broadcasted_iota(jnp.int32, shape, 0) + index * shape[0]
    return jnp.where(rows == lax.broadcasted_iota(jnp.int32, shape, 1), 1.0, 0.0)


def eye(width):
    return unit_rows(0, (width, width))


def pieces_of(pairs_ref, n_z, piece):
    return jnp.concatenate(
        [pairs_ref[h, z * piece : (z + 1) * piece, :] for z in range(n_z) for h in range(2)], 0
    )


def keep_and_give(place_ref, value, keep_ref, give_ref):
    side = value.shape[0] // 2
    even = lax.rem(place_ref[0], 2) == 0
    keep_ref[...] = jnp.where(even, value[:side], value[side:])
    give_ref[...] = jnp.where(even, value[side:], value[:side])


def gram_kernel(piece, place_ref, got_ref, rows_ref, keep_ref, give_ref, top_ref, first_ref):
    share = top_ref.shape[0]
    rows = got_ref[:, :piece, :].reshape(rows_ref.shape)
    rows_ref[...] = rows
    keep_and_give(place_ref, product(rows, rows, TN), keep_ref, give_ref)
    start = pl.multiple_of(place_ref[1] * share, share)
    top_ref[...] = rows_ref[pl.ds(start, share), :]
    first_ref[...] = got_ref[0, piece:, :]


def gram_parts(place, got, piece):
    count, _, width = got.shape
    vmem = pl.BlockSpec(memory_space=pltpu.VMEM)
    shapes = [(count * piece, width), (width // 2, width), (width // 2, width)]
    shapes += [(width // count, width), (piece, width)]
    return pl.pallas_call(
        lambda *refs: gram_kernel(piece, *refs),
        in_specs=[pl.BlockSpec(memory_space=pltpu.SMEM), vmem],
        out_specs=[vmem] * 5,
        out_shape=[jax.ShapeDtypeStruct(shape, jnp.float32) for shape in shapes],
        cost_estimate=pl.CostEstimate(
            flops=200_000_000, bytes_accessed=3_000_000, transcendentals=0
        ),
        compiler_params=pltpu.CompilerParams(vmem_limit_bytes=8 * MIB),
        name="gram_parts",
    )(place, got)


def inner_kernel(place_ref, twisted_ref, rows_ref, keep_ref, give_ref):
    keep_and_give(place_ref, product(twisted_ref[...], rows_ref[...]), keep_ref, give_ref)


def inner_parts(place, twisted, rows):
    width = rows.shape[1]
    vmem = pl.BlockSpec(memory_space=pltpu.VMEM)
    return pl.pallas_call(
        inner_kernel,
        in_specs=[pl.BlockSpec(memory_space=pltpu.SMEM), vmem, vmem],
        out_specs=[vmem] * 2,
        out_shape=[jax.ShapeDtypeStruct((width // 2, width), jnp.float32)] * 2,
        cost_estimate=pl.CostEstimate(
            flops=200_000_000, bytes_accessed=1_000_000, transcendentals=0
        ),
        compiler_params=pltpu.CompilerParams(vmem_limit_bytes=6 * MIB),
        name="inner_parts",
    )(place, twisted, rows)


def factor_kernel(gram_ref, upper_ref, inverse_ref, work, other):
    width = upper_ref.shape[0]
    full = (STEP, width)
    lane = lax.broadcasted_iota(jnp.int32, full, 1)
    work[...] = gram_ref[...].reshape(width, width)
    other[...] = eye(width)
    for first in range(0, width, STEP):
        a_rows = [jnp.broadcast_to(work[first + k : first + k + 1, :], full) for k in range(STEP)]
        x_rows = [jnp.broadcast_to(other[first + k : first + k + 1, :], full) for k in range(STEP)]
        entry, mult, inv = {}, {}, {}
        for i in range(STEP):
            for k in range(i + 1):
                column = a_rows[i][:, first + k : first + k + 1]
                entry[i, k] = jnp.broadcast_to(column, full)
        for k in range(STEP):
            inv[k] = 1.0 / entry[k, k]
            for i in range(k + 1, STEP):
                mult[i, k] = entry[i, k] * inv[k]
            for i in range(k + 1, STEP):
                for l in range(k + 1, i + 1):
                    entry[i, l] = entry[i, l] - mult[i, k] * entry[l, k]
        for i in range(STEP):
            for k in range(i):
                a_rows[i] = a_rows[i] - mult[i, k] * a_rows[k]
                x_rows[i] = x_rows[i] - mult[i, k] * x_rows[k]
        for k in range(STEP):
            root = lax.rsqrt(entry[k, k])
            root = root * (1.5 - 0.5 * entry[k, k] * root * root)
            row = slice(first + k, first + k + 1)
            upper_ref[row, :] = jnp.where(lane >= first + k, a_rows[k] * root, 0.0)[:1]
            inverse_ref[row, :] = (x_rows[k] * root)[:1]
        if first + STEP == width:
            break
        a_back = [a_rows[k] * inv[k] for k in range(STEP)]
        x_back = [x_rows[k] * inv[k] for k in range(STEP)]
        for k in range(STEP - 2, -1, -1):
            for l in range(k + 1, STEP):
                a_back[k] = a_back[k] - mult[l, k] * a_back[l]
                x_back[k] = x_back[k] - mult[l, k] * x_back[l]
        for g in range(first + STEP, width, STEP):
            block = work[g : g + STEP, :]
            a_new, x_new = block, other[g : g + STEP, :]
            for k in range(STEP):
                column = jnp.broadcast_to(block[:, first + k : first + k + 1], full)
                a_new = a_new - column * a_back[k]
                x_new = x_new - column * x_back[k]
            work[g : g + STEP, :] = a_new
            other[g : g + STEP, :] = x_new


def factor(pairs, start):
    width = pairs.shape[2]
    side = width // 2
    shape = jax.ShapeDtypeStruct((width, width), jnp.float32)
    return pl.pallas_call(
        factor_kernel,
        grid=(1,),
        in_specs=[pl.BlockSpec((2, side, width), lambda i: (0, start // side, 0))],
        out_specs=[pl.BlockSpec((width, width), lambda i: (0, 0))] * 2,
        out_shape=(shape, shape),
        scratch_shapes=[pltpu.VMEM((width, width), jnp.float32)] * 2,
        cost_estimate=pl.CostEstimate(
            flops=400_000_000, bytes_accessed=20_000_000, transcendentals=0
        ),
        compiler_params=pltpu.CompilerParams(vmem_limit_bytes=4 * MIB),
        name="factor",
    )(pairs)


def partial_kernel(n_z, piece, share, pairs_ref, mob_ref, out_ref, rhs, held, sems):
    width = pairs_ref.shape[2]
    n_rows = held.shape[0]
    parts = sems.shape[0]
    tile = n_rows // parts
    loads = []
    for k in range(parts):
        rows = pl.ds(k * tile, tile)
        loads.append(pltpu.make_async_copy(mob_ref.at[rows], held.at[rows], sems.at[k]))
        loads[k].start()
    high, low = split(pieces_of(pairs_ref, n_z, piece))
    rhs[:, :width] = high
    rhs[:, width:] = low
    last = pairs_ref.shape[1] - share
    out_ref[:, piece:, :] = jnp.broadcast_to(
        pairs_ref[0, last:, :][None], (out_ref.shape[0], share, width)
    )
    count = tile // piece
    for k in range(parts):
        loads[k].wait()
        high, low = split(held[k * tile : (k + 1) * tile, :])
        wide = exact_dot(high, rhs[...], NN)
        found = wide[:, :width] + wide[:, width:] + exact_dot(low, rhs[:, :width], NN)
        out_ref[k * count : (k + 1) * count, :piece, :] = found.reshape(count, piece, width)


def partial_sums(pairs, mobility, n_z, piece, share):
    n_rows, n_cols = mobility.shape
    width = pairs.shape[2]
    vmem = pl.BlockSpec(memory_space=pltpu.VMEM)
    return pl.pallas_call(
        lambda *refs: partial_kernel(n_z, piece, share, *refs),
        in_specs=[vmem, pl.BlockSpec(memory_space=pl.ANY)],
        out_specs=vmem,
        out_shape=jax.ShapeDtypeStruct((n_rows // piece, piece + share, width), jnp.float32),
        scratch_shapes=[
            pltpu.VMEM((n_cols, 2 * width), jnp.bfloat16),
            pltpu.VMEM(mobility.shape, jnp.float32),
            pltpu.SemaphoreType.DMA((4,)),
        ],
        cost_estimate=pl.CostEstimate(
            flops=6 * n_rows * n_cols * width, bytes_accessed=6_000_000, transcendentals=0
        ),
        compiler_params=pltpu.CompilerParams(vmem_limit_bytes=58 * MIB),
        name="partial_sums",
    )(pairs, mobility)


def image_kernel(piece, got_ref, first_ref, inverse_ref, image_ref, copies_ref, top_ref):
    total = got_ref[0, :piece, :]
    for k in range(1, got_ref.shape[0]):
        total = total + got_ref[k, :piece, :]
    image = product(total, inverse_ref[...], NT) + first_ref[...]
    image_ref[...] = image
    copies_ref[...] = jnp.broadcast_to(image[None], copies_ref.shape)
    top_ref[...] = got_ref[:, piece:, :].reshape(top_ref.shape)


def image_piece(got, first, inverse, piece):
    count, _, width = got.shape
    square = jax.ShapeDtypeStruct((width, width), jnp.float32)
    return pl.pallas_call(
        lambda *refs: image_kernel(piece, *refs),
        grid=(1,),
        in_specs=[
            pl.BlockSpec(got.shape, lambda i: (0, 0, 0)),
            pl.BlockSpec((piece, width), lambda i: (0, 0)),
            pl.BlockSpec((width, width), lambda i: (0, 0)),
        ],
        out_specs=[
            pl.BlockSpec((piece, width), lambda i: (0, 0)),
            pl.BlockSpec((count, piece, width), lambda i: (0, 0, 0)),
            pl.BlockSpec((width, width), lambda i: (0, 0)),
        ],
        out_shape=(
            jax.ShapeDtypeStruct((piece, width), jnp.float32),
            jax.ShapeDtypeStruct((count, piece, width), jnp.float32),
            square,
        ),
        cost_estimate=pl.CostEstimate(
            flops=10_000_000, bytes_accessed=2_000_000, transcendentals=0
        ),
        compiler_params=pltpu.CompilerParams(vmem_limit_bytes=6 * MIB),
        name="image_piece",
    )(got, first, inverse)


def basis_kernel(n_z, piece, place, rows_ref, pairs_ref, inverse_ref, top_ref, *outs):
    cols_left, cols_right, twisted, turned, kernel_ref, state_ref = outs
    width = inverse_ref.shape[0]
    inverse = inverse_ref[...]
    identity = eye(width)
    ratio = -product(inverse, top_ref[...], NT)

    state_ref[:width, :] = ratio
    state_ref[width:, :] = identity

    def go_on(state):
        return jnp.logical_and(state[0] < 40, state[1] > 1e-10)

    def double(state):
        power = state_ref[:width, :]
        both = product(state_ref[...], power)
        state_ref[:width, :] = both[:width]
        state_ref[width:, :] = state_ref[width:, :] + both[width:]
        return state[0] + 1, jnp.max(jnp.abs(both[:width]))

    lax.while_loop(go_on, double, (0, jnp.max(jnp.abs(ratio))))
    total = state_ref[width:, :]
    kernel = total + product(total, identity - product(identity - ratio, total))
    kernel_ref[...] = kernel
    inverse_terms = right_terms(inverse)
    rows = exact_dot(left_terms(rows_ref[...]), inverse_terms, NT)
    rows = rows + unit_rows(place[0], rows_ref.shape)
    cols = exact_dot(left_terms(pieces_of(pairs_ref, n_z, piece)), inverse_terms, NT)
    cols = cols + unit_rows(place[1], cols.shape)
    cols_left[...] = left_terms(cols)
    cols_right[...] = right_terms(cols)
    terms = left_terms(rows)
    twisted[...] = exact_dot(right_terms(kernel.T), terms, NT)
    turned[...] = left_terms(exact_dot(terms, right_terms(kernel), NT))


def bases(place, panel_rows, pairs, inverse, top_rows, n_z, piece):
    width = inverse.shape[0]
    terms = jax.ShapeDtypeStruct((panel_rows.shape[0], 3 * width), jnp.bfloat16)
    vmem = pl.BlockSpec(memory_space=pltpu.VMEM)
    return pl.pallas_call(
        lambda *refs: basis_kernel(n_z, piece, *refs),
        in_specs=[pl.BlockSpec(memory_space=pltpu.SMEM)] + [vmem] * 4,
        out_specs=[vmem] * 5,
        out_shape=(
            terms,
            terms,
            jax.ShapeDtypeStruct(panel_rows.shape[::-1], jnp.float32),
            terms,
            jax.ShapeDtypeStruct((width, width), jnp.float32),
        ),
        scratch_shapes=[pltpu.VMEM((2 * width, width), jnp.float32)],
        cost_estimate=pl.CostEstimate(
            flops=300_000_000, bytes_accessed=10_000_000, transcendentals=0
        ),
        compiler_params=pltpu.CompilerParams(vmem_limit_bytes=16 * MIB),
        name="bases",
    )(place, panel_rows, pairs, inverse, top_rows)


def stream(source_ref, out_ref, held, sems_in, sems_out, prepare, change):
    parts = sems_in.shape[0]
    tile = held.shape[0] // parts
    loads, stores = [], []
    for k in range(parts):
        rows = pl.ds(k * tile, tile)
        loads.append(pltpu.make_async_copy(source_ref.at[rows], held.at[rows], sems_in.at[k]))
        stores.append(pltpu.make_async_copy(held.at[rows], out_ref.at[rows], sems_out.at[k]))
        loads[k].start()
    prepare()
    for k in range(parts):
        loads[k].wait()
        rows = slice(k * tile, (k + 1) * tile)
        held[rows, :] = change(held[rows, :], rows)
        stores[k].start()
    for k in range(parts):
        stores[k].wait()


def first_update_kernel(image_ref, kernel_ref, cols_ref, mob_ref, out_ref, lhs, held, *sems):
    def prepare():
        lhs[...] = left_terms(product(image_ref[...], kernel_ref[...]))

    def change(value, rows):
        return value - exact_dot(lhs[rows, :], cols_ref[...], NT)

    stream(mob_ref, out_ref, held, *sems, prepare, change)


def update_call(kernel, inputs, matrix, terms, name):
    n_rows, n_cols = matrix.shape
    vmem = pl.BlockSpec(memory_space=pltpu.VMEM)
    hbm = pl.BlockSpec(memory_space=pl.ANY)
    return pl.pallas_call(
        kernel,
        in_specs=[vmem] * len(inputs) + [hbm],
        out_specs=hbm,
        out_shape=jax.ShapeDtypeStruct(matrix.shape, jnp.float32),
        scratch_shapes=[
            pltpu.VMEM((n_rows, terms), jnp.bfloat16),
            pltpu.VMEM(matrix.shape, jnp.float32),
            pltpu.SemaphoreType.DMA((4,)),
            pltpu.SemaphoreType.DMA((4,)),
        ],
        cost_estimate=pl.CostEstimate(
            flops=2 * n_rows * n_cols * terms, bytes_accessed=9_000_000, transcendentals=0
        ),
        compiler_params=pltpu.CompilerParams(vmem_limit_bytes=58 * MIB),
        name=name,
    )(*inputs, matrix)


def last_update_kernel(n_z, piece, pairs_ref, cols_ref, turned_ref, half_ref, out_ref, rhs, held, *sems):
    width = pairs_ref.shape[2]

    def prepare():
        start = n_z * piece
        small = pairs_ref[:, start : start + width // 2, :].reshape(width, width)
        change_cols = exact_dot(cols_ref[...], right_terms(small.T), NT)
        rhs[...] = right_terms(pieces_of(pairs_ref, n_z, piece) - change_cols)

    def change(value, rows):
        return value - exact_dot(turned_ref[rows, :], rhs[...], NT)

    stream(half_ref, out_ref, held, *sems, prepare, change)


def on_device(panel, mobility):
    piece, width = panel.shape
    n_row, n_col = lax.axis_size("row"), lax.axis_size("col")
    block_rows, block_cols = mobility.shape
    row, col = lax.axis_index("row"), lax.axis_index("col")
    place = jnp.stack([row, col]).astype(jnp.int32)
    n_z = n_row // 2
    share = width // n_col
    z_groups = [[2 * z + h for z in range(n_z)] for h in range(2)]
    pairs = [[2 * z, 2 * z + 1] for z in range(n_z)]
    transposing = [(i * n_col + j, j * n_col + i) for i in range(n_row) for j in range(n_col)]
    swap = [(i, i ^ 1) for i in range(n_row)]

    def copies(rows, count):
        return jnp.broadcast_to(rows[None], (count,) + rows.shape)

    def gather_row(lone, keep, give, extra):
        summed = keep + lax.ppermute(give, "row", swap)
        sent = copies(jnp.concatenate([lone, summed] + extra, 0), n_z)
        parts = lax.all_to_all(sent, "row", 0, 0, axis_index_groups=z_groups)
        lone = parts[:, :piece].reshape(n_z * piece, width)
        summed = jnp.sum(parts[:, piece : piece + width // 2], 0)
        extra = [parts[0, piece + width // 2 :]] if extra else []
        sent = jnp.concatenate([lone, summed] + extra, 0)
        return lax.all_gather(sent, "row", axis=0, axis_index_groups=pairs)

    turned_panel = lax.ppermute(panel, BOTH, transposing)
    first_cols = mobility[:, :width].reshape(n_col, piece, width)
    got = lax.all_to_all(
        jnp.concatenate([copies(panel, n_col), first_cols], 1), "col", 0, 0
    )
    got, turned_panel = lax.optimization_barrier((got, turned_panel))
    panel_rows, keep, give, top_part, first = gram_parts(place, got, piece)
    panel_pairs = gather_row(turned_panel, keep, give, [top_part])

    sent = partial_sums(panel_pairs, mobility, n_z, piece, share)
    got = lax.all_to_all(sent, "col", 0, 0)
    panel_factor, inverse = factor(panel_pairs, n_z * piece)
    image, image_copies, top_rows = image_piece(got, first, inverse, piece)
    turned_image = lax.ppermute(image, BOTH, transposing)
    image_rows = lax.all_to_all(image_copies, "col", 0, 0).reshape(block_rows, width)
    cols_left, cols_right, twisted, turned, kernel = bases(
        place, panel_rows, panel_pairs, inverse, top_rows, n_z, piece
    )
    image_rows, turned_image = lax.optimization_barrier((image_rows, turned_image))
    keep, give = inner_parts(place, twisted, image_rows)
    image_pairs = gather_row(turned_image, keep, give, [])
    terms = 3 * width
    halfway = update_call(
        first_update_kernel, (image_rows, kernel, cols_right), mobility, terms, "first_update"
    )
    updated = update_call(
        lambda *refs: last_update_kernel(n_z, piece, *refs),
        (image_pairs, cols_left, turned),
        halfway,
        terms,
        "last_update",
    )
    return (updated, panel_factor)


def solution(mesh):
    in_specs = (P(("row", "col"), None), P("row", "col"))
    out_specs = (P("row", "col"), P())
    return jax.shard_map(
        on_device, mesh=mesh, in_specs=in_specs, out_specs=out_specs, check_vma=False
    )
```

time: 146 us -> 138 us (0.945)
  blocking collectives: 4.97 us -> 32 us
  waiting for transfers between devices: 50.3 us -> 29.9 us
  starting transfers between devices: 46.1 us -> 38.1 us
  Pallas kernels: 33.3 us -> 29.4 us
  local copies, waits for them, and re-layouts: 7.21 us -> 5.47 us
    all_to_all x0 -> x1, blocking collectives: none -> 26.1 us  [gather_row(): parts = lax.all_to_all(sent, 'row', 0, 0, axis_index_groups=z_groups)]
    all_to_all x3 -> x2, waiting for transfers between devices: 35.2 us -> 18.6 us  [the longest x1 12 us: gather_row(): parts = lax.all_to_all(sent, 'row', 0, 0, axis_index_groups=z_groups)]
    all_to_all x3 -> x2, starting transfers between devices: 25.3 us -> 16.6 us  [the longest x1 9.05 us: gather_row(): parts = lax.all_to_all(sent, 'row', 0, 0, axis_index_groups=z_groups)]
    ppermute x1, waiting for transfers between devices: 0.01 us -> 4.43 us  [on_device(): turned_panel = lax.ppermute(panel, BOTH, transposing)]
    ppermute x1, waiting for transfers between devices: 3.22 us -> 0.01 us  [on_device(): turned_image = lax.ppermute(image, BOTH, transposing)]
    all_to_all x1, waiting for transfers between devices: 8.25 us -> 5.1 us  [on_device(): got = lax.all_to_all(sent, 'col', 0, 0)]
    ppermute x1, starting transfers between devices: 2.1 us -> 5.25 us  [on_device(): turned_image = lax.ppermute(image, BOTH, transposing)]
    all_to_all x1, waiting for transfers between devices: 2.78 us -> 0.01 us  [on_device(): lax.all_to_all(image_copies, 'col', 0, 0).reshape(block_rows, width)]
  transfers between devices with their start and end apart: 9 -> 8, of which waited for: 7 -> 6; matrix products, arithmetic and copies ran while one was open for 3% -> 0% of each run, Pallas kernels for 13% -> 11%
where the time goes in v3:
time: 138 us; the launch traced here: 137 us
  starting transfers between devices  38.1 us (28%)
  blocking collectives  32 us (23%)
  waiting for transfers between devices  29.9 us (22%)
  Pallas kernels  29.4 us (21%)
  local copies, waits for them, and re-layouts  5.47 us (4%)
    all_to_all x1, blocking collectives, gather_row(): parts = lax.all_to_all(sent, 'row', 0, 0, axis_index_groups=z_groups)  26.1 us
    all_to_all x1, waiting for transfers between devices, gather_row(): parts = lax.all_to_all(sent, 'row', 0, 0, axis_index_groups=z_groups)  12 us
    pallas_call x2, Pallas kernels, update_call(): pl.pallas_call(kernel, in_specs=[vmem] * len(inputs) + [hbm], out_specs=h...  11.6 us
    all_to_all x1, starting transfers between devices, gather_row(): parts = lax.all_to_all(sent, 'row', 0, 0, axis_index_groups=z_groups)  9.05 us
    all_to_all x1, starting transfers between devices, on_device(): lax.all_to_all(jnp.concatenate([copies(panel, n_col), first_cols], 1), 'c...  7.58 us
    all_to_all x1, waiting for transfers between devices, on_device(): lax.all_to_all(jnp.concatenate([copies(panel, n_col), first_cols], 1), 'c...  6.59 us
    all_gather x2, blocking collectives, gather_row(): return lax.all_gather(sent, 'row', axis=0, axis_index_groups=pairs)  5.87 us
    pallas_call x1, Pallas kernels, factor(): pl.pallas_call(factor_kernel, grid=(1,), in_specs=[pl.BlockSpec((2, side,...  5.76 us
  transfers between devices with their start and end apart: 8, of which 6 were waited for; matrix products, arithmetic and copies ran while one was open for 0% of the time, Pallas kernels for 11%

profile of v3, /device:TPU:1, one launch (start us, length us, event | category | flops | bytes accessed | tf_op | source)
XLA Modules:
  0.0 137.0 jit_solution(11759159315460825797)
XLA Ops:
  0.6 0.0 copy-start.6
  0.6 1.1 slice.18
  1.7 0.8 broadcast_in_dim.6
  2.5 1.0 pad_maximum_fusion
  3.6 7.6 %all-to-all-start = ((f32[16,128,128]{2,1,0:T(8,128)}), f32[16,128,128]{2,1,0:T(8,128)S(1)}, u32[]{:S(2)}, u32[]{:S(2)}) async-start(f32[16,128,128]{2,1,0:T(8,128)} %pad_maximum_fusion), calls=%async_computation | async-start | bytes 2097152 | tf_op jit(solution)/shard_map/all_to_all | solution.py:426
  11.2 0.0 copy-done.6
  11.2 4.4 %collective-permute-start = (f32[64,128]{1,0:T(8,128)S(1)}, f32[64,128]{1,0:T(8,128)S(1)}, u32[]{:S(2)}, u32[]{:S(2)}) collective-permute-start(f32[64,128]{1,0:T(8,128)S(1)} %copy-done.6), channel_id=1, source_target_pairs={{0,0},{1,16},{2,32},{3,48},{4,64},{5,80},{6,96},{7,112},{8,128},{9... | collective-permute-start | bytes 98312 | tf_op jit(solution)/shard_map/ppermute | solution.py:424
  15.6 0.1 pad_add_fusion.refs_0_.place_ref
  15.7 4.4 %collective-permute-done = f32[64,128]{1,0:T(8,128)S(1)} collective-permute-done((f32[64,128]{1,0:T(8,128)S(1)}, f32[64,128]{1,0:T(8,128)S(1)}, u32[]{:S(2)}, u32[]{:S(2)}) %collective-permute-start) | collective-permute-done | bytes 32800 | tf_op jit(solution)/shard_map/ppermute | solution.py:424
  20.1 6.6 %all-to-all-done.refs_1_ = f32[16,128,128]{2,1,0:T(8,128)S(1)} async-done(((f32[16,128,128]{2,1,0:T(8,128)}), f32[16,128,128]{2,1,0:T(8,128)S(1)}, u32[]{:S(2)}, u32[]{:S(2)}) %all-to-all-start) | async-done | bytes 1048608 | tf_op jit(solution)/shard_map/all_to_all | solution.py:426
  26.7 1.2 gram_parts.1
  27.9 3.2 %collective-permute-start.1 = (f32[64,128]{1,0:T(8,128)S(1)}, f32[64,128]{1,0:T(8,128)S(1)}, u32[]{:S(2)}, u32[]{:S(2)}) collective-permute-start(f32[64,128]{1,0:T(8,128)S(1)} %get-tuple-element.26), channel_id=1, source_target_pairs={{0,16},{16,0},{32,48},{48,32},{64,80},{80,64},{96,112},{112,96},{1... | collective-permute-start | bytes 98312 | tf_op jit(solution)/shard_map/ppermute | solution.py:415
  31.1 0.9 collective-permute-done.1
  32.0 26.1 %all_to_all.25 = f32[8,136,128]{2,1,0:T(8,128)S(1)} all-to-all(f32[8,136,128]{2,1,0:T(8,128)S(1)} %broadcast_in_dim.7), channel_id=1, replica_groups={{0,32,64,96,128,160,192,224},{16,48,80,112,144,176,208,240},{1,33,65,97..., dimensions={0} | all-to-all | bytes 1114112 | tf_op jit(solution)/shard_map/all_to_all | solution.py:417
  58.2 3.4 %all-gather = f32[1168,128]{1,0:T(8,128)} all-gather(f32[584,128]{1,0:T(8,128)S(1)} %pad_maximum_fusion.1), channel_id=2, replica_groups={{0,16},{32,48},{64,80},{96,112},{128,144},{160,176},{192,208},{224,240}..., dimensions={0}, use_global_device_ids=true | all-gather | bytes 897024 | tf_op jit(solution)/shard_map/all_gather | solution.py:422
  61.6 0.0 copy-start
  61.6 5.0 %partial_sums.1 = f32[16,72,128]{2,1,0:T(8,128)} custom-call(f32[2,584,128]{2,1,0:T(8,128)} %bitcast.10, f32[1024,1024]{1,0:T(8,128)} %mob_ref.1), custom_call_target="tpu_custom_call" | custom-call | flops 805306368 | bytes 6000000 | tf_op jit(solution)/shard_map/partial_sums/pallas_call | solution.py:214
  66.6 3.8 %all-to-all-start.2 = ((f32[16,72,128]{2,1,0:T(8,128)}), f32[16,72,128]{2,1,0:T(8,128)S(1)}, u32[]{:S(2)}, u32[]{:S(2)}) async-start(f32[16,72,128]{2,1,0:T(8,128)} %partial_sums.1), calls=%async_computation.2 | async-start | bytes 1179648 | tf_op jit(solution)/shard_map/all_to_all | solution.py:434
  70.4 0.0 copy-done
  70.4 5.8 %factor.1 = (f32[128,128]{1,0:T(8,128)}, f32[128,128]{1,0:T(8,128)S(1)}) custom-call(f32[2,584,128]{2,1,0:T(8,128)S(1)} %bitcast.11), custom_call_target="tpu_custom_call" | custom-call | flops 400000000 | bytes 20000000 | tf_op jit(solution)/shard_map/factor/pallas_call | solution.py:169
  76.2 5.1 %all-to-all-done.2.refs_0_ = f32[16,72,128]{2,1,0:T(8,128)S(1)} async-done(((f32[16,72,128]{2,1,0:T(8,128)}), f32[16,72,128]{2,1,0:T(8,128)S(1)}, u32[]{:S(2)}, u32[]{:S(2)}) %all-to-all-start.2) | async-done | bytes 589856 | tf_op jit(solution)/shard_map/all_to_all | solution.py:434
  81.3 1.1 image_piece.1
  82.3 3.9 %all-to-all-start.3 = ((f32[16,64,128]{2,1,0:T(8,128)}), f32[16,64,128]{2,1,0:T(8,128)S(1)}, u32[]{:S(2)}, u32[]{:S(2)}) async-start(f32[16,64,128]{2,1,0:T(8,128)} %get-tuple-element.30), calls=%async_computation.3 | async-start | bytes 1048576 | tf_op jit(solution)/shard_map/all_to_all | solution.py:438
  86.2 5.2 %collective-permute-start.2 = (f32[64,128]{1,0:T(8,128)S(1)}, f32[64,128]{1,0:T(8,128)S(1)}, u32[]{:S(2)}, u32[]{:S(2)}) collective-permute-start(f32[64,128]{1,0:T(8,128)S(1)} %get-tuple-element.31), channel_id=1, source_target_pairs={{0,0},{1,16},{2,32},{3,48},{4,64},{5,80},{6,96},{7,112},{8,128},{9... | collective-permute-start | bytes 98312 | tf_op jit(solution)/shard_map/ppermute | solution.py:437
  91.5 3.7 %bases.1 = (bf16[1024,384]{1,0:T(8,128)(2,1)S(1)}, bf16[1024,384]{1,0:T(8,128)(2,1)S(1)}, f32[128,1024]{1,0:T(8,128)S(1)}, bf16[1024,384]{1,0:T(8,128)(2,1)S(1)}, f32[128,128]{1,0:T(8,128)S(1)}) custom-call(s32[2]{0:T(128)S(1)} %pad_add_fusion.refs_0_.place_ref, f32[1024,128]{1,0:T(8,128)S(1)} %get-tuple-element.33.refs_1_, f32[2,584,128]{2,1,0:T(8,128)S(1)} %bitcast.12, ...), custom_call_target="tpu_custom_call" | custom-call | flops 300000000 | bytes 10000000 | tf_op jit(solution)/shard_map/bases/pallas_call | solution.py:311
  95.2 0.0 copy-start.2
  95.2 0.9 copy-done.2
  96.1 0.0 copy-start.3
  96.1 0.9 copy-done.3
  97.0 0.0 copy-start.4
  97.0 0.9 copy-done.4
  97.9 0.0 copy-start.5
  97.9 0.0 collective-permute-done.2
  97.9 0.0 all-to-all-done.3
  97.9 0.0 copy-start.1
  97.9 1.1 inner_parts.1
  99.1 0.9 collective-permute-start.3
  99.9 0.9 collective-permute-done.3
  100.8 0.8 broadcast_in_dim.8
  101.6 9.1 %all-to-all-start.4 = ((f32[8,128,128]{2,1,0:T(8,128)}), f32[8,128,128]{2,1,0:T(8,128)S(1)}, u32[]{:S(2)}, u32[]{:S(2)}) async-start(f32[8,128,128]{2,1,0:T(8,128)} %broadcast_in_dim.8), calls=%async_computation.4 | async-start | bytes 1048576 | tf_op jit(solution)/shard_map/all_to_all | solution.py:417
  110.7 0.0 copy-done.5
  110.7 0.0 copy-done.1
  110.7 5.9 %first_update.1.refs_3_ = f32[1024,1024]{1,0:T(8,128)} custom-call(f32[1024,128]{1,0:T(8,128)} %bitcast.14, f32[128,128]{1,0:T(8,128)} %copy-done.5, bf16[1024,384]{1,0:T(8,128)(2,1)} %copy-done.4, f32[1024,1024]{1,0:T(8,128)} %mob_ref.1), custom_call_target="tpu_custom_call" | custom-call | flops 805306368 | bytes 9000000 | tf_op jit(solution)/shard_map/first_update/pallas_call | solution.py:364
  116.6 12.0 %all-to-all-done.4 = f32[8,128,128]{2,1,0:T(8,128)S(1)} async-done(((f32[8,128,128]{2,1,0:T(8,128)}), f32[8,128,128]{2,1,0:T(8,128)S(1)}, u32[]{:S(2)}, u32[]{:S(2)}) %all-to-all-start.4) | async-done | bytes 524320 | tf_op jit(solution)/shard_map/all_to_all | solution.py:417
  128.7 2.5 %all-gather.1 = f32[1152,128]{1,0:T(8,128)} all-gather(f32[576,128]{1,0:T(8,128)S(1)} %pad_maximum_fusion.2), channel_id=3, replica_groups={{0,16},{32,48},{64,80},{96,112},{128,144},{160,176},{192,208},{224,240}..., dimensions={0}, use_global_device_ids=true | all-gather | bytes 884736 | tf_op jit(solution)/shard_map/all_gather | solution.py:422
  131.2 5.7 %last_update.1 = f32[1024,1024]{1,0:T(8,128)} custom-call(f32[2,576,128]{2,1,0:T(8,128)} %bitcast.15, bf16[1024,384]{1,0:T(8,128)(2,1)} %copy-done.2, bf16[1024,384]{1,0:T(8,128)(2,1)} %copy-done.3, f32[1024,1024]{1,0:T(8,128)} %first_update.1.refs_3_), custom_call_target="tpu_custom_call" | custom-call | flops 805306368 | bytes 9000000 | tf_op jit(solution)/shard_map/last_update/pallas_call | solution.py:364
  (10 shorter events, 0.2 us)
Async XLA Ops:
  0.6 10.5 %copy-start.6 = (f32[64,128]{1,0:T(8,128)S(1)}, f32[64,128]{1,0:T(8,128)}, u32[]{:S(2)}) copy-start(f32[64,128]{1,0:T(8,128)} %param.2) | copy-start | bytes 98308
  3.6 23.1 %all-to-all-start = ((f32[16,128,128]{2,1,0:T(8,128)}), f32[16,128,128]{2,1,0:T(8,128)S(1)}, u32[]{:S(2)}, u32[]{:S(2)}) async-start(f32[16,128,128]{2,1,0:T(8,128)} %pad_maximum_fusion), calls=%async_computation | async-start | bytes 2097152 | tf_op jit(solution)/shard_map/all_to_all | solution.py:426
  11.2 8.9 %collective-permute-start = (f32[64,128]{1,0:T(8,128)S(1)}, f32[64,128]{1,0:T(8,128)S(1)}, u32[]{:S(2)}, u32[]{:S(2)}) collective-permute-start(f32[64,128]{1,0:T(8,128)S(1)} %copy-done.6), channel_id=1, source_target_pairs={{0,0},{1,16},{2,32},{3,48},{4,64},{5,80},{6,96},{7,112},{8,128},{9... | collective-permute-start | bytes 98312 | tf_op jit(solution)/shard_map/ppermute | solution.py:424
  27.9 4.1 %collective-permute-start.1 = (f32[64,128]{1,0:T(8,128)S(1)}, f32[64,128]{1,0:T(8,128)S(1)}, u32[]{:S(2)}, u32[]{:S(2)}) collective-permute-start(f32[64,128]{1,0:T(8,128)S(1)} %get-tuple-element.26), channel_id=1, source_target_pairs={{0,16},{16,0},{32,48},{48,32},{64,80},{80,64},{96,112},{112,96},{1... | collective-permute-start | bytes 98312 | tf_op jit(solution)/shard_map/ppermute | solution.py:415
  61.6 8.8 %copy-start = (f32[1168,128]{1,0:T(8,128)S(1)}, f32[1168,128]{1,0:T(8,128)}, u32[]{:S(2)}) copy-start(f32[1168,128]{1,0:T(8,128)} %all-gather) | copy-start | bytes 1794052
  66.6 14.7 %all-to-all-start.2 = ((f32[16,72,128]{2,1,0:T(8,128)}), f32[16,72,128]{2,1,0:T(8,128)S(1)}, u32[]{:S(2)}, u32[]{:S(2)}) async-start(f32[16,72,128]{2,1,0:T(8,128)} %partial_sums.1), calls=%async_computation.2 | async-start | bytes 1179648 | tf_op jit(solution)/shard_map/all_to_all | solution.py:434
  82.3 15.6 %all-to-all-start.3 = ((f32[16,64,128]{2,1,0:T(8,128)}), f32[16,64,128]{2,1,0:T(8,128)S(1)}, u32[]{:S(2)}, u32[]{:S(2)}) async-start(f32[16,64,128]{2,1,0:T(8,128)} %get-tuple-element.30), calls=%async_computation.3 | async-start | bytes 1048576 | tf_op jit(solution)/shard_map/all_to_all | solution.py:438
  86.2 11.7 %collective-permute-start.2 = (f32[64,128]{1,0:T(8,128)S(1)}, f32[64,128]{1,0:T(8,128)S(1)}, u32[]{:S(2)}, u32[]{:S(2)}) collective-permute-start(f32[64,128]{1,0:T(8,128)S(1)} %get-tuple-element.31), channel_id=1, source_target_pairs={{0,0},{1,16},{2,32},{3,48},{4,64},{5,80},{6,96},{7,112},{8,128},{9... | collective-permute-start | bytes 98312 | tf_op jit(solution)/shard_map/ppermute | solution.py:437
  95.2 0.9 copy-start.2
  96.1 0.9 copy-start.3
  97.0 0.9 copy-start.4
  97.9 12.8 %copy-start.5 = (f32[128,128]{1,0:T(8,128)}, f32[128,128]{1,0:T(8,128)S(1)}, u32[]{:S(2)}) copy-start(f32[128,128]{1,0:T(8,128)S(1)} %get-tuple-element.41.kernel_ref) | copy-start | bytes 196612
  97.9 12.8 %copy-start.1 = (f32[16,64,128]{2,1,0:T(8,128)}, f32[16,64,128]{2,1,0:T(8,128)S(1)}, u32[]{:S(2)}) copy-start(f32[16,64,128]{2,1,0:T(8,128)S(1)} %all-to-all-done.3) | copy-start | bytes 1572868
  99.1 1.7 %collective-permute-start.3 = (f32[64,128]{1,0:T(8,128)S(1)}, f32[64,128]{1,0:T(8,128)S(1)}, u32[]{:S(2)}, u32[]{:S(2)}) collective-permute-start(f32[64,128]{1,0:T(8,128)S(1)} %get-tuple-element.38), channel_id=1, source_target_pairs={{0,16},{16,0},{32,48},{48,32},{64,80},{80,64},{96,112},{112,96},{1... | collective-permute-start | bytes 98312 | tf_op jit(solution)/shard_map/ppermute | solution.py:415
  101.6 27.0 %all-to-all-start.4 = ((f32[8,128,128]{2,1,0:T(8,128)}), f32[8,128,128]{2,1,0:T(8,128)S(1)}, u32[]{:S(2)}, u32[]{:S(2)}) async-start(f32[8,128,128]{2,1,0:T(8,128)} %broadcast_in_dim.8), calls=%async_computation.4 | async-start | bytes 1048576 | tf_op jit(solution)/shard_map/all_to_all | solution.py:417

commit v4 on v3

--- a/solution.py
+++ b/solution.py
@@ -57,66 +57,77 @@
     )
 
 
-def keep_and_give(place_ref, value, keep_ref, give_ref):
+def pack(place_ref, value, keep_ref, give_ref):
     side = value.shape[0] // 2
+    half = side // 2
+    top = value[:side]
+    low = pltpu.roll(value[side:], side, 1)
+    row = lax.broadcasted_iota(jnp.int32, top.shape, 0)
+    lane = lax.broadcasted_iota(jnp.int32, top.shape, 1)
+    rows = jnp.where(jnp.logical_and(row < lane, lane < side), low, top)
+    last = jnp.sum(jnp.where(row == lane, low, 0.0), axis=0, keepdims=True)
     even = lax.rem(place_ref[0], 2) == 0
-    keep_ref[...] = jnp.where(even, value[:side], value[side:])
-    give_ref[...] = jnp.where(even, value[side:], value[:side])
-
-
-def gram_kernel(piece, place_ref, got_ref, rows_ref, keep_ref, give_ref, top_ref, first_ref):
+    keep_ref[:half, :] = jnp.where(even, rows[:half], rows[half:])
+    give_ref[:half, :] = jnp.where(even, rows[half:], rows[:half])
+    keep_ref[half:, :] = jnp.broadcast_to(last, (STEP, last.shape[1]))
+    give_ref[half:, :] = jnp.broadcast_to(last, (STEP, last.shape[1]))
+
+
+def unpack(packed):
+    half = packed.shape[1] - STEP
+    side = 2 * half
+    rows = packed[:, :half, :].reshape(side, packed.shape[2])
+    turned = rows.T
+    row = lax.broadcasted_iota(jnp.int32, (side, side), 0)
+    lane = lax.broadcasted_iota(jnp.int32, (side, side), 1)
+    left, across = rows[:, :side], turned[:side]
+    last = packed[0, half : half + 1, :side]
+    a = jnp.where(row >= lane, left, across)
+    d = jnp.where(row == lane, last, jnp.where(row < lane, left, across))
+    return jnp.concatenate(
+        [
+            jnp.concatenate([a, rows[:, side:]], 1),
+            jnp.concatenate([turned[side:], d], 1),
+        ],
+        0,
+    )
+
+
+def gram_kernel(place_ref, rows_ref, keep_ref, give_ref, top_ref):
     share = top_ref.shape[0]
-    rows = got_ref[:, :piece, :].reshape(rows_ref.shape)
-    rows_ref[...] = rows
-    keep_and_give(place_ref, product(rows, rows, TN), keep_ref, give_ref)
+    rows = rows_ref[...]
+    pack(place_ref, product(rows, rows, TN), keep_ref, give_ref)
     start = pl.multiple_of(place_ref[1] * share, share)
     top_ref[...] = rows_ref[pl.ds(start, share), :]
-    first_ref[...] = got_ref[0, piece:, :]
-
-
-def gram_parts(place, got, piece):
-    count, _, width = got.shape
-    vmem = pl.BlockSpec(memory_space=pltpu.VMEM)
-    shapes = [(count * piece, width), (width // 2, width), (width // 2, width)]
-    shapes += [(width // count, width), (piece, width)]
-    return pl.pallas_call(
-        lambda *refs: gram_kernel(piece, *refs),
-        in_specs=[pl.BlockSpec(memory_space=pltpu.SMEM), vmem],
-        out_specs=[vmem] * 5,
+
+
+def inner_kernel(place_ref, turned_ref, rows_ref, keep_ref, give_ref):
+    terms = product(turned_ref[...], rows_ref[...])
+    pack(place_ref, 0.5 * (terms + terms.T), keep_ref, give_ref)
+
+
+def packed_parts(kernel, place, operands, extra, name):
+    width = operands[-1].shape[1]
+    vmem = pl.BlockSpec(memory_space=pltpu.VMEM)
+    shapes = [(width // 4 + STEP, width)] * 2 + extra
+    return pl.pallas_call(
+        kernel,
+        in_specs=[pl.BlockSpec(memory_space=pltpu.SMEM)] + [vmem] * len(operands),
+        out_specs=[vmem] * len(shapes),
         out_shape=[jax.ShapeDtypeStruct(shape, jnp.float32) for shape in shapes],
         cost_estimate=pl.CostEstimate(
             flops=200_000_000, bytes_accessed=3_000_000, transcendentals=0
         ),
         compiler_params=pltpu.CompilerParams(vmem_limit_bytes=8 * MIB),
-        name="gram_parts",
-    )(place, got)
-
-
-def inner_kernel(place_ref, twisted_ref, rows_ref, keep_ref, give_ref):
-    keep_and_give(place_ref, product(twisted_ref[...], rows_ref[...]), keep_ref, give_ref)
-
-
-def inner_parts(place, twisted, rows):
-    width = rows.shape[1]
-    vmem = pl.BlockSpec(memory_space=pltpu.VMEM)
-    return pl.pallas_call(
-        inner_kernel,
-        in_specs=[pl.BlockSpec(memory_space=pltpu.SMEM), vmem, vmem],
-        out_specs=[vmem] * 2,
-        out_shape=[jax.ShapeDtypeStruct((width // 2, width), jnp.float32)] * 2,
-        cost_estimate=pl.CostEstimate(
-            flops=200_000_000, bytes_accessed=1_000_000, transcendentals=0
-        ),
-        compiler_params=pltpu.CompilerParams(vmem_limit_bytes=6 * MIB),
-        name="inner_parts",
-    )(place, twisted, rows)
+        name=name,
+    )(place, *operands)
 
 
 def factor_kernel(gram_ref, upper_ref, inverse_ref, work, other):
     width = upper_ref.shape[0]
     full = (STEP, width)
     lane = lax.broadcasted_iota(jnp.int32, full, 1)
-    work[...] = gram_ref[...].reshape(width, width)
+    work[...] = unpack(gram_ref[...])
     other[...] = eye(width)
     for first in range(0, width, STEP):
         a_rows = [jnp.broadcast_to(work[first + k : first + k + 1, :], full) for k in range(STEP)]
@@ -162,26 +173,26 @@
             other[g : g + STEP, :] = x_new
 
 
-def factor(pairs, start):
-    width = pairs.shape[2]
-    side = width // 2
+def factor(packed):
+    width = packed.shape[2]
     shape = jax.ShapeDtypeStruct((width, width), jnp.float32)
+    vmem = pl.BlockSpec(memory_space=pltpu.VMEM)
     return pl.pallas_call(
         factor_kernel,
-        grid=(1,),
-        in_specs=[pl.BlockSpec((2, side, width), lambda i: (0, start // side, 0))],
-        out_specs=[pl.BlockSpec((width, width), lambda i: (0, 0))] * 2,
+        in_specs=[vmem],
+        out_specs=[vmem] * 2,
         out_shape=(shape, shape),
         scratch_shapes=[pltpu.VMEM((width, width), jnp.float32)] * 2,
         cost_estimate=pl.CostEstimate(
-            flops=400_000_000, bytes_accessed=20_000_000, transcendentals=0
+            flops=400_000_000, bytes_accessed=200_000, transcendentals=0
         ),
         compiler_params=pltpu.CompilerParams(vmem_limit_bytes=4 * MIB),
         name="factor",
-    )(pairs)
-
-
-def partial_kernel(n_z, piece, share, pairs_ref, mob_ref, out_ref, rhs, held, sems):
+    )(packed)
+
+
+def partial_kernel(n_z, piece, share, place, pairs_ref, inverse_ref, mob_ref, *refs):
+    out_ref, rhs, held, sems = refs
     width = pairs_ref.shape[2]
     n_rows = held.shape[0]
     parts = sems.shape[0]
@@ -191,7 +202,10 @@
         rows = pl.ds(k * tile, tile)
         loads.append(pltpu.make_async_copy(mob_ref.at[rows], held.at[rows], sems.at[k]))
         loads[k].start()
-    high, low = split(pieces_of(pairs_ref, n_z, piece))
+    cols = exact_dot(
+        left_terms(pieces_of(pairs_ref, n_z, piece)), right_terms(inverse_ref[...]), NT
+    )
+    high, low = split(cols + unit_rows(place[1], cols.shape))
     rhs[:, :width] = high
     rhs[:, width:] = low
     last = pairs_ref.shape[1] - share
@@ -207,13 +221,13 @@
         out_ref[k * count : (k + 1) * count, :piece, :] = found.reshape(count, piece, width)
 
 
-def partial_sums(pairs, mobility, n_z, piece, share):
+def partial_sums(place, pairs, inverse, mobility, n_z, piece, share):
     n_rows, n_cols = mobility.shape
     width = pairs.shape[2]
     vmem = pl.BlockSpec(memory_space=pltpu.VMEM)
     return pl.pallas_call(
         lambda *refs: partial_kernel(n_z, piece, share, *refs),
-        in_specs=[vmem, pl.BlockSpec(memory_space=pl.ANY)],
+        in_specs=[pl.BlockSpec(memory_space=pltpu.SMEM), vmem, vmem, pl.BlockSpec(memory_space=pl.ANY)],
         out_specs=vmem,
         out_shape=jax.ShapeDtypeStruct((n_rows // piece, piece + share, width), jnp.float32),
         scratch_shapes=[
@@ -226,55 +240,56 @@
         ),
         compiler_params=pltpu.CompilerParams(vmem_limit_bytes=58 * MIB),
         name="partial_sums",
-    )(pairs, mobility)
-
-
-def image_kernel(piece, got_ref, first_ref, inverse_ref, image_ref, copies_ref, top_ref):
-    total = got_ref[0, :piece, :]
+    )(place, pairs, inverse, mobility)
+
+
+def image_kernel(piece, got_ref, image_ref, copies_ref, top_ref):
+    image = got_ref[0, :piece, :]
     for k in range(1, got_ref.shape[0]):
-        total = total + got_ref[k, :piece, :]
-    image = product(total, inverse_ref[...], NT) + first_ref[...]
+        image = image + got_ref[k, :piece, :]
     image_ref[...] = image
     copies_ref[...] = jnp.broadcast_to(image[None], copies_ref.shape)
     top_ref[...] = got_ref[:, piece:, :].reshape(top_ref.shape)
 
 
-def image_piece(got, first, inverse, piece):
+def image_piece(got, piece):
     count, _, width = got.shape
-    square = jax.ShapeDtypeStruct((width, width), jnp.float32)
+    vmem = pl.BlockSpec(memory_space=pltpu.VMEM)
     return pl.pallas_call(
         lambda *refs: image_kernel(piece, *refs),
-        grid=(1,),
-        in_specs=[
-            pl.BlockSpec(got.shape, lambda i: (0, 0, 0)),
-            pl.BlockSpec((piece, width), lambda i: (0, 0)),
-            pl.BlockSpec((width, width), lambda i: (0, 0)),
-        ],
-        out_specs=[
-            pl.BlockSpec((piece, width), lambda i: (0, 0)),
-            pl.BlockSpec((count, piece, width), lambda i: (0, 0, 0)),
-            pl.BlockSpec((width, width), lambda i: (0, 0)),
-        ],
+        in_specs=[vmem],
+        out_specs=[vmem] * 3,
         out_shape=(
             jax.ShapeDtypeStruct((piece, width), jnp.float32),
             jax.ShapeDtypeStruct((count, piece, width), jnp.float32),
-            square,
+            jax.ShapeDtypeStruct((width, width), jnp.float32),
         ),
         cost_estimate=pl.CostEstimate(
             flops=10_000_000, bytes_accessed=2_000_000, transcendentals=0
         ),
         compiler_params=pltpu.CompilerParams(vmem_limit_bytes=6 * MIB),
         name="image_piece",
-    )(got, first, inverse)
-
-
-def basis_kernel(n_z, piece, place, rows_ref, pairs_ref, inverse_ref, top_ref, *outs):
-    cols_left, cols_right, twisted, turned, kernel_ref, state_ref = outs
+    )(got)
+
+
+def basis_kernel(n_z, piece, place, rows_ref, pairs_ref, inverse_ref, *outs):
+    cols_ref, cols_right, basis_rows, turned_rows = outs
+    inverse_terms = right_terms(inverse_ref[...])
+    rows = exact_dot(left_terms(rows_ref[...]), inverse_terms, NT)
+    rows = rows + unit_rows(place[0], rows_ref.shape)
+    basis_rows[...] = rows
+    turned_rows[...] = rows.T
+    cols = exact_dot(left_terms(pieces_of(pairs_ref, n_z, piece)), inverse_terms, NT)
+    cols = cols + unit_rows(place[1], cols.shape)
+    cols_ref[...] = cols
+    cols_right[...] = right_terms(cols)
+
+
+def kernel_kernel(inverse_ref, top_ref, rows_ref, cols_ref, *outs):
+    cols_left, rows_left, kernel_ref, state_ref = outs
     width = inverse_ref.shape[0]
-    inverse = inverse_ref[...]
     identity = eye(width)
-    ratio = -product(inverse, top_ref[...], NT)
-
+    ratio = -product(inverse_ref[...], top_ref[...], NT)
     state_ref[:width, :] = ratio
     state_ref[width:, :] = identity
 
@@ -292,40 +307,26 @@
     total = state_ref[width:, :]
     kernel = total + product(total, identity - product(identity - ratio, total))
     kernel_ref[...] = kernel
-    inverse_terms = right_terms(inverse)
-    rows = exact_dot(left_terms(rows_ref[...]), inverse_terms, NT)
-    rows = rows + unit_rows(place[0], rows_ref.shape)
-    cols = exact_dot(left_terms(pieces_of(pairs_ref, n_z, piece)), inverse_terms, NT)
-    cols = cols + unit_rows(place[1], cols.shape)
-    cols_left[...] = left_terms(cols)
-    cols_right[...] = right_terms(cols)
-    terms = left_terms(rows)
-    twisted[...] = exact_dot(right_terms(kernel.T), terms, NT)
-    turned[...] = left_terms(exact_dot(terms, right_terms(kernel), NT))
-
-
-def bases(place, panel_rows, pairs, inverse, top_rows, n_z, piece):
-    width = inverse.shape[0]
-    terms = jax.ShapeDtypeStruct((panel_rows.shape[0], 3 * width), jnp.bfloat16)
-    vmem = pl.BlockSpec(memory_space=pltpu.VMEM)
-    return pl.pallas_call(
-        lambda *refs: basis_kernel(n_z, piece, *refs),
-        in_specs=[pl.BlockSpec(memory_space=pltpu.SMEM)] + [vmem] * 4,
-        out_specs=[vmem] * 5,
-        out_shape=(
-            terms,
-            terms,
-            jax.ShapeDtypeStruct(panel_rows.shape[::-1], jnp.float32),
-            terms,
-            jax.ShapeDtypeStruct((width, width), jnp.float32),
-        ),
-        scratch_shapes=[pltpu.VMEM((2 * width, width), jnp.float32)],
+    kernel_terms = right_terms(kernel)
+    cols_left[...] = left_terms(exact_dot(left_terms(cols_ref[...]), kernel_terms, NT))
+    rows_left[...] = left_terms(exact_dot(left_terms(rows_ref[...]), kernel_terms, NT))
+
+
+def side_call(kernel, operands, shapes, scratch, name):
+    vmem = pl.BlockSpec(memory_space=pltpu.VMEM)
+    smem = pl.BlockSpec(memory_space=pltpu.SMEM)
+    return pl.pallas_call(
+        kernel,
+        in_specs=[smem if operand.ndim == 1 else vmem for operand in operands],
+        out_specs=[vmem] * len(shapes),
+        out_shape=shapes,
+        scratch_shapes=scratch,
         cost_estimate=pl.CostEstimate(
             flops=300_000_000, bytes_accessed=10_000_000, transcendentals=0
         ),
-        compiler_params=pltpu.CompilerParams(vmem_limit_bytes=16 * MIB),
-        name="bases",
-    )(place, panel_rows, pairs, inverse, top_rows)
+        compiler_params=pltpu.CompilerParams(vmem_limit_bytes=58 * MIB),
+        name=name,
+    )(*operands)
 
 
 def stream(source_ref, out_ref, held, sems_in, sems_out, prepare, change):
@@ -381,12 +382,9 @@
 
 
 def last_update_kernel(n_z, piece, pairs_ref, cols_ref, turned_ref, half_ref, out_ref, rhs, held, *sems):
-    width = pairs_ref.shape[2]
-
     def prepare():
-        start = n_z * piece
-        small = pairs_ref[:, start : start + width // 2, :].reshape(width, width)
-        change_cols = exact_dot(cols_ref[...], right_terms(small.T), NT)
+        small = unpack(pairs_ref[:, n_z * piece :, :])
+        change_cols = exact_dot(cols_ref[...], right_terms(small), NT)
         rhs[...] = right_terms(pieces_of(pairs_ref, n_z, piece) - change_cols)
 
     def change(value, rows):
@@ -416,31 +414,48 @@
         sent = copies(jnp.concatenate([lone, summed] + extra, 0), n_z)
         parts = lax.all_to_all(sent, "row", 0, 0, axis_index_groups=z_groups)
         lone = parts[:, :piece].reshape(n_z * piece, width)
-        summed = jnp.sum(parts[:, piece : piece + width // 2], 0)
-        extra = [parts[0, piece + width // 2 :]] if extra else []
+        packed = summed.shape[0]
+        summed = jnp.sum(parts[:, piece : piece + packed], 0)
+        extra = [parts[0, piece + packed :]] if extra else []
         sent = jnp.concatenate([lone, summed] + extra, 0)
         return lax.all_gather(sent, "row", axis=0, axis_index_groups=pairs)
 
     turned_panel = lax.ppermute(panel, BOTH, transposing)
-    first_cols = mobility[:, :width].reshape(n_col, piece, width)
-    got = lax.all_to_all(
-        jnp.concatenate([copies(panel, n_col), first_cols], 1), "col", 0, 0
-    )
-    got, turned_panel = lax.optimization_barrier((got, turned_panel))
-    panel_rows, keep, give, top_part, first = gram_parts(place, got, piece)
+    panel_rows = lax.all_to_all(copies(panel, n_col), "col", 0, 0).reshape(block_rows, width)
+    panel_rows, turned_panel = lax.optimization_barrier((panel_rows, turned_panel))
+    keep, give, top_part = packed_parts(
+        gram_kernel, place, (panel_rows,), [(share, width)], "gram_parts"
+    )
     panel_pairs = gather_row(turned_panel, keep, give, [top_part])
 
-    sent = partial_sums(panel_pairs, mobility, n_z, piece, share)
+    start = n_z * piece
+    panel_factor, inverse = factor(panel_pairs[:, start : start + keep.shape[0]])
+    sent = partial_sums(place, panel_pairs, inverse, mobility, n_z, piece, share)
     got = lax.all_to_all(sent, "col", 0, 0)
-    panel_factor, inverse = factor(panel_pairs, n_z * piece)
-    image, image_copies, top_rows = image_piece(got, first, inverse, piece)
+    long = jax.ShapeDtypeStruct((block_rows, width), jnp.float32)
+    wide = jax.ShapeDtypeStruct((block_rows, 3 * width), jnp.bfloat16)
+    tall = jax.ShapeDtypeStruct((width, block_rows), jnp.float32)
+    square = jax.ShapeDtypeStruct((width, width), jnp.float32)
+    basis_cols, cols_right, basis_rows, turned_rows = side_call(
+        lambda *refs: basis_kernel(n_z, piece, *refs),
+        (place, panel_rows, panel_pairs, inverse),
+        [long, wide, long, tall],
+        [],
+        "bases",
+    )
+    got, turned_rows = lax.optimization_barrier((got, turned_rows))
+    image, image_copies, top_rows = image_piece(got, piece)
     turned_image = lax.ppermute(image, BOTH, transposing)
     image_rows = lax.all_to_all(image_copies, "col", 0, 0).reshape(block_rows, width)
-    cols_left, cols_right, twisted, turned, kernel = bases(
-        place, panel_rows, panel_pairs, inverse, top_rows, n_z, piece
+    cols_left, turned, kernel = side_call(
+        kernel_kernel,
+        (inverse, top_rows, basis_rows, basis_cols),
+        [wide, wide, square],
+        [pltpu.VMEM((2 * width, width), jnp.float32)],
+        "kernel",
     )
     image_rows, turned_image = lax.optimization_barrier((image_rows, turned_image))
-    keep, give = inner_parts(place, twisted, image_rows)
+    keep, give = packed_parts(inner_kernel, place, (turned_rows, image_rows), [], "inner_parts")
     image_pairs = gather_row(turned_image, keep, give, [])
     terms = 3 * width
     halfway = update_call(

time: 138 us -> 134 us (0.971)
  waiting for transfers between devices: 29.9 us -> 24.6 us
  Pallas kernels: 29.4 us -> 34.4 us
  starting transfers between devices: 38.1 us -> 35.5 us
    all_to_all x1, waiting for transfers between devices: 12 us -> 4.54 us  [gather_row(): parts = lax.all_to_all(sent, 'row', 0, 0, axis_index_groups=z_groups)]
    pallas_call x5 -> x6, Pallas kernels: 12.9 us -> 17.8 us  [the longest x2 8.55 us: side_call(): pl.pallas_call(kernel, in_specs=[smem if operand.ndim == 1 else vmem for...]
    ppermute x1, waiting for transfers between devices: 0.01 us -> 4.8 us  [on_device(): turned_image = lax.ppermute(image, BOTH, transposing)]
    all_to_all x1, starting transfers between devices: 9.05 us -> 4.92 us  [gather_row(): parts = lax.all_to_all(sent, 'row', 0, 0, axis_index_groups=z_groups)]
    all_to_all x1, waiting for transfers between devices: 6.59 us -> 3.12 us  [on_device(): lax.all_to_all(copies(panel, n_col), 'col', 0, 0).reshape(block_rows, width)]
    all_to_all x1, waiting for transfers between devices: 5.1 us -> 7.72 us  [on_device(): got = lax.all_to_all(sent, 'col', 0, 0)]
    ppermute x1, waiting for transfers between devices: 4.43 us -> 2.71 us  [on_device(): turned_panel = lax.ppermute(panel, BOTH, transposing)]
    unnamed x14 -> x16, local copies, waits for them, and re-layouts: 2.7 us -> 3.08 us
  transfers between devices with their start and end apart: 8 -> 8, of which waited for: 6 -> 7; matrix products, arithmetic and copies ran while one was open for 0% -> 0% of each run, Pallas kernels for 11% -> 11%
where the time goes in v4:
time: 134 us; the launch traced here: 133 us
  starting transfers between devices  35.5 us (26%)
  Pallas kernels  34.4 us (26%)
  blocking collectives  31.5 us (24%)
  waiting for transfers between devices  24.6 us (18%)
  local copies, waits for them, and re-layouts  5.54 us (4%)
    all_to_all x1, blocking collectives, gather_row(): parts = lax.all_to_all(sent, 'row', 0, 0, axis_index_groups=z_groups)  25.4 us
    pallas_call x2, Pallas kernels, update_call(): pl.pallas_call(kernel, in_specs=[vmem] * len(inputs) + [hbm], out_specs=h...  11.6 us
    pallas_call x2, Pallas kernels, side_call(): pl.pallas_call(kernel, in_specs=[smem if operand.ndim == 1 else vmem for...  8.55 us
    all_to_all x1, waiting for transfers between devices, on_device(): got = lax.all_to_all(sent, 'col', 0, 0)  7.72 us
    all_to_all x1, starting transfers between devices, on_device(): lax.all_to_all(copies(panel, n_col), 'col', 0, 0).reshape(block_rows, width)  7.58 us
    all_gather x2, blocking collectives, gather_row(): return lax.all_gather(sent, 'row', axis=0, axis_index_groups=pairs)  6.03 us
    pallas_call x1, Pallas kernels, factor(): pl.pallas_call(factor_kernel, in_specs=[vmem], out_specs=[vmem] * 2, out_...  5.86 us
    ppermute x1, starting transfers between devices, on_device(): turned_image = lax.ppermute(image, BOTH, transposing)  5.23 us
  transfers between devices with their start and end apart: 8, of which 7 were waited for; matrix products, arithmetic and copies ran while one was open for 0% of the time, Pallas kernels for 11%

profile of v4, /device:TPU:1, one launch (start us, length us, event | category | flops | bytes accessed | tf_op | source)
XLA Modules:
  0.0 132.6 jit_solution(9947154170557231134)
XLA Ops:
  0.6 1.6 %broadcast_in_dim.6 = f32[16,64,128]{2,1,0:T(8,128)} broadcast(f32[64,128]{1,0:T(8,128)} %param.2), dimensions={1,2} | broadcast | bytes 557056 | tf_op jit(solution)/shard_map/broadcast_in_dim | solution.py:410
  2.2 7.6 %all-to-all-start = ((f32[16,64,128]{2,1,0:T(8,128)}), f32[16,64,128]{2,1,0:T(8,128)S(1)}, u32[]{:S(2)}, u32[]{:S(2)}) async-start(f32[16,64,128]{2,1,0:T(8,128)} %broadcast_in_dim.6), calls=%async_computation | async-start | bytes 1048576 | tf_op jit(solution)/shard_map/all_to_all | solution.py:424
  9.8 4.4 %collective-permute-start = (f32[64,128]{1,0:T(8,128)}, f32[64,128]{1,0:T(8,128)S(1)}, u32[]{:S(2)}, u32[]{:S(2)}) collective-permute-start(f32[64,128]{1,0:T(8,128)} %param.2), channel_id=1, source_target_pairs={{0,0},{1,16},{2,32},{3,48},{4,64},{5,80},{6,96},{7,112},{8,128},{9... | collective-permute-start | bytes 98312 | tf_op jit(solution)/shard_map/ppermute | solution.py:423
  14.2 0.1 pad_add_fusion.place_ref.refs_0_
  14.3 0.0 copy-start.5
  14.3 2.7 %collective-permute-done = f32[64,128]{1,0:T(8,128)S(1)} collective-permute-done((f32[64,128]{1,0:T(8,128)}, f32[64,128]{1,0:T(8,128)S(1)}, u32[]{:S(2)}, u32[]{:S(2)}) %collective-permute-start) | collective-permute-done | bytes 32800 | tf_op jit(solution)/shard_map/ppermute | solution.py:423
  17.0 3.1 %all-to-all-done = f32[16,64,128]{2,1,0:T(8,128)S(1)} async-done(((f32[16,64,128]{2,1,0:T(8,128)}), f32[16,64,128]{2,1,0:T(8,128)S(1)}, u32[]{:S(2)}, u32[]{:S(2)}) %all-to-all-start) | async-done | bytes 524320 | tf_op jit(solution)/shard_map/all_to_all | solution.py:424
  20.1 0.0 copy-start.1
  20.1 1.3 gram_parts.1
  21.4 2.2 %collective-permute-start.1 = (f32[40,128]{1,0:T(8,128)S(1)}, f32[40,128]{1,0:T(8,128)S(1)}, u32[]{:S(2)}, u32[]{:S(2)}) collective-permute-start(f32[40,128]{1,0:T(8,128)S(1)} %get-tuple-element.28), channel_id=1, source_target_pairs={{0,16},{16,0},{32,48},{48,32},{64,80},{80,64},{96,112},{112,96},{1... | collective-permute-start | bytes 61448 | tf_op jit(solution)/shard_map/ppermute | solution.py:413
  23.6 0.8 collective-permute-done.1
  24.5 25.4 %all_to_all.25 = f32[8,112,128]{2,1,0:T(8,128)S(1)} all-to-all(f32[8,112,128]{2,1,0:T(8,128)S(1)} %broadcast_in_dim.7), channel_id=1, replica_groups={{0,32,64,96,128,160,192,224},{16,48,80,112,144,176,208,240},{1,33,65,97..., dimensions={0} | all-to-all | bytes 917504 | tf_op jit(solution)/shard_map/all_to_all | solution.py:415
  50.0 3.6 %all-gather = f32[1120,128]{1,0:T(8,128)S(1)} all-gather(f32[560,128]{1,0:T(8,128)S(1)} %pad_maximum_fusion), channel_id=2, replica_groups={{0,16},{32,48},{64,80},{96,112},{128,144},{160,176},{192,208},{224,240}..., dimensions={0}, use_global_device_ids=true | all-gather | bytes 860160 | tf_op jit(solution)/shard_map/all_gather | solution.py:421
  53.6 0.0 copy-start.7
  53.6 5.9 %factor.1 = (f32[128,128]{1,0:T(8,128)}, f32[128,128]{1,0:T(8,128)S(1)}) custom-call(f32[2,40,128]{2,1,0:T(8,128)S(1)} %slice.27.gram_ref), custom_call_target="tpu_custom_call" | custom-call | flops 400000000 | bytes 200000 | tf_op jit(solution)/shard_map/factor/pallas_call | solution.py:180
  59.5 0.0 copy-start.2
  59.5 0.6 copy-done.2
  60.1 0.0 copy-done.5
  60.1 0.0 copy-done.7
  60.1 5.0 %partial_sums.1 = f32[16,72,128]{2,1,0:T(8,128)} custom-call(s32[2]{0:T(128)} %copy-done.5, f32[2,560,128]{2,1,0:T(8,128)} %bitcast.15, f32[128,128]{1,0:T(8,128)} %copy-done.2, f32[1024,1024]{1,0:T(8,128)} %mob_ref.1), custom_call_target="tpu_custom_call" | custom-call | flops 805306368 | bytes 6000000 | tf_op jit(solution)/shard_map/partial_sums/pallas_call | solution.py:228
  65.1 0.0 copy-done.1
  65.1 4.8 %all-to-all-start.2 = ((f32[16,72,128]{2,1,0:T(8,128)}), f32[16,72,128]{2,1,0:T(8,128)S(1)}, u32[]{:S(2)}, u32[]{:S(2)}) async-start(f32[16,72,128]{2,1,0:T(8,128)} %partial_sums.1), calls=%async_computation.2 | async-start | bytes 1179648 | tf_op jit(solution)/shard_map/all_to_all | solution.py:434
  69.8 3.2 %bases.1 = (f32[1024,128]{1,0:T(8,128)}, bf16[1024,384]{1,0:T(8,128)(2,1)}, f32[1024,128]{1,0:T(8,128)}, f32[128,1024]{1,0:T(8,128)}) custom-call(s32[2]{0:T(128)} %copy-done.5, f32[1024,128]{1,0:T(8,128)} %bitcast.13, f32[2,560,128]{2,1,0:T(8,128)} %bitcast.16, f32[128,128]{1,0:T(8,128)} %copy-done.2), custom_call_target="tpu_custom_call" | custom-call | flops 300000000 | bytes 10000000 | tf_op jit(solution)/shard_map/bases/pallas_call | solution.py:318
  73.0 7.7 %all-to-all-done.2.refs_0_ = f32[16,72,128]{2,1,0:T(8,128)S(1)} async-done(((f32[16,72,128]{2,1,0:T(8,128)}), f32[16,72,128]{2,1,0:T(8,128)S(1)}, u32[]{:S(2)}, u32[]{:S(2)}) %all-to-all-start.2) | async-done | bytes 589856 | tf_op jit(solution)/shard_map/all_to_all | solution.py:434
  80.7 0.9 image_piece.1
  81.6 0.0 copy-start.4
  81.6 0.6 copy-done.4
  82.2 3.9 %all-to-all-start.3 = ((f32[16,64,128]{2,1,0:T(8,128)}), f32[16,64,128]{2,1,0:T(8,128)S(1)}, u32[]{:S(2)}, u32[]{:S(2)}) async-start(f32[16,64,128]{2,1,0:T(8,128)} %get-tuple-element.33), calls=%async_computation.3 | async-start | bytes 1048576 | tf_op jit(solution)/shard_map/all_to_all | solution.py:449
  86.1 5.2 %collective-permute-start.2 = (f32[64,128]{1,0:T(8,128)S(1)}, f32[64,128]{1,0:T(8,128)S(1)}, u32[]{:S(2)}, u32[]{:S(2)}) collective-permute-start(f32[64,128]{1,0:T(8,128)S(1)} %get-tuple-element.34), channel_id=1, source_target_pairs={{0,0},{1,16},{2,32},{3,48},{4,64},{5,80},{6,96},{7,112},{8,128},{9... | collective-permute-start | bytes 98312 | tf_op jit(solution)/shard_map/ppermute | solution.py:448
  91.4 4.8 %collective-permute-done.2 = f32[64,128]{1,0:T(8,128)S(1)} collective-permute-done((f32[64,128]{1,0:T(8,128)S(1)}, f32[64,128]{1,0:T(8,128)S(1)}, u32[]{:S(2)}, u32[]{:S(2)}) %collective-permute-start.2) | collective-permute-done | bytes 32800 | tf_op jit(solution)/shard_map/ppermute | solution.py:448
  96.2 0.0 all-to-all-done.3
  96.2 0.0 copy-start
  96.2 0.0 copy-start.3
  96.2 1.2 copy-done.3
  97.4 0.0 copy-start.6
  97.4 0.6 copy-done.6
  98.0 1.3 inner_parts.1
  99.3 2.5 %collective-permute-start.3 = (f32[40,128]{1,0:T(8,128)S(1)}, f32[40,128]{1,0:T(8,128)S(1)}, u32[]{:S(2)}, u32[]{:S(2)}) collective-permute-start(f32[40,128]{1,0:T(8,128)S(1)} %get-tuple-element.39), channel_id=1, source_target_pairs={{0,16},{16,0},{32,48},{48,32},{64,80},{80,64},{96,112},{112,96},{1... | collective-permute-start | bytes 61448 | tf_op jit(solution)/shard_map/ppermute | solution.py:413
  101.8 0.8 collective-permute-done.3
  102.6 0.8 broadcast_in_dim.8
  103.4 4.9 %all-to-all-start.4 = ((f32[8,104,128]{2,1,0:T(8,128)}), f32[8,104,128]{2,1,0:T(8,128)S(1)}, u32[]{:S(2)}, u32[]{:S(2)}) async-start(f32[8,104,128]{2,1,0:T(8,128)} %broadcast_in_dim.8), calls=%async_computation.4 | async-start | bytes 851968 | tf_op jit(solution)/shard_map/all_to_all | solution.py:415
  108.3 5.4 %kernel.1 = (bf16[1024,384]{1,0:T(8,128)(2,1)}, bf16[1024,384]{1,0:T(8,128)(2,1)}, f32[128,128]{1,0:T(8,128)}) custom-call(f32[128,128]{1,0:T(8,128)} %copy-done.2, f32[128,128]{1,0:T(8,128)} %copy-done.4, f32[1024,128]{1,0:T(8,128)} %get-tuple-element.41.rows_ref, f32[1024,128]{1,0:T(8,128)} %get-tuple-element.42.cols_ref), custom_call_target="tpu_custom_call" | custom-call | flops 300000000 | bytes 10000000 | tf_op jit(solution)/shard_map/kernel/pallas_call | solution.py:318
  113.7 0.0 copy-done
  113.7 5.9 %first_update.1.refs_3_ = f32[1024,1024]{1,0:T(8,128)} custom-call(f32[1024,128]{1,0:T(8,128)} %bitcast.11, f32[128,128]{1,0:T(8,128)} %get-tuple-element.45.kernel_ref, bf16[1024,384]{1,0:T(8,128)(2,1)} %get-tuple-element.46.cols_ref, f32[1024,1024]{1,0:T(8,128)} %mob_ref.1), custom_call_target="tpu_custom_call" | custom-call | flops 805306368 | bytes 9000000 | tf_op jit(solution)/shard_map/first_update/pallas_call | solution.py:365
  119.7 4.5 %all-to-all-done.4 = f32[8,104,128]{2,1,0:T(8,128)S(1)} async-done(((f32[8,104,128]{2,1,0:T(8,128)}), f32[8,104,128]{2,1,0:T(8,128)S(1)}, u32[]{:S(2)}, u32[]{:S(2)}) %all-to-all-start.4) | async-done | bytes 426016 | tf_op jit(solution)/shard_map/all_to_all | solution.py:415
  124.3 2.5 %all-gather.1 = f32[1104,128]{1,0:T(8,128)} all-gather(f32[552,128]{1,0:T(8,128)S(1)} %pad_maximum_fusion.1), channel_id=3, replica_groups={{0,16},{32,48},{64,80},{96,112},{128,144},{160,176},{192,208},{224,240}..., dimensions={0}, use_global_device_ids=true | all-gather | bytes 847872 | tf_op jit(solution)/shard_map/all_gather | solution.py:421
  126.7 5.7 %last_update.1 = f32[1024,1024]{1,0:T(8,128)} custom-call(f32[2,552,128]{2,1,0:T(8,128)} %bitcast.17, bf16[1024,384]{1,0:T(8,128)(2,1)} %get-tuple-element.43.refs_1_, bf16[1024,384]{1,0:T(8,128)(2,1)} %get-tuple-element.44.refs_2_, f32[1024,1024]{1,0:T(8,128)} %first_update.1.refs_3_), custom_call_target="tpu_custom_call" | custom-call | flops 805306368 | bytes 9000000 | tf_op jit(solution)/shard_map/last_update/pallas_call | solution.py:365
  (13 shorter events, 0.2 us)
Async XLA Ops:
  2.2 17.9 %all-to-all-start = ((f32[16,64,128]{2,1,0:T(8,128)}), f32[16,64,128]{2,1,0:T(8,128)S(1)}, u32[]{:S(2)}, u32[]{:S(2)}) async-start(f32[16,64,128]{2,1,0:T(8,128)} %broadcast_in_dim.6), calls=%async_computation | async-start | bytes 1048576 | tf_op jit(solution)/shard_map/all_to_all | solution.py:424
  9.8 7.2 %collective-permute-start = (f32[64,128]{1,0:T(8,128)}, f32[64,128]{1,0:T(8,128)S(1)}, u32[]{:S(2)}, u32[]{:S(2)}) collective-permute-start(f32[64,128]{1,0:T(8,128)} %param.2), channel_id=1, source_target_pairs={{0,0},{1,16},{2,32},{3,48},{4,64},{5,80},{6,96},{7,112},{8,128},{9... | collective-permute-start | bytes 98312 | tf_op jit(solution)/shard_map/ppermute | solution.py:423
  14.3 45.8 %copy-start.5 = (s32[2]{0:T(128)}, s32[2]{0:T(128)S(1)}, u32[]{:S(2)}) copy-start(s32[2]{0:T(128)S(1)} %pad_add_fusion.place_ref.refs_0_) | copy-start | bytes 28
  20.1 44.9 %copy-start.1 = (f32[16,64,128]{2,1,0:T(8,128)}, f32[16,64,128]{2,1,0:T(8,128)S(1)}, u32[]{:S(2)}) copy-start(f32[16,64,128]{2,1,0:T(8,128)S(1)} %all-to-all-done) | copy-start | bytes 1572868
  21.4 3.1 %collective-permute-start.1 = (f32[40,128]{1,0:T(8,128)S(1)}, f32[40,128]{1,0:T(8,128)S(1)}, u32[]{:S(2)}, u32[]{:S(2)}) collective-permute-start(f32[40,128]{1,0:T(8,128)S(1)} %get-tuple-element.28), channel_id=1, source_target_pairs={{0,16},{16,0},{32,48},{48,32},{64,80},{80,64},{96,112},{112,96},{1... | collective-permute-start | bytes 61448 | tf_op jit(solution)/shard_map/ppermute | solution.py:413
  53.6 6.5 %copy-start.7 = (f32[1120,128]{1,0:T(8,128)}, f32[1120,128]{1,0:T(8,128)S(1)}, u32[]{:S(2)}) copy-start(f32[1120,128]{1,0:T(8,128)S(1)} %all-gather) | copy-start | bytes 1720324
  59.5 0.6 copy-start.2
  65.1 15.6 %all-to-all-start.2 = ((f32[16,72,128]{2,1,0:T(8,128)}), f32[16,72,128]{2,1,0:T(8,128)S(1)}, u32[]{:S(2)}, u32[]{:S(2)}) async-start(f32[16,72,128]{2,1,0:T(8,128)} %partial_sums.1), calls=%async_computation.2 | async-start | bytes 1179648 | tf_op jit(solution)/shard_map/all_to_all | solution.py:434
  81.6 0.6 copy-start.4
  82.2 14.0 %all-to-all-start.3 = ((f32[16,64,128]{2,1,0:T(8,128)}), f32[16,64,128]{2,1,0:T(8,128)S(1)}, u32[]{:S(2)}, u32[]{:S(2)}) async-start(f32[16,64,128]{2,1,0:T(8,128)} %get-tuple-element.33), calls=%async_computation.3 | async-start | bytes 1048576 | tf_op jit(solution)/shard_map/all_to_all | solution.py:449
  86.1 10.0 %collective-permute-start.2 = (f32[64,128]{1,0:T(8,128)S(1)}, f32[64,128]{1,0:T(8,128)S(1)}, u32[]{:S(2)}, u32[]{:S(2)}) collective-permute-start(f32[64,128]{1,0:T(8,128)S(1)} %get-tuple-element.34), channel_id=1, source_target_pairs={{0,0},{1,16},{2,32},{3,48},{4,64},{5,80},{6,96},{7,112},{8,128},{9... | collective-permute-start | bytes 98312 | tf_op jit(solution)/shard_map/ppermute | solution.py:448
  96.2 17.6 %copy-start = (f32[16,64,128]{2,1,0:T(8,128)}, f32[16,64,128]{2,1,0:T(8,128)S(1)}, u32[]{:S(2)}) copy-start(f32[16,64,128]{2,1,0:T(8,128)S(1)} %all-to-all-done.3) | copy-start | bytes 1572868
  96.2 1.2 copy-start.3
  97.4 0.6 copy-start.6
  99.3 3.3 %collective-permute-start.3 = (f32[40,128]{1,0:T(8,128)S(1)}, f32[40,128]{1,0:T(8,128)S(1)}, u32[]{:S(2)}, u32[]{:S(2)}) collective-permute-start(f32[40,128]{1,0:T(8,128)S(1)} %get-tuple-element.39), channel_id=1, source_target_pairs={{0,16},{16,0},{32,48},{48,32},{64,80},{80,64},{96,112},{112,96},{1... | collective-permute-start | bytes 61448 | tf_op jit(solution)/shard_map/ppermute | solution.py:413
  103.4 20.8 %all-to-all-start.4 = ((f32[8,104,128]{2,1,0:T(8,128)}), f32[8,104,128]{2,1,0:T(8,128)S(1)}, u32[]{:S(2)}, u32[]{:S(2)}) async-start(f32[8,104,128]{2,1,0:T(8,128)} %broadcast_in_dim.8), calls=%async_computation.4 | async-start | bytes 851968 | tf_op jit(solution)/shard_map/all_to_all | solution.py:415

commit v5 on v4

--- a/solution.py
+++ b/solution.py
@@ -57,7 +57,7 @@
     )
 
 
-def pack(place_ref, value, keep_ref, give_ref):
+def pack(value, keep_ref, give_ref):
     side = value.shape[0] // 2
     half = side // 2
     top = value[:side]
@@ -66,7 +66,7 @@
     lane = lax.broadcasted_iota(jnp.int32, top.shape, 1)
     rows = jnp.where(jnp.logical_and(row < lane, lane < side), low, top)
     last = jnp.sum(jnp.where(row == lane, low, 0.0), axis=0, keepdims=True)
-    even = lax.rem(place_ref[0], 2) == 0
+    even = lax.rem(lax.axis_index("row"), 2) == 0
     keep_ref[:half, :] = jnp.where(even, rows[:half], rows[half:])
     give_ref[:half, :] = jnp.where(even, rows[half:], rows[:half])
     keep_ref[half:, :] = jnp.broadcast_to(last, (STEP, last.shape[1]))
@@ -93,26 +93,26 @@
     )
 
 
-def gram_kernel(place_ref, rows_ref, keep_ref, give_ref, top_ref):
+def gram_kernel(rows_ref, keep_ref, give_ref, top_ref):
     share = top_ref.shape[0]
     rows = rows_ref[...]
-    pack(place_ref, product(rows, rows, TN), keep_ref, give_ref)
-    start = pl.multiple_of(place_ref[1] * share, share)
+    pack(product(rows, rows, TN), keep_ref, give_ref)
+    start = pl.multiple_of(lax.axis_index("col") * share, share)
     top_ref[...] = rows_ref[pl.ds(start, share), :]
 
 
-def inner_kernel(place_ref, turned_ref, rows_ref, keep_ref, give_ref):
+def inner_kernel(turned_ref, rows_ref, keep_ref, give_ref):
     terms = product(turned_ref[...], rows_ref[...])
-    pack(place_ref, 0.5 * (terms + terms.T), keep_ref, give_ref)
-
-
-def packed_parts(kernel, place, operands, extra, name):
+    pack(0.5 * (terms + terms.T), keep_ref, give_ref)
+
+
+def packed_parts(kernel, operands, extra, name):
     width = operands[-1].shape[1]
     vmem = pl.BlockSpec(memory_space=pltpu.VMEM)
     shapes = [(width // 4 + STEP, width)] * 2 + extra
     return pl.pallas_call(
         kernel,
-        in_specs=[pl.BlockSpec(memory_space=pltpu.SMEM)] + [vmem] * len(operands),
+        in_specs=[vmem] * len(operands),
         out_specs=[vmem] * len(shapes),
         out_shape=[jax.ShapeDtypeStruct(shape, jnp.float32) for shape in shapes],
         cost_estimate=pl.CostEstimate(
@@ -120,7 +120,7 @@
         ),
         compiler_params=pltpu.CompilerParams(vmem_limit_bytes=8 * MIB),
         name=name,
-    )(place, *operands)
+    )(*operands)
 
 
 def factor_kernel(gram_ref, upper_ref, inverse_ref, work, other):
@@ -191,21 +191,14 @@
     )(packed)
 
 
-def partial_kernel(n_z, piece, share, place, pairs_ref, inverse_ref, mob_ref, *refs):
-    out_ref, rhs, held, sems = refs
+def partial_kernel(n_z, piece, share, pairs_ref, inverse_ref, mob_ref, out_ref, rhs):
     width = pairs_ref.shape[2]
-    n_rows = held.shape[0]
-    parts = sems.shape[0]
-    tile = n_rows // parts
-    loads = []
-    for k in range(parts):
-        rows = pl.ds(k * tile, tile)
-        loads.append(pltpu.make_async_copy(mob_ref.at[rows], held.at[rows], sems.at[k]))
-        loads[k].start()
+    n_rows = mob_ref.shape[0]
+    tile = 256
     cols = exact_dot(
         left_terms(pieces_of(pairs_ref, n_z, piece)), right_terms(inverse_ref[...]), NT
     )
-    high, low = split(cols + unit_rows(place[1], cols.shape))
+    high, low = split(cols + unit_rows(lax.axis_index("col"), cols.shape))
     rhs[:, :width] = high
     rhs[:, width:] = low
     last = pairs_ref.shape[1] - share
@@ -213,34 +206,29 @@
         pairs_ref[0, last:, :][None], (out_ref.shape[0], share, width)
     )
     count = tile // piece
-    for k in range(parts):
-        loads[k].wait()
-        high, low = split(held[k * tile : (k + 1) * tile, :])
+    for k in range(n_rows // tile):
+        high, low = split(mob_ref[k * tile : (k + 1) * tile, :])
         wide = exact_dot(high, rhs[...], NN)
         found = wide[:, :width] + wide[:, width:] + exact_dot(low, rhs[:, :width], NN)
         out_ref[k * count : (k + 1) * count, :piece, :] = found.reshape(count, piece, width)
 
 
-def partial_sums(place, pairs, inverse, mobility, n_z, piece, share):
+def partial_sums(pairs, inverse, mobility, n_z, piece, share):
     n_rows, n_cols = mobility.shape
     width = pairs.shape[2]
     vmem = pl.BlockSpec(memory_space=pltpu.VMEM)
     return pl.pallas_call(
         lambda *refs: partial_kernel(n_z, piece, share, *refs),
-        in_specs=[pl.BlockSpec(memory_space=pltpu.SMEM), vmem, vmem, pl.BlockSpec(memory_space=pl.ANY)],
+        in_specs=[vmem] * 3,
         out_specs=vmem,
         out_shape=jax.ShapeDtypeStruct((n_rows // piece, piece + share, width), jnp.float32),
-        scratch_shapes=[
-            pltpu.VMEM((n_cols, 2 * width), jnp.bfloat16),
-            pltpu.VMEM(mobility.shape, jnp.float32),
-            pltpu.SemaphoreType.DMA((4,)),
-        ],
+        scratch_shapes=[pltpu.VMEM((n_cols, 2 * width), jnp.bfloat16)],
         cost_estimate=pl.CostEstimate(
             flops=6 * n_rows * n_cols * width, bytes_accessed=6_000_000, transcendentals=0
         ),
-        compiler_params=pltpu.CompilerParams(vmem_limit_bytes=58 * MIB),
+        compiler_params=pltpu.CompilerParams(vmem_limit_bytes=14 * MIB),
         name="partial_sums",
-    )(place, pairs, inverse, mobility)
+    )(pairs, inverse, mobility)
 
 
 def image_kernel(piece, got_ref, image_ref, copies_ref, top_ref):
@@ -272,21 +260,13 @@
     )(got)
 
 
-def basis_kernel(n_z, piece, place, rows_ref, pairs_ref, inverse_ref, *outs):
-    cols_ref, cols_right, basis_rows, turned_rows = outs
-    inverse_terms = right_terms(inverse_ref[...])
-    rows = exact_dot(left_terms(rows_ref[...]), inverse_terms, NT)
-    rows = rows + unit_rows(place[0], rows_ref.shape)
-    basis_rows[...] = rows
-    turned_rows[...] = rows.T
-    cols = exact_dot(left_terms(pieces_of(pairs_ref, n_z, piece)), inverse_terms, NT)
-    cols = cols + unit_rows(place[1], cols.shape)
-    cols_ref[...] = cols
-    cols_right[...] = right_terms(cols)
-
-
-def kernel_kernel(inverse_ref, top_ref, rows_ref, cols_ref, *outs):
-    cols_left, rows_left, kernel_ref, state_ref = outs
+def rows_kernel(rows_ref, inverse_ref, turned_ref):
+    rows = exact_dot(left_terms(rows_ref[...]), right_terms(inverse_ref[...]), NT)
+    turned_ref[...] = (rows + unit_rows(lax.axis_index("row"), rows.shape)).T
+
+
+def kernel_kernel(n_z, piece, inverse_ref, top_ref, turned_ref, pairs_ref, *outs):
+    cols_left, cols_right, rows_left, kernel_ref, state_ref = outs
     width = inverse_ref.shape[0]
     identity = eye(width)
     ratio = -product(inverse_ref[...], top_ref[...], NT)
@@ -308,23 +288,27 @@
     kernel = total + product(total, identity - product(identity - ratio, total))
     kernel_ref[...] = kernel
     kernel_terms = right_terms(kernel)
-    cols_left[...] = left_terms(exact_dot(left_terms(cols_ref[...]), kernel_terms, NT))
-    rows_left[...] = left_terms(exact_dot(left_terms(rows_ref[...]), kernel_terms, NT))
+    cols = exact_dot(
+        left_terms(pieces_of(pairs_ref, n_z, piece)), right_terms(inverse_ref[...]), NT
+    )
+    cols = cols + unit_rows(lax.axis_index("col"), cols.shape)
+    cols_right[...] = right_terms(cols)
+    cols_left[...] = left_terms(exact_dot(left_terms(cols), kernel_terms, NT))
+    rows_left[...] = left_terms(exact_dot(left_terms(turned_ref[...].T), kernel_terms, NT))
 
 
 def side_call(kernel, operands, shapes, scratch, name):
     vmem = pl.BlockSpec(memory_space=pltpu.VMEM)
-    smem = pl.BlockSpec(memory_space=pltpu.SMEM)
     return pl.pallas_call(
         kernel,
-        in_specs=[smem if operand.ndim == 1 else vmem for operand in operands],
+        in_specs=[vmem] * len(operands),
         out_specs=[vmem] * len(shapes),
         out_shape=shapes,
         scratch_shapes=scratch,
         cost_estimate=pl.CostEstimate(
             flops=300_000_000, bytes_accessed=10_000_000, transcendentals=0
         ),
-        compiler_params=pltpu.CompilerParams(vmem_limit_bytes=58 * MIB),
+        compiler_params=pltpu.CompilerParams(vmem_limit_bytes=14 * MIB),
         name=name,
     )(*operands)
 
@@ -361,12 +345,13 @@
 def update_call(kernel, inputs, matrix, terms, name):
     n_rows, n_cols = matrix.shape
     vmem = pl.BlockSpec(memory_space=pltpu.VMEM)
-    hbm = pl.BlockSpec(memory_space=pl.ANY)
+    hbm = pl.BlockSpec(memory_space=pltpu.HBM)
+    matrix = pltpu.with_memory_space_constraint(matrix, pltpu.HBM)
     return pl.pallas_call(
         kernel,
         in_specs=[vmem] * len(inputs) + [hbm],
         out_specs=hbm,
-        out_shape=jax.ShapeDtypeStruct(matrix.shape, jnp.float32),
+        out_shape=pltpu.HBM(matrix.shape, jnp.float32),
         scratch_shapes=[
             pltpu.VMEM((n_rows, terms), jnp.bfloat16),
             pltpu.VMEM(matrix.shape, jnp.float32),
@@ -376,7 +361,7 @@
         cost_estimate=pl.CostEstimate(
             flops=2 * n_rows * n_cols * terms, bytes_accessed=9_000_000, transcendentals=0
         ),
-        compiler_params=pltpu.CompilerParams(vmem_limit_bytes=58 * MIB),
+        compiler_params=pltpu.CompilerParams(vmem_limit_bytes=14 * MIB),
         name=name,
     )(*inputs, matrix)
 
@@ -397,8 +382,6 @@
     piece, width = panel.shape
     n_row, n_col = lax.axis_size("row"), lax.axis_size("col")
     block_rows, block_cols = mobility.shape
-    row, col = lax.axis_index("row"), lax.axis_index("col")
-    place = jnp.stack([row, col]).astype(jnp.int32)
     n_z = n_row // 2
     share = width // n_col
     z_groups = [[2 * z + h for z in range(n_z)] for h in range(2)]
@@ -424,38 +407,31 @@
     panel_rows = lax.all_to_all(copies(panel, n_col), "col", 0, 0).reshape(block_rows, width)
     panel_rows, turned_panel = lax.optimization_barrier((panel_rows, turned_panel))
     keep, give, top_part = packed_parts(
-        gram_kernel, place, (panel_rows,), [(share, width)], "gram_parts"
+        gram_kernel, (panel_rows,), [(share, width)], "gram_parts"
     )
     panel_pairs = gather_row(turned_panel, keep, give, [top_part])
 
     start = n_z * piece
     panel_factor, inverse = factor(panel_pairs[:, start : start + keep.shape[0]])
-    sent = partial_sums(place, panel_pairs, inverse, mobility, n_z, piece, share)
+    sent = partial_sums(panel_pairs, inverse, mobility, n_z, piece, share)
     got = lax.all_to_all(sent, "col", 0, 0)
-    long = jax.ShapeDtypeStruct((block_rows, width), jnp.float32)
     wide = jax.ShapeDtypeStruct((block_rows, 3 * width), jnp.bfloat16)
     tall = jax.ShapeDtypeStruct((width, block_rows), jnp.float32)
     square = jax.ShapeDtypeStruct((width, width), jnp.float32)
-    basis_cols, cols_right, basis_rows, turned_rows = side_call(
-        lambda *refs: basis_kernel(n_z, piece, *refs),
-        (place, panel_rows, panel_pairs, inverse),
-        [long, wide, long, tall],
-        [],
-        "bases",
-    )
+    (turned_rows,) = side_call(rows_kernel, (panel_rows, inverse), [tall], [], "basis_rows")
     got, turned_rows = lax.optimization_barrier((got, turned_rows))
     image, image_copies, top_rows = image_piece(got, piece)
     turned_image = lax.ppermute(image, BOTH, transposing)
     image_rows = lax.all_to_all(image_copies, "col", 0, 0).reshape(block_rows, width)
-    cols_left, turned, kernel = side_call(
-        kernel_kernel,
-        (inverse, top_rows, basis_rows, basis_cols),
-        [wide, wide, square],
+    cols_left, cols_right, rows_left, kernel = side_call(
+        lambda *refs: kernel_kernel(n_z, piece, *refs),
+        (inverse, top_rows, turned_rows, panel_pairs),
+        [wide, wide, wide, square],
         [pltpu.VMEM((2 * width, width), jnp.float32)],
         "kernel",
     )
     image_rows, turned_image = lax.optimization_barrier((image_rows, turned_image))
-    keep, give = packed_parts(inner_kernel, place, (turned_rows, image_rows), [], "inner_parts")
+    keep, give = packed_parts(inner_kernel, (turned_rows, image_rows), [], "inner_parts")
     image_pairs = gather_row(turned_image, keep, give, [])
     terms = 3 * width
     halfway = update_call(
@@ -463,7 +439,7 @@
     )
     updated = update_call(
         lambda *refs: last_update_kernel(n_z, piece, *refs),
-        (image_pairs, cols_left, turned),
+        (image_pairs, cols_left, rows_left),
         halfway,
         terms,
         "last_update",

time: 134 us -> 128 us (0.955)
  Pallas kernels: 34.4 us -> 23.1 us
  waiting for transfers between devices: 24.6 us -> 30.9 us
  local copies, waits for them, and re-layouts: 5.54 us -> 3.42 us
    pallas_call x4, Pallas kernels: 11.1 us -> 5.07 us  [the longest x2 3.61 us: side_call(): pl.pallas_call(kernel, in_specs=[vmem] * len(operands), out_specs=[vmem]...]
    all_to_all x1, waiting for transfers between devices: 4.54 us -> 8.09 us  [gather_row(): parts = lax.all_to_all(sent, 'row', 0, 0, axis_index_groups=z_groups)]
    unnamed x16 -> x2, local copies, waits for them, and re-layouts: 3.08 us -> 0.01 us
    pallas_call x2, Pallas kernels: 11.6 us -> 8.86 us  [update_call(): pl.pallas_call(kernel, in_specs=[vmem] * len(inputs) + [hbm], out_specs=h...]
    all_to_all x1, waiting for transfers between devices: 7.72 us -> 10.4 us  [on_device(): got = lax.all_to_all(sent, 'col', 0, 0)]
    pallas_call x1, Pallas kernels: 4.96 us -> 2.43 us  [partial_sums(): pl.pallas_call(lambda *refs: partial_kernel(n_z, piece, share, *refs), in...]
  transfers between devices with their start and end apart: 8 -> 8, of which waited for: 7 -> 7; matrix products, arithmetic and copies ran while one was open for 0% -> 0% of each run, Pallas kernels for 11% -> 7%
where the time goes in v5:
time: 128 us; the launch traced here: 126 us
  starting transfers between devices  35.5 us (28%)
  blocking collectives  31.3 us (24%)
  waiting for transfers between devices  30.9 us (24%)
  Pallas kernels  23.1 us (18%)
  local copies, waits for them, and re-layouts  3.42 us (3%)
    all_to_all x1, blocking collectives, gather_row(): parts = lax.all_to_all(sent, 'row', 0, 0, axis_index_groups=z_groups)  25.4 us
    all_to_all x1, waiting for transfers between devices, on_device(): got = lax.all_to_all(sent, 'col', 0, 0)  10.4 us
    pallas_call x2, Pallas kernels, update_call(): pl.pallas_call(kernel, in_specs=[vmem] * len(inputs) + [hbm], out_specs=h...  8.86 us
    all_to_all x1, waiting for transfers between devices, gather_row(): parts = lax.all_to_all(sent, 'row', 0, 0, axis_index_groups=z_groups)  8.09 us
    all_to_all x1, starting transfers between devices, on_device(): lax.all_to_all(copies(panel, n_col), 'col', 0, 0).reshape(block_rows, width)  7.58 us
    all_gather x2, blocking collectives, gather_row(): return lax.all_gather(sent, 'row', axis=0, axis_index_groups=pairs)  5.9 us
    pallas_call x1, Pallas kernels, factor(): pl.pallas_call(factor_kernel, in_specs=[vmem], out_specs=[vmem] * 2, out_...  5.86 us
    ppermute x1, starting transfers between devices, on_device(): turned_image = lax.ppermute(image, BOTH, transposing)  5.24 us
  transfers between devices with their start and end apart: 8, of which 7 were waited for; matrix products, arithmetic and copies ran while one was open for 0% of the time, Pallas kernels for 7%

profile of v5, /device:TPU:1, one launch (start us, length us, event | category | flops | bytes accessed | tf_op | source)
XLA Modules:
  0.0 126.1 jit_solution(9355404983382242802)
XLA Ops:
  0.6 1.6 %broadcast_in_dim.6 = f32[16,64,128]{2,1,0:T(8,128)} broadcast(f32[64,128]{1,0:T(8,128)} %param.2), dimensions={1,2} | broadcast | bytes 557056 | tf_op jit(solution)/shard_map/broadcast_in_dim | solution.py:393
  2.2 7.6 %all-to-all-start = ((f32[16,64,128]{2,1,0:T(8,128)}), f32[16,64,128]{2,1,0:T(8,128)S(1)}, u32[]{:S(2)}, u32[]{:S(2)}) async-start(f32[16,64,128]{2,1,0:T(8,128)} %broadcast_in_dim.6), calls=%async_computation | async-start | bytes 1048576 | tf_op jit(solution)/shard_map/all_to_all | solution.py:407
  9.8 4.4 %collective-permute-start = (f32[64,128]{1,0:T(8,128)}, f32[64,128]{1,0:T(8,128)S(1)}, u32[]{:S(2)}, u32[]{:S(2)}) collective-permute-start(f32[64,128]{1,0:T(8,128)} %param.2), channel_id=1, source_target_pairs={{0,0},{1,16},{2,32},{3,48},{4,64},{5,80},{6,96},{7,112},{8,128},{9... | collective-permute-start | bytes 98312 | tf_op jit(solution)/shard_map/ppermute | solution.py:406
  14.2 2.8 %collective-permute-done = f32[64,128]{1,0:T(8,128)S(1)} collective-permute-done((f32[64,128]{1,0:T(8,128)}, f32[64,128]{1,0:T(8,128)S(1)}, u32[]{:S(2)}, u32[]{:S(2)}) %collective-permute-start) | collective-permute-done | bytes 32800 | tf_op jit(solution)/shard_map/ppermute | solution.py:406
  17.0 3.1 %all-to-all-done = f32[16,64,128]{2,1,0:T(8,128)S(1)} async-done(((f32[16,64,128]{2,1,0:T(8,128)}), f32[16,64,128]{2,1,0:T(8,128)S(1)}, u32[]{:S(2)}, u32[]{:S(2)}) %all-to-all-start) | async-done | bytes 524320 | tf_op jit(solution)/shard_map/all_to_all | solution.py:407
  20.1 0.0 copy-start
  20.1 0.7 gram_parts.1
  20.9 2.2 %collective-permute-start.1 = (f32[40,128]{1,0:T(8,128)S(1)}, f32[40,128]{1,0:T(8,128)S(1)}, u32[]{:S(2)}, u32[]{:S(2)}) collective-permute-start(f32[40,128]{1,0:T(8,128)S(1)} %get-tuple-element.25), channel_id=1, source_target_pairs={{0,16},{16,0},{32,48},{48,32},{64,80},{80,64},{96,112},{112,96},{1... | collective-permute-start | bytes 61448 | tf_op jit(solution)/shard_map/ppermute | solution.py:396
  23.1 0.8 collective-permute-done.1
  24.0 25.4 %all_to_all.25 = f32[8,112,128]{2,1,0:T(8,128)S(1)} all-to-all(f32[8,112,128]{2,1,0:T(8,128)S(1)} %broadcast_in_dim.7), channel_id=1, replica_groups={{0,32,64,96,128,160,192,224},{16,48,80,112,144,176,208,240},{1,33,65,97..., dimensions={0} | all-to-all | bytes 917504 | tf_op jit(solution)/shard_map/all_to_all | solution.py:398
  49.5 3.6 %all-gather = f32[1120,128]{1,0:T(8,128)S(1)} all-gather(f32[560,128]{1,0:T(8,128)S(1)} %pad_maximum_fusion), channel_id=2, replica_groups={{0,16},{32,48},{64,80},{96,112},{128,144},{160,176},{192,208},{224,240}..., dimensions={0}, use_global_device_ids=true | all-gather | bytes 860160 | tf_op jit(solution)/shard_map/all_gather | solution.py:404
  53.1 5.9 %factor.1 = (f32[128,128]{1,0:T(8,128)}, f32[128,128]{1,0:T(8,128)S(1)}) custom-call(f32[2,40,128]{2,1,0:T(8,128)S(1)} %slice.27.gram_ref), custom_call_target="tpu_custom_call" | custom-call | flops 400000000 | bytes 200000 | tf_op jit(solution)/shard_map/factor/pallas_call | solution.py:180
  58.9 0.0 copy-done
  58.9 2.4 %partial_sums.1 = f32[16,72,128]{2,1,0:T(8,128)} custom-call(f32[2,560,128]{2,1,0:T(8,128)S(1)} %bitcast.9, f32[128,128]{1,0:T(8,128)S(1)} %get-tuple-element.27.refs_1_.inverse_ref.refs_0_, f32[1024,1024]{1,0:T(8,128)S(1)} %copy-done), custom_call_target="tpu_custom_call" | custom-call | flops 805306368 | bytes 6000000 | tf_op jit(solution)/shard_map/partial_sums/pallas_call | solution.py:220
  61.3 4.7 %all-to-all-start.2 = ((f32[16,72,128]{2,1,0:T(8,128)}), f32[16,72,128]{2,1,0:T(8,128)S(1)}, u32[]{:S(2)}, u32[]{:S(2)}) async-start(f32[16,72,128]{2,1,0:T(8,128)} %partial_sums.1), calls=%async_computation.2 | async-start | bytes 1179648 | tf_op jit(solution)/shard_map/all_to_all | solution.py:417
  66.1 0.5 basis_rows.1.turned_ref.refs_2_
  66.6 10.4 %all-to-all-done.2.refs_0_ = f32[16,72,128]{2,1,0:T(8,128)S(1)} async-done(((f32[16,72,128]{2,1,0:T(8,128)}), f32[16,72,128]{2,1,0:T(8,128)S(1)}, u32[]{:S(2)}, u32[]{:S(2)}) %all-to-all-start.2) | async-done | bytes 589856 | tf_op jit(solution)/shard_map/all_to_all | solution.py:417
  77.0 0.9 image_piece.1
  77.8 3.9 %all-to-all-start.3 = ((f32[16,64,128]{2,1,0:T(8,128)}), f32[16,64,128]{2,1,0:T(8,128)S(1)}, u32[]{:S(2)}, u32[]{:S(2)}) async-start(f32[16,64,128]{2,1,0:T(8,128)} %get-tuple-element.29), calls=%async_computation.3 | async-start | bytes 1048576 | tf_op jit(solution)/shard_map/all_to_all | solution.py:425
  81.8 5.2 %collective-permute-start.2 = (f32[64,128]{1,0:T(8,128)S(1)}, f32[64,128]{1,0:T(8,128)S(1)}, u32[]{:S(2)}, u32[]{:S(2)}) collective-permute-start(f32[64,128]{1,0:T(8,128)S(1)} %get-tuple-element.30), channel_id=1, source_target_pairs={{0,0},{1,16},{2,32},{3,48},{4,64},{5,80},{6,96},{7,112},{8,128},{9... | collective-permute-start | bytes 98312 | tf_op jit(solution)/shard_map/ppermute | solution.py:424
  87.0 4.8 %collective-permute-done.2 = f32[64,128]{1,0:T(8,128)S(1)} collective-permute-done((f32[64,128]{1,0:T(8,128)S(1)}, f32[64,128]{1,0:T(8,128)S(1)}, u32[]{:S(2)}, u32[]{:S(2)}) %collective-permute-start.2) | collective-permute-done | bytes 32800 | tf_op jit(solution)/shard_map/ppermute | solution.py:424
  91.8 0.0 all-to-all-done.3
  91.8 0.7 inner_parts.1
  92.5 2.5 %collective-permute-start.3 = (f32[40,128]{1,0:T(8,128)S(1)}, f32[40,128]{1,0:T(8,128)S(1)}, u32[]{:S(2)}, u32[]{:S(2)}) collective-permute-start(f32[40,128]{1,0:T(8,128)S(1)} %get-tuple-element.35), channel_id=1, source_target_pairs={{0,16},{16,0},{32,48},{48,32},{64,80},{80,64},{96,112},{112,96},{1... | collective-permute-start | bytes 61448 | tf_op jit(solution)/shard_map/ppermute | solution.py:396
  95.0 0.8 collective-permute-done.3
  95.9 0.8 broadcast_in_dim.8
  96.7 4.9 %all-to-all-start.4 = ((f32[8,104,128]{2,1,0:T(8,128)}), f32[8,104,128]{2,1,0:T(8,128)}, u32[]{:S(2)}, u32[]{:S(2)}) async-start(f32[8,104,128]{2,1,0:T(8,128)} %broadcast_in_dim.8), calls=%async_computation.4 | async-start | bytes 851968 | tf_op jit(solution)/shard_map/all_to_all | solution.py:398
  101.6 3.1 %kernel.1 = (bf16[1024,384]{1,0:T(8,128)(2,1)S(1)}, bf16[1024,384]{1,0:T(8,128)(2,1)S(1)}, bf16[1024,384]{1,0:T(8,128)(2,1)S(1)}, f32[128,128]{1,0:T(8,128)S(1)}) custom-call(f32[128,128]{1,0:T(8,128)S(1)} %get-tuple-element.27.refs_1_.inverse_ref.refs_0_, f32[128,128]{1,0:T(8,128)S(1)} %get-tuple-element.36.refs_1_, ...), custom_call_target="tpu_custom_call" | custom-call | flops 300000000 | bytes 10000000 | tf_op jit(solution)/shard_map/kernel/pallas_call | solution.py:302
  104.8 4.7 %first_update.1.refs_3_ = f32[1024,1024]{1,0:T(8,128)} custom-call(f32[1024,128]{1,0:T(8,128)S(1)} %bitcast.12, f32[128,128]{1,0:T(8,128)S(1)} %get-tuple-element.39.kernel_ref, bf16[1024,384]{1,0:T(8,128)(2,1)S(1)} %get-tuple-element.40.cols_ref, f32[1024,1024]{1,0:T(8,128)} %mob_ref.1), custom_call_target="tpu_custom_call" | custom-call | flops 805306368 | bytes 9000000 | tf_op jit(solution)/shard_map/first_update/pallas_call | solution.py:350
  109.5 8.1 %all-to-all-done.4 = f32[8,104,128]{2,1,0:T(8,128)} async-done(((f32[8,104,128]{2,1,0:T(8,128)}), f32[8,104,128]{2,1,0:T(8,128)}, u32[]{:S(2)}, u32[]{:S(2)}) %all-to-all-start.4) | async-done | bytes 426016 | tf_op jit(solution)/shard_map/all_to_all | solution.py:398
  117.6 0.9 slice_reduce_fusion
  118.5 1.0 slice.28
  119.5 2.3 %all-gather.1 = f32[1104,128]{1,0:T(8,128)S(1)} all-gather(f32[552,128]{1,0:T(8,128)S(1)} %pad_maximum_fusion.1), channel_id=3, replica_groups={{0,16},{32,48},{64,80},{96,112},{128,144},{160,176},{192,208},{224,240}..., dimensions={0}, use_global_device_ids=true | all-gather | bytes 847872 | tf_op jit(solution)/shard_map/all_gather | solution.py:404
  121.8 4.1 %last_update.1 = f32[1024,1024]{1,0:T(8,128)} custom-call(f32[2,552,128]{2,1,0:T(8,128)S(1)} %bitcast.13, bf16[1024,384]{1,0:T(8,128)(2,1)S(1)} %get-tuple-element.37.refs_1_, bf16[1024,384]{1,0:T(8,128)(2,1)S(1)} %get-tuple-element.38.refs_2_, f32[1024,1024]{1,0:T(8,128)} %first_update.1.refs_3_), custom_call_target="tpu_custom_call" | custom-call | flops 805306368 | bytes 9000000 | tf_op jit(solution)/shard_map/last_update/pallas_call | solution.py:350
  (11 shorter events, 0.1 us)
Async XLA Ops:
  2.2 17.9 %all-to-all-start = ((f32[16,64,128]{2,1,0:T(8,128)}), f32[16,64,128]{2,1,0:T(8,128)S(1)}, u32[]{:S(2)}, u32[]{:S(2)}) async-start(f32[16,64,128]{2,1,0:T(8,128)} %broadcast_in_dim.6), calls=%async_computation | async-start | bytes 1048576 | tf_op jit(solution)/shard_map/all_to_all | solution.py:407
  9.8 7.2 %collective-permute-start = (f32[64,128]{1,0:T(8,128)}, f32[64,128]{1,0:T(8,128)S(1)}, u32[]{:S(2)}, u32[]{:S(2)}) collective-permute-start(f32[64,128]{1,0:T(8,128)} %param.2), channel_id=1, source_target_pairs={{0,0},{1,16},{2,32},{3,48},{4,64},{5,80},{6,96},{7,112},{8,128},{9... | collective-permute-start | bytes 98312 | tf_op jit(solution)/shard_map/ppermute | solution.py:406
  20.1 38.8 %copy-start = (f32[1024,1024]{1,0:T(8,128)S(1)}, f32[1024,1024]{1,0:T(8,128)}, u32[]{:S(2)}) copy-start(f32[1024,1024]{1,0:T(8,128)} %mob_ref.1) | copy-start | bytes 12582916
  20.9 3.1 %collective-permute-start.1 = (f32[40,128]{1,0:T(8,128)S(1)}, f32[40,128]{1,0:T(8,128)S(1)}, u32[]{:S(2)}, u32[]{:S(2)}) collective-permute-start(f32[40,128]{1,0:T(8,128)S(1)} %get-tuple-element.25), channel_id=1, source_target_pairs={{0,16},{16,0},{32,48},{48,32},{64,80},{80,64},{96,112},{112,96},{1... | collective-permute-start | bytes 61448 | tf_op jit(solution)/shard_map/ppermute | solution.py:396
  61.3 15.6 %all-to-all-start.2 = ((f32[16,72,128]{2,1,0:T(8,128)}), f32[16,72,128]{2,1,0:T(8,128)S(1)}, u32[]{:S(2)}, u32[]{:S(2)}) async-start(f32[16,72,128]{2,1,0:T(8,128)} %partial_sums.1), calls=%async_computation.2 | async-start | bytes 1179648 | tf_op jit(solution)/shard_map/all_to_all | solution.py:417
  77.8 14.0 %all-to-all-start.3 = ((f32[16,64,128]{2,1,0:T(8,128)}), f32[16,64,128]{2,1,0:T(8,128)S(1)}, u32[]{:S(2)}, u32[]{:S(2)}) async-start(f32[16,64,128]{2,1,0:T(8,128)} %get-tuple-element.29), calls=%async_computation.3 | async-start | bytes 1048576 | tf_op jit(solution)/shard_map/all_to_all | solution.py:425
  81.8 10.0 %collective-permute-start.2 = (f32[64,128]{1,0:T(8,128)S(1)}, f32[64,128]{1,0:T(8,128)S(1)}, u32[]{:S(2)}, u32[]{:S(2)}) collective-permute-start(f32[64,128]{1,0:T(8,128)S(1)} %get-tuple-element.30), channel_id=1, source_target_pairs={{0,0},{1,16},{2,32},{3,48},{4,64},{5,80},{6,96},{7,112},{8,128},{9... | collective-permute-start | bytes 98312 | tf_op jit(solution)/shard_map/ppermute | solution.py:424
  92.5 3.3 %collective-permute-start.3 = (f32[40,128]{1,0:T(8,128)S(1)}, f32[40,128]{1,0:T(8,128)S(1)}, u32[]{:S(2)}, u32[]{:S(2)}) collective-permute-start(f32[40,128]{1,0:T(8,128)S(1)} %get-tuple-element.35), channel_id=1, source_target_pairs={{0,16},{16,0},{32,48},{48,32},{64,80},{80,64},{96,112},{112,96},{1... | collective-permute-start | bytes 61448 | tf_op jit(solution)/shard_map/ppermute | solution.py:396
  96.7 20.9 %all-to-all-start.4 = ((f32[8,104,128]{2,1,0:T(8,128)}), f32[8,104,128]{2,1,0:T(8,128)}, u32[]{:S(2)}, u32[]{:S(2)}) async-start(f32[8,104,128]{2,1,0:T(8,128)} %broadcast_in_dim.8), calls=%async_computation.4 | async-start | bytes 851968 | tf_op jit(solution)/shard_map/all_to_all | solution.py:398

commit v6 on v5

--- a/solution.py
+++ b/solution.py
@@ -28,6 +28,10 @@
     return high, (value - high.astype(jnp.float32)).astype(jnp.bfloat16)
 
 
+def both_terms(value):
+    return jnp.concatenate(split(value), 1)
+
+
 def left_terms(value):
     high, low = split(value)
     return jnp.concatenate([high, low, high], 1)
@@ -38,6 +42,14 @@
     return jnp.concatenate([high, high, low], 1)
 
 
+def to_left(pair):
+    return jnp.concatenate([pair, pair[:, : pair.shape[1] // 2]], 1)
+
+
+def to_right(pair):
+    return jnp.concatenate([pair[:, : pair.shape[1] // 2], pair], 1)
+
+
 def exact_dot(first_op, second_op, dims):
     return lax.dot_general(first_op, second_op, dims, preferred_element_type=jnp.float32)
 
@@ -51,10 +63,9 @@
     return unit_rows(0, (width, width))
 
 
-def pieces_of(pairs_ref, n_z, piece):
-    return jnp.concatenate(
-        [pairs_ref[h, z * piece : (z + 1) * piece, :] for z in range(n_z) for h in range(2)], 0
-    )
+def pieces_of(parts_ref, piece):
+    count, _, width = parts_ref.shape
+    return parts_ref[:, :piece, :].reshape(count * piece, width)
 
 
 def pack(value, keep_ref, give_ref):
@@ -73,15 +84,20 @@
     give_ref[half:, :] = jnp.broadcast_to(last, (STEP, last.shape[1]))
 
 
-def unpack(packed):
-    half = packed.shape[1] - STEP
+def unpack(parts_ref, piece):
+    width = parts_ref.shape[2]
+    half = width // 4
+    stop = piece + half + STEP
+    sums = [parts_ref[h, piece:stop, :] for h in range(2)]
+    for i in range(2, parts_ref.shape[0]):
+        sums[i % 2] = sums[i % 2] + parts_ref[i, piece:stop, :]
     side = 2 * half
-    rows = packed[:, :half, :].reshape(side, packed.shape[2])
+    rows = jnp.concatenate([sums[0][:half], sums[1][:half]], 0)
     turned = rows.T
     row = lax.broadcasted_iota(jnp.int32, (side, side), 0)
     lane = lax.broadcasted_iota(jnp.int32, (side, side), 1)
     left, across = rows[:, :side], turned[:side]
-    last = packed[0, half : half + 1, :side]
+    last = sums[0][half : half + 1, :side]
     a = jnp.where(row >= lane, left, across)
     d = jnp.where(row == lane, last, jnp.where(row < lane, left, across))
     return jnp.concatenate(
@@ -123,11 +139,11 @@
     )(*operands)
 
 
-def factor_kernel(gram_ref, upper_ref, inverse_ref, work, other):
+def factor_kernel(piece, parts_ref, upper_ref, inverse_ref, work, other):
     width = upper_ref.shape[0]
     full = (STEP, width)
     lane = lax.broadcasted_iota(jnp.int32, full, 1)
-    work[...] = unpack(gram_ref[...])
+    work[...] = unpack(parts_ref, piece)
     other[...] = eye(width)
     for first in range(0, width, STEP):
         a_rows = [jnp.broadcast_to(work[first + k : first + k + 1, :], full) for k in range(STEP)]
@@ -173,12 +189,12 @@
             other[g : g + STEP, :] = x_new
 
 
-def factor(packed):
-    width = packed.shape[2]
+def factor(parts, piece):
+    width = parts.shape[2]
     shape = jax.ShapeDtypeStruct((width, width), jnp.float32)
     vmem = pl.BlockSpec(memory_space=pltpu.VMEM)
     return pl.pallas_call(
-        factor_kernel,
+        lambda *refs: factor_kernel(piece, *refs),
         in_specs=[vmem],
         out_specs=[vmem] * 2,
         out_shape=(shape, shape),
@@ -188,22 +204,22 @@
         ),
         compiler_params=pltpu.CompilerParams(vmem_limit_bytes=4 * MIB),
         name="factor",
-    )(packed)
-
-
-def partial_kernel(n_z, piece, share, pairs_ref, inverse_ref, mob_ref, out_ref, rhs):
-    width = pairs_ref.shape[2]
+    )(parts)
+
+
+def partial_kernel(piece, share, parts_ref, inverse_ref, mob_ref, out_ref, rhs):
+    width = parts_ref.shape[2]
     n_rows = mob_ref.shape[0]
     tile = 256
     cols = exact_dot(
-        left_terms(pieces_of(pairs_ref, n_z, piece)), right_terms(inverse_ref[...]), NT
+        left_terms(pieces_of(parts_ref, piece)), right_terms(inverse_ref[...]), NT
     )
     high, low = split(cols + unit_rows(lax.axis_index("col"), cols.shape))
     rhs[:, :width] = high
     rhs[:, width:] = low
-    last = pairs_ref.shape[1] - share
+    last = parts_ref.shape[1] - share
     out_ref[:, piece:, :] = jnp.broadcast_to(
-        pairs_ref[0, last:, :][None], (out_ref.shape[0], share, width)
+        parts_ref[0, last:, :][None], (out_ref.shape[0], share, width)
     )
     count = tile // piece
     for k in range(n_rows // tile):
@@ -213,12 +229,12 @@
         out_ref[k * count : (k + 1) * count, :piece, :] = found.reshape(count, piece, width)
 
 
-def partial_sums(pairs, inverse, mobility, n_z, piece, share):
+def partial_sums(parts, inverse, mobility, piece, share):
     n_rows, n_cols = mobility.shape
-    width = pairs.shape[2]
-    vmem = pl.BlockSpec(memory_space=pltpu.VMEM)
-    return pl.pallas_call(
-        lambda *refs: partial_kernel(n_z, piece, share, *refs),
+    width = parts.shape[2]
+    vmem = pl.BlockSpec(memory_space=pltpu.VMEM)
+    return pl.pallas_call(
+        lambda *refs: partial_kernel(piece, share, *refs),
         in_specs=[vmem] * 3,
         out_specs=vmem,
         out_shape=jax.ShapeDtypeStruct((n_rows // piece, piece + share, width), jnp.float32),
@@ -228,7 +244,7 @@
         ),
         compiler_params=pltpu.CompilerParams(vmem_limit_bytes=14 * MIB),
         name="partial_sums",
-    )(pairs, inverse, mobility)
+    )(parts, inverse, mobility)
 
 
 def image_kernel(piece, got_ref, image_ref, copies_ref, top_ref):
@@ -265,8 +281,8 @@
     turned_ref[...] = (rows + unit_rows(lax.axis_index("row"), rows.shape)).T
 
 
-def kernel_kernel(n_z, piece, inverse_ref, top_ref, turned_ref, pairs_ref, *outs):
-    cols_left, cols_right, rows_left, kernel_ref, state_ref = outs
+def kernel_kernel(piece, inverse_ref, top_ref, turned_ref, parts_ref, *outs):
+    cols_out, rows_left, kernel_ref, state_ref = outs
     width = inverse_ref.shape[0]
     identity = eye(width)
     ratio = -product(inverse_ref[...], top_ref[...], NT)
@@ -289,12 +305,11 @@
     kernel_ref[...] = kernel
     kernel_terms = right_terms(kernel)
     cols = exact_dot(
-        left_terms(pieces_of(pairs_ref, n_z, piece)), right_terms(inverse_ref[...]), NT
+        left_terms(pieces_of(parts_ref, piece)), right_terms(inverse_ref[...]), NT
     )
     cols = cols + unit_rows(lax.axis_index("col"), cols.shape)
-    cols_right[...] = right_terms(cols)
-    cols_left[...] = left_terms(exact_dot(left_terms(cols), kernel_terms, NT))
-    rows_left[...] = left_terms(exact_dot(left_terms(turned_ref[...].T), kernel_terms, NT))
+    cols_out[...] = both_terms(cols)
+    rows_left[...] = both_terms(exact_dot(left_terms(turned_ref[...].T), kernel_terms, NT))
 
 
 def side_call(kernel, operands, shapes, scratch, name):
@@ -313,79 +328,64 @@
     )(*operands)
 
 
-def stream(source_ref, out_ref, held, sems_in, sems_out, prepare, change):
-    parts = sems_in.shape[0]
-    tile = held.shape[0] // parts
+def update_kernel(piece, *refs):
+    parts_ref, image_ref, kernel_ref, cols_ref, rows_left, mob_ref = refs[:6]
+    out_ref, lhs, rhs, held, sems_in, sems_out = refs[6:]
+    count = sems_in.shape[0]
+    tile = held.shape[0] // count
     loads, stores = [], []
-    for k in range(parts):
+    for k in range(count):
         rows = pl.ds(k * tile, tile)
-        loads.append(pltpu.make_async_copy(source_ref.at[rows], held.at[rows], sems_in.at[k]))
+        loads.append(pltpu.make_async_copy(mob_ref.at[rows], held.at[rows], sems_in.at[k]))
         stores.append(pltpu.make_async_copy(held.at[rows], out_ref.at[rows], sems_out.at[k]))
         loads[k].start()
-    prepare()
-    for k in range(parts):
+    middle = lhs.shape[1] // 2
+    lhs[:, :middle] = left_terms(product(image_ref[...], kernel_ref[...]))
+    lhs[:, middle:] = to_left(rows_left[...])
+    small = right_terms(product(unpack(parts_ref, piece), kernel_ref[...]))
+    change = exact_dot(to_left(cols_ref[...]), small, NT)
+    rhs[:, :middle] = to_right(cols_ref[...])
+    rhs[:, middle:] = right_terms(pieces_of(parts_ref, piece) - change)
+    for k in range(count):
         loads[k].wait()
         rows = slice(k * tile, (k + 1) * tile)
-        held[rows, :] = change(held[rows, :], rows)
+        held[rows, :] = held[rows, :] - exact_dot(lhs[rows, :], rhs[...], NT)
         stores[k].start()
-    for k in range(parts):
+    for k in range(count):
         stores[k].wait()
 
 
-def first_update_kernel(image_ref, kernel_ref, cols_ref, mob_ref, out_ref, lhs, held, *sems):
-    def prepare():
-        lhs[...] = left_terms(product(image_ref[...], kernel_ref[...]))
-
-    def change(value, rows):
-        return value - exact_dot(lhs[rows, :], cols_ref[...], NT)
-
-    stream(mob_ref, out_ref, held, *sems, prepare, change)
-
-
-def update_call(kernel, inputs, matrix, terms, name):
-    n_rows, n_cols = matrix.shape
+def update(operands, mobility, piece):
+    n_rows, n_cols = mobility.shape
+    terms = 3 * operands[-1].shape[1]
     vmem = pl.BlockSpec(memory_space=pltpu.VMEM)
     hbm = pl.BlockSpec(memory_space=pltpu.HBM)
-    matrix = pltpu.with_memory_space_constraint(matrix, pltpu.HBM)
-    return pl.pallas_call(
-        kernel,
-        in_specs=[vmem] * len(inputs) + [hbm],
+    mobility = pltpu.with_memory_space_constraint(mobility, pltpu.HBM)
+    return pl.pallas_call(
+        lambda *refs: update_kernel(piece, *refs),
+        in_specs=[vmem] * len(operands) + [hbm],
         out_specs=hbm,
-        out_shape=pltpu.HBM(matrix.shape, jnp.float32),
+        out_shape=pltpu.HBM(mobility.shape, jnp.float32),
         scratch_shapes=[
             pltpu.VMEM((n_rows, terms), jnp.bfloat16),
-            pltpu.VMEM(matrix.shape, jnp.float32),
+            pltpu.VMEM((n_cols, terms), jnp.bfloat16),
+            pltpu.VMEM(mobility.shape, jnp.float32),
             pltpu.SemaphoreType.DMA((4,)),
             pltpu.SemaphoreType.DMA((4,)),
         ],
         cost_estimate=pl.CostEstimate(
             flops=2 * n_rows * n_cols * terms, bytes_accessed=9_000_000, transcendentals=0
         ),
-        compiler_params=pltpu.CompilerParams(vmem_limit_bytes=14 * MIB),
-        name=name,
-    )(*inputs, matrix)
-
-
-def last_update_kernel(n_z, piece, pairs_ref, cols_ref, turned_ref, half_ref, out_ref, rhs, held, *sems):
-    def prepare():
-        small = unpack(pairs_ref[:, n_z * piece :, :])
-        change_cols = exact_dot(cols_ref[...], right_terms(small), NT)
-        rhs[...] = right_terms(pieces_of(pairs_ref, n_z, piece) - change_cols)
-
-    def change(value, rows):
-        return value - exact_dot(turned_ref[rows, :], rhs[...], NT)
-
-    stream(half_ref, out_ref, held, *sems, prepare, change)
+        compiler_params=pltpu.CompilerParams(vmem_limit_bytes=20 * MIB),
+        name="update",
+    )(*operands, mobility)
 
 
 def on_device(panel, mobility):
     piece, width = panel.shape
     n_row, n_col = lax.axis_size("row"), lax.axis_size("col")
     block_rows, block_cols = mobility.shape
-    n_z = n_row // 2
     share = width // n_col
-    z_groups = [[2 * z + h for z in range(n_z)] for h in range(2)]
-    pairs = [[2 * z, 2 * z + 1] for z in range(n_z)]
     transposing = [(i * n_col + j, j * n_col + i) for i in range(n_row) for j in range(n_col)]
     swap = [(i, i ^ 1) for i in range(n_row)]
 
@@ -394,14 +394,8 @@
 
     def gather_row(lone, keep, give, extra):
         summed = keep + lax.ppermute(give, "row", swap)
-        sent = copies(jnp.concatenate([lone, summed] + extra, 0), n_z)
-        parts = lax.all_to_all(sent, "row", 0, 0, axis_index_groups=z_groups)
-        lone = parts[:, :piece].reshape(n_z * piece, width)
-        packed = summed.shape[0]
-        summed = jnp.sum(parts[:, piece : piece + packed], 0)
-        extra = [parts[0, piece + packed :]] if extra else []
         sent = jnp.concatenate([lone, summed] + extra, 0)
-        return lax.all_gather(sent, "row", axis=0, axis_index_groups=pairs)
+        return lax.all_gather(sent, "row", axis=0)
 
     turned_panel = lax.ppermute(panel, BOTH, transposing)
     panel_rows = lax.all_to_all(copies(panel, n_col), "col", 0, 0).reshape(block_rows, width)
@@ -409,13 +403,12 @@
     keep, give, top_part = packed_parts(
         gram_kernel, (panel_rows,), [(share, width)], "gram_parts"
     )
-    panel_pairs = gather_row(turned_panel, keep, give, [top_part])
-
-    start = n_z * piece
-    panel_factor, inverse = factor(panel_pairs[:, start : start + keep.shape[0]])
-    sent = partial_sums(panel_pairs, inverse, mobility, n_z, piece, share)
+    panel_parts = gather_row(turned_panel, keep, give, [top_part])
+
+    panel_factor, inverse = factor(panel_parts, piece)
+    sent = partial_sums(panel_parts, inverse, mobility, piece, share)
     got = lax.all_to_all(sent, "col", 0, 0)
-    wide = jax.ShapeDtypeStruct((block_rows, 3 * width), jnp.bfloat16)
+    wide = jax.ShapeDtypeStruct((block_rows, 2 * width), jnp.bfloat16)
     tall = jax.ShapeDtypeStruct((width, block_rows), jnp.float32)
     square = jax.ShapeDtypeStruct((width, width), jnp.float32)
     (turned_rows,) = side_call(rows_kernel, (panel_rows, inverse), [tall], [], "basis_rows")
@@ -423,27 +416,20 @@
     image, image_copies, top_rows = image_piece(got, piece)
     turned_image = lax.ppermute(image, BOTH, transposing)
     image_rows = lax.all_to_all(image_copies, "col", 0, 0).reshape(block_rows, width)
-    cols_left, cols_right, rows_left, kernel = side_call(
-        lambda *refs: kernel_kernel(n_z, piece, *refs),
-        (inverse, top_rows, turned_rows, panel_pairs),
-        [wide, wide, wide, square],
+    basis_cols, rows_left, kernel = side_call(
+        lambda *refs: kernel_kernel(piece, *refs),
+        (inverse, top_rows, turned_rows, panel_parts),
+        [wide, wide, square],
         [pltpu.VMEM((2 * width, width), jnp.float32)],
         "kernel",
     )
-    image_rows, turned_image = lax.optimization_barrier((image_rows, turned_image))
+    image_rows, turned_image, rows_left = lax.optimization_barrier(
+        (image_rows, turned_image, rows_left)
+    )
     keep, give = packed_parts(inner_kernel, (turned_rows, image_rows), [], "inner_parts")
-    image_pairs = gather_row(turned_image, keep, give, [])
-    terms = 3 * width
-    halfway = update_call(
-        first_update_kernel, (image_rows, kernel, cols_right), mobility, terms, "first_update"
-    )
-    updated = update_call(
-        lambda *refs: last_update_kernel(n_z, piece, *refs),
-        (image_pairs, cols_left, rows_left),
-        halfway,
-        terms,
-        "last_update",
-    )
+    image_parts = gather_row(turned_image, keep, give, [])
+    operands = (image_parts, image_rows, kernel, basis_cols, rows_left)
+    updated = update(operands, mobility, piece)
     return (updated, panel_factor)
 
 

time: 128 us -> 120 us (0.938)
  blocking collectives: 31.3 us -> 43.9 us
  waiting for transfers between devices: 30.9 us -> 20.1 us
  Pallas kernels: 23.1 us -> 18.8 us
  starting transfers between devices: 35.5 us -> 31.3 us
    all_gather x2, blocking collectives: 5.9 us -> 43.9 us  [gather_row(): return lax.all_gather(sent, 'row', axis=0)]
    all_to_all x1 -> x0, blocking collectives: 25.4 us -> none  [gather_row(): parts = lax.all_to_all(sent, 'row', 0, 0, axis_index_groups=z_groups)]
    all_to_all x1 -> x0, waiting for transfers between devices: 8.09 us -> none  [gather_row(): parts = lax.all_to_all(sent, 'row', 0, 0, axis_index_groups=z_groups)]
    all_to_all x1 -> x0, starting transfers between devices: 4.93 us -> none  [gather_row(): parts = lax.all_to_all(sent, 'row', 0, 0, axis_index_groups=z_groups)]
    pallas_call x4 -> x3, Pallas kernels: 17.1 us -> 13.2 us  [the longest x1 5.86 us: factor(): pl.pallas_call(lambda *refs: factor_kernel(piece, *refs), in_specs=[vmem]...]
    ppermute x1, waiting for transfers between devices: 4.78 us -> 2.23 us  [on_device(): turned_image = lax.ppermute(image, BOTH, transposing)]
    unnamed x2, local copies, waits for them, and re-layouts: 0.01 us -> 2.19 us
  transfers between devices with their start and end apart: 8 -> 7, of which waited for: 7 -> 6; matrix products, arithmetic and copies ran while one was open for 0% -> 0% of each run, Pallas kernels for 7% -> 3%
where the time goes in v6:
time: 120 us; the launch traced here: 119 us
  blocking collectives  43.9 us (37%)
  starting transfers between devices  31.3 us (26%)
  waiting for transfers between devices  20.1 us (17%)
  Pallas kernels  18.8 us (16%)
  local copies, waits for them, and re-layouts  3.79 us (3%)
    all_gather x2, blocking collectives, gather_row(): return lax.all_gather(sent, 'row', axis=0)  43.9 us
    all_to_all x1, waiting for transfers between devices, on_device(): got = lax.all_to_all(sent, 'col', 0, 0)  10.3 us
    all_to_all x1, starting transfers between devices, on_device(): lax.all_to_all(copies(panel, n_col), 'col', 0, 0).reshape(block_rows, width)  7.58 us
    pallas_call x1, Pallas kernels, factor(): pl.pallas_call(lambda *refs: factor_kernel(piece, *refs), in_specs=[vmem]...  5.86 us
    all_to_all x1, starting transfers between devices, on_device(): got = lax.all_to_all(sent, 'col', 0, 0)  5.26 us
    ppermute x1, starting transfers between devices, on_device(): turned_image = lax.ppermute(image, BOTH, transposing)  5.03 us
    pallas_call x1, Pallas kernels, update(): pl.pallas_call(lambda *refs: update_kernel(piece, *refs), in_specs=[vmem]...  4.94 us
    ppermute x2, starting transfers between devices, gather_row(): summed = keep + lax.ppermute(give, 'row', swap)  4.73 us
  transfers between devices with their start and end apart: 7, of which 6 were waited for; matrix products, arithmetic and copies ran while one was open for 0% of the time, Pallas kernels for 3%

profile of v6, /device:TPU:1, one launch (start us, length us, event | category | flops | bytes accessed | tf_op | source)
XLA Modules:
  0.0 118.8 jit_solution(11302743938481625552)
XLA Ops:
  0.6 1.6 %broadcast_in_dim.2 = f32[16,64,128]{2,1,0:T(8,128)} broadcast(f32[64,128]{1,0:T(8,128)} %param.2), dimensions={1,2} | broadcast | bytes 557056 | tf_op jit(solution)/shard_map/broadcast_in_dim | solution.py:393
  2.2 7.6 %all-to-all-start = ((f32[16,64,128]{2,1,0:T(8,128)}), f32[16,64,128]{2,1,0:T(8,128)S(1)}, u32[]{:S(2)}, u32[]{:S(2)}) async-start(f32[16,64,128]{2,1,0:T(8,128)} %broadcast_in_dim.2), calls=%async_computation | async-start | bytes 1048576 | tf_op jit(solution)/shard_map/all_to_all | solution.py:401
  9.8 4.4 %collective-permute-start = (f32[64,128]{1,0:T(8,128)}, f32[64,128]{1,0:T(8,128)S(1)}, u32[]{:S(2)}, u32[]{:S(2)}) collective-permute-start(f32[64,128]{1,0:T(8,128)} %param.2), channel_id=1, source_target_pairs={{0,0},{1,16},{2,32},{3,48},{4,64},{5,80},{6,96},{7,112},{8,128},{9... | collective-permute-start | bytes 98312 | tf_op jit(solution)/shard_map/ppermute | solution.py:400
  14.2 2.8 %collective-permute-done = f32[64,128]{1,0:T(8,128)S(1)} collective-permute-done((f32[64,128]{1,0:T(8,128)}, f32[64,128]{1,0:T(8,128)S(1)}, u32[]{:S(2)}, u32[]{:S(2)}) %collective-permute-start) | collective-permute-done | bytes 32800 | tf_op jit(solution)/shard_map/ppermute | solution.py:400
  17.0 3.1 %all-to-all-done = f32[16,64,128]{2,1,0:T(8,128)S(1)} async-done(((f32[16,64,128]{2,1,0:T(8,128)}), f32[16,64,128]{2,1,0:T(8,128)S(1)}, u32[]{:S(2)}, u32[]{:S(2)}) %all-to-all-start) | async-done | bytes 524320 | tf_op jit(solution)/shard_map/all_to_all | solution.py:401
  20.1 0.7 gram_parts.1
  20.8 2.2 %collective-permute-start.1 = (f32[40,128]{1,0:T(8,128)S(1)}, f32[40,128]{1,0:T(8,128)S(1)}, u32[]{:S(2)}, u32[]{:S(2)}) collective-permute-start(f32[40,128]{1,0:T(8,128)S(1)} %get-tuple-element.25), channel_id=1, source_target_pairs={{0,16},{16,0},{32,48},{48,32},{64,80},{80,64},{96,112},{112,96},{1... | collective-permute-start | bytes 61448 | tf_op jit(solution)/shard_map/ppermute | solution.py:396
  23.1 0.8 collective-permute-done.1
  23.9 24.0 %all-gather = f32[1792,128]{1,0:T(8,128)S(1)} all-gather(f32[112,128]{1,0:T(8,128)S(1)} %pad_maximum_fusion), channel_id=2, replica_groups=mesh['row'=16,'col'=16] {'row'}, dimensions={0}, use_global_device_ids=true | all-gather | bytes 974848 | tf_op jit(solution)/shard_map/all_gather | solution.py:398
  48.0 5.9 %factor.1 = (f32[128,128]{1,0:T(8,128)}, f32[128,128]{1,0:T(8,128)S(1)}) custom-call(f32[16,112,128]{2,1,0:T(8,128)S(1)} %bitcast.4), custom_call_target="tpu_custom_call" | custom-call | flops 400000000 | bytes 200000 | tf_op jit(solution)/shard_map/factor/pallas_call | solution.py:196
  53.8 0.0 copy-start
  53.8 2.2 %copy-done = f32[1024,1024]{1,0:T(8,128)S(1)} copy-done((f32[1024,1024]{1,0:T(8,128)S(1)}, f32[1024,1024]{1,0:T(8,128)}, u32[]{:S(2)}) %copy-start) | copy-done | bytes 4194328
  56.0 2.4 %partial_sums.1 = f32[16,72,128]{2,1,0:T(8,128)} custom-call(f32[16,112,128]{2,1,0:T(8,128)S(1)} %bitcast.5, f32[128,128]{1,0:T(8,128)S(1)} %get-tuple-element.27.refs_1_.inverse_ref.refs_0_, f32[1024,1024]{1,0:T(8,128)S(1)} %copy-done), custom_call_target="tpu_custom_call" | custom-call | flops 805306368 | bytes 6000000 | tf_op jit(solution)/shard_map/partial_sums/pallas_call | solution.py:236
  58.5 5.3 %all-to-all-start.1 = ((f32[16,72,128]{2,1,0:T(8,128)}), f32[16,72,128]{2,1,0:T(8,128)S(1)}, u32[]{:S(2)}, u32[]{:S(2)}) async-start(f32[16,72,128]{2,1,0:T(8,128)} %partial_sums.1), calls=%async_computation.1 | async-start | bytes 1179648 | tf_op jit(solution)/shard_map/all_to_all | solution.py:410
  63.7 0.5 basis_rows.1.refs_2_.turned_ref
  64.2 10.3 %all-to-all-done.1.refs_0_ = f32[16,72,128]{2,1,0:T(8,128)S(1)} async-done(((f32[16,72,128]{2,1,0:T(8,128)}), f32[16,72,128]{2,1,0:T(8,128)S(1)}, u32[]{:S(2)}, u32[]{:S(2)}) %all-to-all-start.1) | async-done | bytes 589856 | tf_op jit(solution)/shard_map/all_to_all | solution.py:410
  74.5 0.9 image_piece.1
  75.3 4.3 %all-to-all-start.2 = ((f32[16,64,128]{2,1,0:T(8,128)}), f32[16,64,128]{2,1,0:T(8,128)S(1)}, u32[]{:S(2)}, u32[]{:S(2)}) async-start(f32[16,64,128]{2,1,0:T(8,128)} %get-tuple-element.29), calls=%async_computation.2 | async-start | bytes 1048576 | tf_op jit(solution)/shard_map/all_to_all | solution.py:418
  79.6 5.0 %collective-permute-start.2 = (f32[64,128]{1,0:T(8,128)S(1)}, f32[64,128]{1,0:T(8,128)S(1)}, u32[]{:S(2)}, u32[]{:S(2)}) collective-permute-start(f32[64,128]{1,0:T(8,128)S(1)} %get-tuple-element.30), channel_id=1, source_target_pairs={{0,0},{1,16},{2,32},{3,48},{4,64},{5,80},{6,96},{7,112},{8,128},{9... | collective-permute-start | bytes 98312 | tf_op jit(solution)/shard_map/ppermute | solution.py:417
  84.7 2.8 %kernel.1 = (bf16[1024,256]{1,0:T(8,128)(2,1)S(1)}, bf16[1024,256]{1,0:T(8,128)(2,1)S(1)}, f32[128,128]{1,0:T(8,128)S(1)}) custom-call(f32[128,128]{1,0:T(8,128)S(1)} %get-tuple-element.27.refs_1_.inverse_ref.refs_0_, f32[128,128]{1,0:T(8,128)S(1)} %get-tuple-element.31.refs_1_, f32[128,1024]{1,0:T(8,128)S(1)} %basis_rows.1.refs_2_.turned_ref, ...), custom_call_target="tpu_custom_call" | custom-call | flops 300000000 | bytes 10000000 | tf_op jit(solution)/shard_map/kernel/pallas_call | solution.py:317
  87.4 2.2 %collective-permute-done.2 = f32[64,128]{1,0:T(8,128)S(1)} collective-permute-done((f32[64,128]{1,0:T(8,128)S(1)}, f32[64,128]{1,0:T(8,128)S(1)}, u32[]{:S(2)}, u32[]{:S(2)}) %collective-permute-start.2) | collective-permute-done | bytes 32800 | tf_op jit(solution)/shard_map/ppermute | solution.py:417
  89.7 0.0 all-to-all-done.2
  89.7 0.7 inner_parts.1
  90.4 2.5 %collective-permute-start.3 = (f32[40,128]{1,0:T(8,128)S(1)}, f32[40,128]{1,0:T(8,128)S(1)}, u32[]{:S(2)}, u32[]{:S(2)}) collective-permute-start(f32[40,128]{1,0:T(8,128)S(1)} %get-tuple-element.37), channel_id=1, source_target_pairs={{0,16},{16,0},{32,48},{48,32},{64,80},{80,64},{96,112},{112,96},{1... | collective-permute-start | bytes 61448 | tf_op jit(solution)/shard_map/ppermute | solution.py:396
  92.9 0.8 collective-permute-done.3
  93.8 19.9 %all-gather.1 = f32[1664,128]{1,0:T(8,128)S(1)} all-gather(f32[104,128]{1,0:T(8,128)S(1)} %pad_maximum_fusion.1), channel_id=3, replica_groups=mesh['row'=16,'col'=16] {'row'}, dimensions={0}, use_global_device_ids=true | all-gather | bytes 905216 | tf_op jit(solution)/shard_map/all_gather | solution.py:398
  113.6 4.9 %update.1 = f32[1024,1024]{1,0:T(8,128)} custom-call(f32[16,104,128]{2,1,0:T(8,128)S(1)} %bitcast.9, f32[1024,128]{1,0:T(8,128)S(1)} %bitcast.8, f32[128,128]{1,0:T(8,128)S(1)} %get-tuple-element.38.refs_2_, bf16[1024,256]{1,0:T(8,128)(2,1)S(1)} %get-tuple-element.39.refs_3_, bf16[1024,256]{1,0:T(8,128)(2,1)S(1)} %get-tuple-element.40.refs_4_, ...), custom_call_target="tpu_custom_call" | custom-call | flops 1610612736 | bytes 9000000 | tf_op jit(solution)/shard_map/update/pallas_call | solution.py:364
  (4 shorter events, 0.0 us)
Async XLA Ops:
  2.2 17.9 %all-to-all-start = ((f32[16,64,128]{2,1,0:T(8,128)}), f32[16,64,128]{2,1,0:T(8,128)S(1)}, u32[]{:S(2)}, u32[]{:S(2)}) async-start(f32[16,64,128]{2,1,0:T(8,128)} %broadcast_in_dim.2), calls=%async_computation | async-start | bytes 1048576 | tf_op jit(solution)/shard_map/all_to_all | solution.py:401
  9.8 7.2 %collective-permute-start = (f32[64,128]{1,0:T(8,128)}, f32[64,128]{1,0:T(8,128)S(1)}, u32[]{:S(2)}, u32[]{:S(2)}) collective-permute-start(f32[64,128]{1,0:T(8,128)} %param.2), channel_id=1, source_target_pairs={{0,0},{1,16},{2,32},{3,48},{4,64},{5,80},{6,96},{7,112},{8,128},{9... | collective-permute-start | bytes 98312 | tf_op jit(solution)/shard_map/ppermute | solution.py:400
  20.8 3.1 %collective-permute-start.1 = (f32[40,128]{1,0:T(8,128)S(1)}, f32[40,128]{1,0:T(8,128)S(1)}, u32[]{:S(2)}, u32[]{:S(2)}) collective-permute-start(f32[40,128]{1,0:T(8,128)S(1)} %get-tuple-element.25), channel_id=1, source_target_pairs={{0,16},{16,0},{32,48},{48,32},{64,80},{80,64},{96,112},{112,96},{1... | collective-permute-start | bytes 61448 | tf_op jit(solution)/shard_map/ppermute | solution.py:396
  53.8 2.2 %copy-start = (f32[1024,1024]{1,0:T(8,128)S(1)}, f32[1024,1024]{1,0:T(8,128)}, u32[]{:S(2)}) copy-start(f32[1024,1024]{1,0:T(8,128)} %refs_5_.1) | copy-start | bytes 12582916
  58.5 16.0 %all-to-all-start.1 = ((f32[16,72,128]{2,1,0:T(8,128)}), f32[16,72,128]{2,1,0:T(8,128)S(1)}, u32[]{:S(2)}, u32[]{:S(2)}) async-start(f32[16,72,128]{2,1,0:T(8,128)} %partial_sums.1), calls=%async_computation.1 | async-start | bytes 1179648 | tf_op jit(solution)/shard_map/all_to_all | solution.py:410
  75.3 14.3 %all-to-all-start.2 = ((f32[16,64,128]{2,1,0:T(8,128)}), f32[16,64,128]{2,1,0:T(8,128)S(1)}, u32[]{:S(2)}, u32[]{:S(2)}) async-start(f32[16,64,128]{2,1,0:T(8,128)} %get-tuple-element.29), calls=%async_computation.2 | async-start | bytes 1048576 | tf_op jit(solution)/shard_map/all_to_all | solution.py:418
  79.6 10.0 %collective-permute-start.2 = (f32[64,128]{1,0:T(8,128)S(1)}, f32[64,128]{1,0:T(8,128)S(1)}, u32[]{:S(2)}, u32[]{:S(2)}) collective-permute-start(f32[64,128]{1,0:T(8,128)S(1)} %get-tuple-element.30), channel_id=1, source_target_pairs={{0,0},{1,16},{2,32},{3,48},{4,64},{5,80},{6,96},{7,112},{8,128},{9... | collective-permute-start | bytes 98312 | tf_op jit(solution)/shard_map/ppermute | solution.py:417
  90.4 3.3 %collective-permute-start.3 = (f32[40,128]{1,0:T(8,128)S(1)}, f32[40,128]{1,0:T(8,128)S(1)}, u32[]{:S(2)}, u32[]{:S(2)}) collective-permute-start(f32[40,128]{1,0:T(8,128)S(1)} %get-tuple-element.37), channel_id=1, source_target_pairs={{0,16},{16,0},{32,48},{48,32},{64,80},{80,64},{96,112},{112,96},{1... | collective-permute-start | bytes 61448 | tf_op jit(solution)/shard_map/ppermute | solution.py:396

commit v7 on v6

--- a/solution.py
+++ b/solution.py
@@ -139,13 +139,14 @@
     )(*operands)
 
 
-def factor_kernel(piece, parts_ref, upper_ref, inverse_ref, work, other):
+def eliminate(gram, upper_ref, inverse_ref, work, other, beside):
     width = upper_ref.shape[0]
     full = (STEP, width)
     lane = lax.broadcasted_iota(jnp.int32, full, 1)
-    work[...] = unpack(parts_ref, piece)
+    work[...] = gram
     other[...] = eye(width)
     for first in range(0, width, STEP):
+        beside(first // STEP)
         a_rows = [jnp.broadcast_to(work[first + k : first + k + 1, :], full) for k in range(STEP)]
         x_rows = [jnp.broadcast_to(other[first + k : first + k + 1, :], full) for k in range(STEP)]
         entry, mult, inv = {}, {}, {}
@@ -189,62 +190,85 @@
             other[g : g + STEP, :] = x_new
 
 
-def factor(parts, piece):
-    width = parts.shape[2]
-    shape = jax.ShapeDtypeStruct((width, width), jnp.float32)
-    vmem = pl.BlockSpec(memory_space=pltpu.VMEM)
-    return pl.pallas_call(
-        lambda *refs: factor_kernel(piece, *refs),
-        in_specs=[vmem],
-        out_specs=[vmem] * 2,
-        out_shape=(shape, shape),
-        scratch_shapes=[pltpu.VMEM((width, width), jnp.float32)] * 2,
-        cost_estimate=pl.CostEstimate(
-            flops=400_000_000, bytes_accessed=200_000, transcendentals=0
-        ),
-        compiler_params=pltpu.CompilerParams(vmem_limit_bytes=4 * MIB),
-        name="factor",
-    )(parts)
-
-
-def partial_kernel(piece, share, parts_ref, inverse_ref, mob_ref, out_ref, rhs):
+def product_kernel(piece, share, parts_ref, mob_ref, upper_ref, inverse_ref, out_ref, *refs):
+    work, other, rhs, held, found, sems = refs
     width = parts_ref.shape[2]
-    n_rows = mob_ref.shape[0]
-    tile = 256
-    cols = exact_dot(
-        left_terms(pieces_of(parts_ref, piece)), right_terms(inverse_ref[...]), NT
-    )
-    high, low = split(cols + unit_rows(lax.axis_index("col"), cols.shape))
-    rhs[:, :width] = high
-    rhs[:, width:] = low
+    count = sems.shape[0]
+    tile = held.shape[0] // count
+    loads = []
+    for k in range(count):
+        rows = pl.ds(k * tile, tile)
+        loads.append(pltpu.make_async_copy(mob_ref.at[rows], held.at[rows], sems.at[k]))
+        loads[k].start()
+    rhs[...] = both_terms(pieces_of(parts_ref, piece))
     last = parts_ref.shape[1] - share
     out_ref[:, piece:, :] = jnp.broadcast_to(
         parts_ref[0, last:, :][None], (out_ref.shape[0], share, width)
     )
-    count = tile // piece
-    for k in range(n_rows // tile):
-        high, low = split(mob_ref[k * tile : (k + 1) * tile, :])
+
+    def beside(index):
+        k = index // 3 - 1
+        if index % 3 or not 0 <= k < count:
+            return
+        loads[k].wait()
+        rows = slice(k * tile, (k + 1) * tile)
+        high, low = split(held[rows, :])
         wide = exact_dot(high, rhs[...], NN)
-        found = wide[:, :width] + wide[:, width:] + exact_dot(low, rhs[:, :width], NN)
-        out_ref[k * count : (k + 1) * count, :piece, :] = found.reshape(count, piece, width)
-
-
-def partial_sums(parts, inverse, mobility, piece, share):
+        low_part = exact_dot(low, rhs[:, :width], NN)
+        found[rows, :] = wide[:, :width] + wide[:, width:] + low_part
+
+    eliminate(unpack(parts_ref, piece), upper_ref, inverse_ref, work, other, beside)
+    image = exact_dot(left_terms(found[...]), right_terms(inverse_ref[...]), NT)
+    image = image + jnp.where(lax.axis_index("col") == 0, held[:, :width], 0.0)
+    out_ref[:, :piece, :] = image.reshape(out_ref.shape[0], piece, width)
+
+
+def factor_and_product(parts, mobility, piece, share):
     n_rows, n_cols = mobility.shape
     width = parts.shape[2]
     vmem = pl.BlockSpec(memory_space=pltpu.VMEM)
-    return pl.pallas_call(
-        lambda *refs: partial_kernel(piece, share, *refs),
-        in_specs=[vmem] * 3,
-        out_specs=vmem,
-        out_shape=jax.ShapeDtypeStruct((n_rows // piece, piece + share, width), jnp.float32),
-        scratch_shapes=[pltpu.VMEM((n_cols, 2 * width), jnp.bfloat16)],
+    square = jax.ShapeDtypeStruct((width, width), jnp.float32)
+    mobility = pltpu.with_memory_space_constraint(mobility, pltpu.HBM)
+    return pl.pallas_call(
+        lambda *refs: product_kernel(piece, share, *refs),
+        in_specs=[vmem, pl.BlockSpec(memory_space=pltpu.HBM)],
+        out_specs=[vmem] * 3,
+        out_shape=(
+            square,
+            square,
+            jax.ShapeDtypeStruct((n_rows // piece, piece + share, width), jnp.float32),
+        ),
+        scratch_shapes=[
+            pltpu.VMEM((width, width), jnp.float32),
+            pltpu.VMEM((width, width), jnp.float32),
+            pltpu.VMEM((n_cols, 2 * width), jnp.bfloat16),
+            pltpu.VMEM(mobility.shape, jnp.float32),
+            pltpu.VMEM((n_rows, width), jnp.float32),
+            pltpu.SemaphoreType.DMA((4,)),
+        ],
         cost_estimate=pl.CostEstimate(
             flops=6 * n_rows * n_cols * width, bytes_accessed=6_000_000, transcendentals=0
         ),
-        compiler_params=pltpu.CompilerParams(vmem_limit_bytes=14 * MIB),
-        name="partial_sums",
-    )(parts, inverse, mobility)
+        compiler_params=pltpu.CompilerParams(vmem_limit_bytes=20 * MIB),
+        name="factor_and_product",
+    )(parts, mobility)
+
+
+def copy_kernel(rows_ref, out_ref):
+    out_ref[...] = jnp.broadcast_to(rows_ref[...][None], out_ref.shape)
+
+
+def copies(rows, count):
+    vmem = pl.BlockSpec(memory_space=pltpu.VMEM)
+    return pl.pallas_call(
+        copy_kernel,
+        in_specs=[vmem],
+        out_specs=vmem,
+        out_shape=jax.ShapeDtypeStruct((count,) + rows.shape, rows.dtype),
+        cost_estimate=pl.CostEstimate(flops=0, bytes_accessed=600_000, transcendentals=0),
+        compiler_params=pltpu.CompilerParams(vmem_limit_bytes=4 * MIB),
+        name="copies",
+    )(rows)
 
 
 def image_kernel(piece, got_ref, image_ref, copies_ref, top_ref):
@@ -282,7 +306,7 @@
 
 
 def kernel_kernel(piece, inverse_ref, top_ref, turned_ref, parts_ref, *outs):
-    cols_out, rows_left, kernel_ref, state_ref = outs
+    cols_out, rows_left, state_ref = outs
     width = inverse_ref.shape[0]
     identity = eye(width)
     ratio = -product(inverse_ref[...], top_ref[...], NT)
@@ -302,13 +326,12 @@
     lax.while_loop(go_on, double, (0, jnp.max(jnp.abs(ratio))))
     total = state_ref[width:, :]
     kernel = total + product(total, identity - product(identity - ratio, total))
-    kernel_ref[...] = kernel
     kernel_terms = right_terms(kernel)
     cols = exact_dot(
         left_terms(pieces_of(parts_ref, piece)), right_terms(inverse_ref[...]), NT
     )
     cols = cols + unit_rows(lax.axis_index("col"), cols.shape)
-    cols_out[...] = both_terms(cols)
+    cols_out[...] = both_terms(exact_dot(left_terms(cols), kernel_terms, NT))
     rows_left[...] = both_terms(exact_dot(left_terms(turned_ref[...].T), kernel_terms, NT))
 
 
@@ -329,8 +352,8 @@
 
 
 def update_kernel(piece, *refs):
-    parts_ref, image_ref, kernel_ref, cols_ref, rows_left, mob_ref = refs[:6]
-    out_ref, lhs, rhs, held, sems_in, sems_out = refs[6:]
+    parts_ref, image_ref, cols_ref, rows_left, mob_ref = refs[:5]
+    out_ref, lhs, rhs, held, sems_in, sems_out = refs[5:]
     count = sems_in.shape[0]
     tile = held.shape[0] // count
     loads, stores = [], []
@@ -340,9 +363,9 @@
         stores.append(pltpu.make_async_copy(held.at[rows], out_ref.at[rows], sems_out.at[k]))
         loads[k].start()
     middle = lhs.shape[1] // 2
-    lhs[:, :middle] = left_terms(product(image_ref[...], kernel_ref[...]))
+    lhs[:, :middle] = left_terms(image_ref[...])
     lhs[:, middle:] = to_left(rows_left[...])
-    small = right_terms(product(unpack(parts_ref, piece), kernel_ref[...]))
+    small = right_terms(unpack(parts_ref, piece))
     change = exact_dot(to_left(cols_ref[...]), small, NT)
     rhs[:, :middle] = to_right(cols_ref[...])
     rhs[:, middle:] = right_terms(pieces_of(parts_ref, piece) - change)
@@ -389,9 +412,6 @@
     transposing = [(i * n_col + j, j * n_col + i) for i in range(n_row) for j in range(n_col)]
     swap = [(i, i ^ 1) for i in range(n_row)]
 
-    def copies(rows, count):
-        return jnp.broadcast_to(rows[None], (count,) + rows.shape)
-
     def gather_row(lone, keep, give, extra):
         summed = keep + lax.ppermute(give, "row", swap)
         sent = jnp.concatenate([lone, summed] + extra, 0)
@@ -405,21 +425,19 @@
     )
     panel_parts = gather_row(turned_panel, keep, give, [top_part])
 
-    panel_factor, inverse = factor(panel_parts, piece)
-    sent = partial_sums(panel_parts, inverse, mobility, piece, share)
+    panel_factor, inverse, sent = factor_and_product(panel_parts, mobility, piece, share)
     got = lax.all_to_all(sent, "col", 0, 0)
     wide = jax.ShapeDtypeStruct((block_rows, 2 * width), jnp.bfloat16)
     tall = jax.ShapeDtypeStruct((width, block_rows), jnp.float32)
-    square = jax.ShapeDtypeStruct((width, width), jnp.float32)
     (turned_rows,) = side_call(rows_kernel, (panel_rows, inverse), [tall], [], "basis_rows")
     got, turned_rows = lax.optimization_barrier((got, turned_rows))
     image, image_copies, top_rows = image_piece(got, piece)
     turned_image = lax.ppermute(image, BOTH, transposing)
     image_rows = lax.all_to_all(image_copies, "col", 0, 0).reshape(block_rows, width)
-    basis_cols, rows_left, kernel = side_call(
+    cols_right, rows_left = side_call(
         lambda *refs: kernel_kernel(piece, *refs),
         (inverse, top_rows, turned_rows, panel_parts),
-        [wide, wide, square],
+        [wide, wide],
         [pltpu.VMEM((2 * width, width), jnp.float32)],
         "kernel",
     )
@@ -428,7 +446,7 @@
     )
     keep, give = packed_parts(inner_kernel, (turned_rows, image_rows), [], "inner_parts")
     image_parts = gather_row(turned_image, keep, give, [])
-    operands = (image_parts, image_rows, kernel, basis_cols, rows_left)
+    operands = (image_parts, image_rows, cols_right, rows_left)
     updated = update(operands, mobility, piece)
     return (updated, panel_factor)
 

time: 120 us -> 115 us (0.958)
  local copies, waits for them, and re-layouts: 3.79 us -> 0.75 us
    broadcast_in_dim x1 -> x0, local copies, waits for them, and re-layouts: 1.6 us -> none  [copies(): return jnp.broadcast_to(rows[None], (count,) + rows.shape)]
    unnamed x2, local copies, waits for them, and re-layouts: 2.19 us -> 0.75 us
where the time goes in v7:
time: 115 us
  blocking collectives  43.8 us (38%)
  starting transfers between devices  31.3 us (27%)
  waiting for transfers between devices  20.3 us (18%)
  Pallas kernels  17.8 us (15%)
    all_gather x2, blocking collectives, gather_row(): return lax.all_gather(sent, 'row', axis=0)  43.8 us
    all_to_all x1, waiting for transfers between devices, on_device(): got = lax.all_to_all(sent, 'col', 0, 0)  10.3 us
    all_to_all x1, starting transfers between devices, on_device(): lax.all_to_all(copies(panel, n_col), 'col', 0, 0).reshape(block_rows, width)  7.58 us
    pallas_call x1, Pallas kernels, factor_and_product(): pl.pallas_call(lambda *refs: product_kernel(piece, share, *refs), in_spec...  6.88 us
    all_to_all x1, starting transfers between devices, on_device(): got = lax.all_to_all(sent, 'col', 0, 0)  5.26 us
    ppermute x1, starting transfers between devices, on_device(): turned_image = lax.ppermute(image, BOTH, transposing)  5.03 us
    ppermute x2, starting transfers between devices, gather_row(): summed = keep + lax.ppermute(give, 'row', swap)  4.72 us
    pallas_call x1, Pallas kernels, update(): pl.pallas_call(lambda *refs: update_kernel(piece, *refs), in_specs=[vmem]...  4.69 us
  transfers between devices with their start and end apart: 7, of which 6 were waited for; matrix products, arithmetic and copies ran while one was open for 0% of the time, Pallas kernels for 3%

profile of v7, /device:TPU:1, one launch (start us, length us, event | category | flops | bytes accessed | tf_op | source)
XLA Modules:
  0.0 114.6 jit_solution(4107245813633539933)
XLA Ops:
  0.6 0.0 copy-start
  0.6 0.7 copy-done
  1.4 0.8 copies.1
  2.2 7.6 %all-to-all-start = ((f32[16,64,128]{2,1,0:T(8,128)}), f32[16,64,128]{2,1,0:T(8,128)S(1)}, u32[]{:S(2)}, u32[]{:S(2)}) async-start(f32[16,64,128]{2,1,0:T(8,128)} %copies.1), calls=%async_computation | async-start | bytes 1048576 | tf_op jit(solution)/shard_map/all_to_all | solution.py:421
  9.8 4.4 %collective-permute-start = (f32[64,128]{1,0:T(8,128)}, f32[64,128]{1,0:T(8,128)S(1)}, u32[]{:S(2)}, u32[]{:S(2)}) collective-permute-start(f32[64,128]{1,0:T(8,128)} %rows_ref.1), channel_id=1, source_target_pairs={{0,0},{1,16},{2,32},{3,48},{4,64},{5,80},{6,96},{7,112},{8,128},{9... | collective-permute-start | bytes 98312 | tf_op jit(solution)/shard_map/ppermute | solution.py:420
  14.2 2.8 %collective-permute-done = f32[64,128]{1,0:T(8,128)S(1)} collective-permute-done((f32[64,128]{1,0:T(8,128)}, f32[64,128]{1,0:T(8,128)S(1)}, u32[]{:S(2)}, u32[]{:S(2)}) %collective-permute-start) | collective-permute-done | bytes 32800 | tf_op jit(solution)/shard_map/ppermute | solution.py:420
  17.0 3.1 %all-to-all-done = f32[16,64,128]{2,1,0:T(8,128)S(1)} async-done(((f32[16,64,128]{2,1,0:T(8,128)}), f32[16,64,128]{2,1,0:T(8,128)S(1)}, u32[]{:S(2)}, u32[]{:S(2)}) %all-to-all-start) | async-done | bytes 524320 | tf_op jit(solution)/shard_map/all_to_all | solution.py:421
  20.1 0.7 gram_parts.1
  20.9 2.2 %collective-permute-start.1 = (f32[40,128]{1,0:T(8,128)S(1)}, f32[40,128]{1,0:T(8,128)S(1)}, u32[]{:S(2)}, u32[]{:S(2)}) collective-permute-start(f32[40,128]{1,0:T(8,128)S(1)} %get-tuple-element.25), channel_id=1, source_target_pairs={{0,16},{16,0},{32,48},{48,32},{64,80},{80,64},{96,112},{112,96},{1... | collective-permute-start | bytes 61448 | tf_op jit(solution)/shard_map/ppermute | solution.py:416
  23.1 0.8 collective-permute-done.1
  23.9 24.0 %all-gather = f32[1792,128]{1,0:T(8,128)S(1)} all-gather(f32[112,128]{1,0:T(8,128)S(1)} %pad_maximum_fusion), channel_id=2, replica_groups=mesh['row'=16,'col'=16] {'row'}, dimensions={0}, use_global_device_ids=true | all-gather | bytes 974848 | tf_op jit(solution)/shard_map/all_gather | solution.py:418
  48.0 6.9 %factor_and_product.1 = (f32[128,128]{1,0:T(8,128)}, f32[128,128]{1,0:T(8,128)S(1)}, f32[16,72,128]{2,1,0:T(8,128)}) custom-call(f32[16,112,128]{2,1,0:T(8,128)S(1)} %bitcast.4, f32[1024,1024]{1,0:T(8,128)} %refs_4_.1), custom_call_target="tpu_custom_call" | custom-call | flops 805306368 | bytes 6000000 | tf_op jit(solution)/shard_map/factor_and_product/pallas_call | solution.py:232
  54.9 5.3 %all-to-all-start.1 = ((f32[16,72,128]{2,1,0:T(8,128)}), f32[16,72,128]{2,1,0:T(8,128)S(1)}, u32[]{:S(2)}, u32[]{:S(2)}) async-start(f32[16,72,128]{2,1,0:T(8,128)} %get-tuple-element.27), calls=%async_computation.1 | async-start | bytes 1179648 | tf_op jit(solution)/shard_map/all_to_all | solution.py:429
  60.1 0.5 basis_rows.1.refs_2_.turned_ref
  60.6 10.3 %all-to-all-done.1.refs_0_ = f32[16,72,128]{2,1,0:T(8,128)S(1)} async-done(((f32[16,72,128]{2,1,0:T(8,128)}), f32[16,72,128]{2,1,0:T(8,128)S(1)}, u32[]{:S(2)}, u32[]{:S(2)}) %all-to-all-start.1) | async-done | bytes 589856 | tf_op jit(solution)/shard_map/all_to_all | solution.py:429
  70.9 0.9 image_piece.1
  71.8 4.3 %all-to-all-start.2 = ((f32[16,64,128]{2,1,0:T(8,128)}), f32[16,64,128]{2,1,0:T(8,128)S(1)}, u32[]{:S(2)}, u32[]{:S(2)}) async-start(f32[16,64,128]{2,1,0:T(8,128)} %get-tuple-element.30), calls=%async_computation.2 | async-start | bytes 1048576 | tf_op jit(solution)/shard_map/all_to_all | solution.py:436
  76.0 5.0 %collective-permute-start.2 = (f32[64,128]{1,0:T(8,128)S(1)}, f32[64,128]{1,0:T(8,128)S(1)}, u32[]{:S(2)}, u32[]{:S(2)}) collective-permute-start(f32[64,128]{1,0:T(8,128)S(1)} %get-tuple-element.31), channel_id=1, source_target_pairs={{0,0},{1,16},{2,32},{3,48},{4,64},{5,80},{6,96},{7,112},{8,128},{9... | collective-permute-start | bytes 98312 | tf_op jit(solution)/shard_map/ppermute | solution.py:435
  81.1 2.6 %kernel.1 = (bf16[1024,256]{1,0:T(8,128)(2,1)S(1)}, bf16[1024,256]{1,0:T(8,128)(2,1)S(1)}) custom-call(f32[128,128]{1,0:T(8,128)S(1)} %get-tuple-element.28.inverse_ref.refs_0_, f32[128,128]{1,0:T(8,128)S(1)} %get-tuple-element.32.refs_1_, f32[128,1024]{1,0:T(8,128)S(1)} %basis_rows.1.refs_2_.turned_ref, f32[16,112,128]{2,1,0:T(8,128)S(1)} %bitcast.5), custom_call_target="tpu_custom_call" | custom-call | flops 300000000 | bytes 10000000 | tf_op jit(solution)/shard_map/kernel/pallas_call | solution.py:340
  83.7 2.4 %collective-permute-done.2 = f32[64,128]{1,0:T(8,128)S(1)} collective-permute-done((f32[64,128]{1,0:T(8,128)S(1)}, f32[64,128]{1,0:T(8,128)S(1)}, u32[]{:S(2)}, u32[]{:S(2)}) %collective-permute-start.2) | collective-permute-done | bytes 32800 | tf_op jit(solution)/shard_map/ppermute | solution.py:435
  86.1 0.0 all-to-all-done.2
  86.1 0.7 inner_parts.1
  86.8 2.5 %collective-permute-start.3 = (f32[40,128]{1,0:T(8,128)S(1)}, f32[40,128]{1,0:T(8,128)S(1)}, u32[]{:S(2)}, u32[]{:S(2)}) collective-permute-start(f32[40,128]{1,0:T(8,128)S(1)} %get-tuple-element.38), channel_id=1, source_target_pairs={{0,16},{16,0},{32,48},{48,32},{64,80},{80,64},{96,112},{112,96},{1... | collective-permute-start | bytes 61448 | tf_op jit(solution)/shard_map/ppermute | solution.py:416
  89.3 0.8 collective-permute-done.3
  90.2 19.7 %all-gather.1 = f32[1664,128]{1,0:T(8,128)S(1)} all-gather(f32[104,128]{1,0:T(8,128)S(1)} %pad_maximum_fusion.1), channel_id=3, replica_groups=mesh['row'=16,'col'=16] {'row'}, dimensions={0}, use_global_device_ids=true | all-gather | bytes 905216 | tf_op jit(solution)/shard_map/all_gather | solution.py:418
  109.9 4.7 %update.1 = f32[1024,1024]{1,0:T(8,128)} custom-call(f32[16,104,128]{2,1,0:T(8,128)S(1)} %bitcast.8, f32[1024,128]{1,0:T(8,128)S(1)} %bitcast.7, bf16[1024,256]{1,0:T(8,128)(2,1)S(1)} %get-tuple-element.39.refs_2_, bf16[1024,256]{1,0:T(8,128)(2,1)S(1)} %get-tuple-element.40.refs_3_, f32[1024,1024]{1,0:T(8,128)} %refs_4_.1), custom_call_target="tpu_custom_call" | custom-call | flops 1610612736 | bytes 9000000 | tf_op jit(solution)/shard_map/update/pallas_call | solution.py:387
  (4 shorter events, 0.0 us)
Async XLA Ops:
  0.6 0.8 copy-start
  2.2 17.9 %all-to-all-start = ((f32[16,64,128]{2,1,0:T(8,128)}), f32[16,64,128]{2,1,0:T(8,128)S(1)}, u32[]{:S(2)}, u32[]{:S(2)}) async-start(f32[16,64,128]{2,1,0:T(8,128)} %copies.1), calls=%async_computation | async-start | bytes 1048576 | tf_op jit(solution)/shard_map/all_to_all | solution.py:421
  9.8 7.2 %collective-permute-start = (f32[64,128]{1,0:T(8,128)}, f32[64,128]{1,0:T(8,128)S(1)}, u32[]{:S(2)}, u32[]{:S(2)}) collective-permute-start(f32[64,128]{1,0:T(8,128)} %rows_ref.1), channel_id=1, source_target_pairs={{0,0},{1,16},{2,32},{3,48},{4,64},{5,80},{6,96},{7,112},{8,128},{9... | collective-permute-start | bytes 98312 | tf_op jit(solution)/shard_map/ppermute | solution.py:420
  20.9 3.1 %collective-permute-start.1 = (f32[40,128]{1,0:T(8,128)S(1)}, f32[40,128]{1,0:T(8,128)S(1)}, u32[]{:S(2)}, u32[]{:S(2)}) collective-permute-start(f32[40,128]{1,0:T(8,128)S(1)} %get-tuple-element.25), channel_id=1, source_target_pairs={{0,16},{16,0},{32,48},{48,32},{64,80},{80,64},{96,112},{112,96},{1... | collective-permute-start | bytes 61448 | tf_op jit(solution)/shard_map/ppermute | solution.py:416
  54.9 16.0 %all-to-all-start.1 = ((f32[16,72,128]{2,1,0:T(8,128)}), f32[16,72,128]{2,1,0:T(8,128)S(1)}, u32[]{:S(2)}, u32[]{:S(2)}) async-start(f32[16,72,128]{2,1,0:T(8,128)} %get-tuple-element.27), calls=%async_computation.1 | async-start | bytes 1179648 | tf_op jit(solution)/shard_map/all_to_all | solution.py:429
  71.8 14.3 %all-to-all-start.2 = ((f32[16,64,128]{2,1,0:T(8,128)}), f32[16,64,128]{2,1,0:T(8,128)S(1)}, u32[]{:S(2)}, u32[]{:S(2)}) async-start(f32[16,64,128]{2,1,0:T(8,128)} %get-tuple-element.30), calls=%async_computation.2 | async-start | bytes 1048576 | tf_op jit(solution)/shard_map/all_to_all | solution.py:436
  76.0 10.0 %collective-permute-start.2 = (f32[64,128]{1,0:T(8,128)S(1)}, f32[64,128]{1,0:T(8,128)S(1)}, u32[]{:S(2)}, u32[]{:S(2)}) collective-permute-start(f32[64,128]{1,0:T(8,128)S(1)} %get-tuple-element.31), channel_id=1, source_target_pairs={{0,0},{1,16},{2,32},{3,48},{4,64},{5,80},{6,96},{7,112},{8,128},{9... | collective-permute-start | bytes 98312 | tf_op jit(solution)/shard_map/ppermute | solution.py:435
  86.8 3.3 %collective-permute-start.3 = (f32[40,128]{1,0:T(8,128)S(1)}, f32[40,128]{1,0:T(8,128)S(1)}, u32[]{:S(2)}, u32[]{:S(2)}) collective-permute-start(f32[40,128]{1,0:T(8,128)S(1)} %get-tuple-element.38), channel_id=1, source_target_pairs={{0,16},{16,0},{32,48},{48,32},{64,80},{80,64},{96,112},{112,96},{1... | collective-permute-start | bytes 61448 | tf_op jit(solution)/shard_map/ppermute | solution.py:416

commit v8 on v7

--- a/solution.py
+++ b/solution.py
@@ -254,21 +254,48 @@
     )(parts, mobility)
 
 
-def copy_kernel(rows_ref, out_ref):
-    out_ref[...] = jnp.broadcast_to(rows_ref[...][None], out_ref.shape)
+def copy_kernel(rows_ref, out_ref, sems):
+    sends = []
+    for k in range(out_ref.shape[0]):
+        sends.append(pltpu.make_async_copy(rows_ref, out_ref.at[k], sems.at[k]))
+        sends[k].start()
+    for send in sends:
+        send.wait()
 
 
 def copies(rows, count):
-    vmem = pl.BlockSpec(memory_space=pltpu.VMEM)
+    hbm = pl.BlockSpec(memory_space=pltpu.HBM)
+    shape = (count,) + rows.shape
     return pl.pallas_call(
         copy_kernel,
-        in_specs=[vmem],
-        out_specs=vmem,
-        out_shape=jax.ShapeDtypeStruct((count,) + rows.shape, rows.dtype),
+        in_specs=[hbm],
+        out_specs=hbm,
+        out_shape=pltpu.HBM(shape, rows.dtype),
+        scratch_shapes=[pltpu.SemaphoreType.DMA((count,))],
         cost_estimate=pl.CostEstimate(flops=0, bytes_accessed=600_000, transcendentals=0),
         compiler_params=pltpu.CompilerParams(vmem_limit_bytes=4 * MIB),
         name="copies",
-    )(rows)
+    )(pltpu.with_memory_space_constraint(rows, pltpu.HBM))
+
+
+def join_kernel(lone_ref, keep_ref, came_ref, mob_ref, out_ref):
+    piece = lone_ref.shape[0]
+    out_ref[:piece, :] = lone_ref[...]
+    out_ref[piece:, :] = keep_ref[...] + came_ref[...]
+
+
+def join(lone, keep, came, mobility):
+    vmem = pl.BlockSpec(memory_space=pltpu.VMEM)
+    shape = (lone.shape[0] + keep.shape[0], lone.shape[1])
+    return pl.pallas_call(
+        join_kernel,
+        in_specs=[vmem] * 3 + [pl.BlockSpec(memory_space=pltpu.HBM)],
+        out_specs=vmem,
+        out_shape=jax.ShapeDtypeStruct(shape, jnp.float32),
+        cost_estimate=pl.CostEstimate(flops=0, bytes_accessed=100_000, transcendentals=0),
+        compiler_params=pltpu.CompilerParams(vmem_limit_bytes=4 * MIB),
+        name="join",
+    )(lone, keep, came, pltpu.with_memory_space_constraint(mobility, pltpu.HBM))
 
 
 def image_kernel(piece, got_ref, image_ref, copies_ref, top_ref):
@@ -353,26 +380,21 @@
 
 def update_kernel(piece, *refs):
     parts_ref, image_ref, cols_ref, rows_left, mob_ref = refs[:5]
-    out_ref, lhs, rhs, held, sems_in, sems_out = refs[5:]
-    count = sems_in.shape[0]
+    out_ref, lhs, rhs, held, sems = refs[5:]
+    count = sems.shape[0]
     tile = held.shape[0] // count
-    loads, stores = [], []
-    for k in range(count):
-        rows = pl.ds(k * tile, tile)
-        loads.append(pltpu.make_async_copy(mob_ref.at[rows], held.at[rows], sems_in.at[k]))
-        stores.append(pltpu.make_async_copy(held.at[rows], out_ref.at[rows], sems_out.at[k]))
-        loads[k].start()
     middle = lhs.shape[1] // 2
     lhs[:, :middle] = left_terms(image_ref[...])
     lhs[:, middle:] = to_left(rows_left[...])
     small = right_terms(unpack(parts_ref, piece))
     change = exact_dot(to_left(cols_ref[...]), small, NT)
-    rhs[:, :middle] = to_right(cols_ref[...])
-    rhs[:, middle:] = right_terms(pieces_of(parts_ref, piece) - change)
+    rhs[:middle, :] = to_right(cols_ref[...]).T
+    rhs[middle:, :] = right_terms(pieces_of(parts_ref, piece) - change).T
+    stores = []
     for k in range(count):
-        loads[k].wait()
-        rows = slice(k * tile, (k + 1) * tile)
-        held[rows, :] = held[rows, :] - exact_dot(lhs[rows, :], rhs[...], NT)
+        rows = pl.ds(k * tile, tile)
+        held[rows, :] = mob_ref[rows, :] - exact_dot(lhs[rows, :], rhs[...], NN)
+        stores.append(pltpu.make_async_copy(held.at[rows], out_ref.at[rows], sems.at[k]))
         stores[k].start()
     for k in range(count):
         stores[k].wait()
@@ -383,17 +405,15 @@
     terms = 3 * operands[-1].shape[1]
     vmem = pl.BlockSpec(memory_space=pltpu.VMEM)
     hbm = pl.BlockSpec(memory_space=pltpu.HBM)
-    mobility = pltpu.with_memory_space_constraint(mobility, pltpu.HBM)
     return pl.pallas_call(
         lambda *refs: update_kernel(piece, *refs),
-        in_specs=[vmem] * len(operands) + [hbm],
+        in_specs=[vmem] * (len(operands) + 1),
         out_specs=hbm,
         out_shape=pltpu.HBM(mobility.shape, jnp.float32),
         scratch_shapes=[
             pltpu.VMEM((n_rows, terms), jnp.bfloat16),
-            pltpu.VMEM((n_cols, terms), jnp.bfloat16),
+            pltpu.VMEM((terms, n_cols), jnp.bfloat16),
             pltpu.VMEM(mobility.shape, jnp.float32),
-            pltpu.SemaphoreType.DMA((4,)),
             pltpu.SemaphoreType.DMA((4,)),
         ],
         cost_estimate=pl.CostEstimate(
@@ -412,18 +432,14 @@
     transposing = [(i * n_col + j, j * n_col + i) for i in range(n_row) for j in range(n_col)]
     swap = [(i, i ^ 1) for i in range(n_row)]
 
-    def gather_row(lone, keep, give, extra):
-        summed = keep + lax.ppermute(give, "row", swap)
-        sent = jnp.concatenate([lone, summed] + extra, 0)
-        return lax.all_gather(sent, "row", axis=0)
-
     turned_panel = lax.ppermute(panel, BOTH, transposing)
     panel_rows = lax.all_to_all(copies(panel, n_col), "col", 0, 0).reshape(block_rows, width)
     panel_rows, turned_panel = lax.optimization_barrier((panel_rows, turned_panel))
     keep, give, top_part = packed_parts(
         gram_kernel, (panel_rows,), [(share, width)], "gram_parts"
     )
-    panel_parts = gather_row(turned_panel, keep, give, [top_part])
+    packed = keep + lax.ppermute(give, "row", swap)
+    panel_parts = lax.all_gather(jnp.concatenate([turned_panel, packed, top_part], 0), "row", axis=0)
 
     panel_factor, inverse, sent = factor_and_product(panel_parts, mobility, piece, share)
     got = lax.all_to_all(sent, "col", 0, 0)
@@ -445,7 +461,8 @@
         (image_rows, turned_image, rows_left)
     )
     keep, give = packed_parts(inner_kernel, (turned_rows, image_rows), [], "inner_parts")
-    image_parts = gather_row(turned_image, keep, give, [])
+    came = lax.ppermute(give, "row", swap)
+    image_parts = lax.all_gather(join(turned_image, keep, came, mobility), "row", axis=0)
     operands = (image_parts, image_rows, cols_right, rows_left)
     updated = update(operands, mobility, piece)
     return (updated, panel_factor)

time: 115 us -> 129 us (1.12)
  Pallas kernels: 17.8 us -> 33 us
    pallas_call x1 -> x2, Pallas kernels: 0.84 us -> 17.1 us  [the longest x1 17.1 us: copies(): pl.pallas_call(copy_kernel, in_specs=[hbm], out_specs=hbm, out_shape=pltp...]
    pallas_call x1, Pallas kernels: 4.69 us -> 3.21 us  [update(): pl.pallas_call(lambda *refs: update_kernel(piece, *refs), in_specs=[vmem]...]
where the time goes in v8:
time: 129 us
  blocking collectives  43.7 us (34%)
  Pallas kernels  33 us (26%)
  starting transfers between devices  31.3 us (24%)
  waiting for transfers between devices  19.9 us (15%)
    all_gather x1, blocking collectives, on_device(): lax.all_gather(jnp.concatenate([turned_panel, packed, top_part], 0), 'row...  24 us
    all_gather x1, blocking collectives, on_device(): lax.all_gather(join(turned_image, keep, came, mobility), 'row', axis=0)  19.7 us
    pallas_call x1, Pallas kernels, copies(): pl.pallas_call(copy_kernel, in_specs=[hbm], out_specs=hbm, out_shape=pltp...  17.1 us
    all_to_all x1, waiting for transfers between devices, on_device(): got = lax.all_to_all(sent, 'col', 0, 0)  10.3 us
    all_to_all x1, starting transfers between devices, on_device(): lax.all_to_all(copies(panel, n_col), 'col', 0, 0).reshape(block_rows, width)  7.6 us
    pallas_call x1, Pallas kernels, factor_and_product(): pl.pallas_call(lambda *refs: product_kernel(piece, share, *refs), in_spec...  6.87 us
    all_to_all x1, starting transfers between devices, on_device(): got = lax.all_to_all(sent, 'col', 0, 0)  5.27 us
    ppermute x1, starting transfers between devices, on_device(): turned_image = lax.ppermute(image, BOTH, transposing)  5.03 us
  transfers between devices with their start and end apart: 7, of which 6 were waited for; matrix products, arithmetic and copies ran while one was open for 0% of the time, Pallas kernels for 3%

profile of v8, /device:TPU:1, one launch (start us, length us, event | category | flops | bytes accessed | tf_op | source)
XLA Modules:
  0.0 128.6 jit_solution(14965221768085092346)
XLA Ops:
  0.6 17.1 %copies.1 = f32[16,64,128]{2,1,0:T(8,128)} custom-call(f32[64,128]{1,0:T(8,128)} %rows_ref.1), custom_call_target="tpu_custom_call" | custom-call | bytes 600000 | tf_op jit(solution)/shard_map/copies/pallas_call | solution.py:269
  17.8 7.6 %all-to-all-start = ((f32[16,64,128]{2,1,0:T(8,128)}), f32[16,64,128]{2,1,0:T(8,128)S(1)}, u32[]{:S(2)}, u32[]{:S(2)}) async-start(f32[16,64,128]{2,1,0:T(8,128)} %copies.1), calls=%async_computation | async-start | bytes 1048576 | tf_op jit(solution)/shard_map/all_to_all | solution.py:436
  25.4 4.4 %collective-permute-start = (f32[64,128]{1,0:T(8,128)}, f32[64,128]{1,0:T(8,128)S(1)}, u32[]{:S(2)}, u32[]{:S(2)}) collective-permute-start(f32[64,128]{1,0:T(8,128)} %rows_ref.1), channel_id=1, source_target_pairs={{0,0},{1,16},{2,32},{3,48},{4,64},{5,80},{6,96},{7,112},{8,128},{9... | collective-permute-start | bytes 98312 | tf_op jit(solution)/shard_map/ppermute | solution.py:435
  29.8 2.8 %collective-permute-done = f32[64,128]{1,0:T(8,128)S(1)} collective-permute-done((f32[64,128]{1,0:T(8,128)}, f32[64,128]{1,0:T(8,128)S(1)}, u32[]{:S(2)}, u32[]{:S(2)}) %collective-permute-start) | collective-permute-done | bytes 32800 | tf_op jit(solution)/shard_map/ppermute | solution.py:435
  32.6 3.1 %all-to-all-done = f32[16,64,128]{2,1,0:T(8,128)S(1)} async-done(((f32[16,64,128]{2,1,0:T(8,128)}), f32[16,64,128]{2,1,0:T(8,128)S(1)}, u32[]{:S(2)}, u32[]{:S(2)}) %all-to-all-start) | async-done | bytes 524320 | tf_op jit(solution)/shard_map/all_to_all | solution.py:436
  35.7 0.7 gram_parts.1
  36.4 2.2 %collective-permute-start.1 = (f32[40,128]{1,0:T(8,128)S(1)}, f32[40,128]{1,0:T(8,128)S(1)}, u32[]{:S(2)}, u32[]{:S(2)}) collective-permute-start(f32[40,128]{1,0:T(8,128)S(1)} %get-tuple-element.25), channel_id=1, source_target_pairs={{0,16},{16,0},{32,48},{48,32},{64,80},{80,64},{96,112},{112,96},{1... | collective-permute-start | bytes 61448 | tf_op jit(solution)/shard_map/ppermute | solution.py:441
  38.6 0.8 collective-permute-done.1
  39.5 24.0 %all-gather = f32[1792,128]{1,0:T(8,128)S(1)} all-gather(f32[112,128]{1,0:T(8,128)S(1)} %pad_maximum_fusion), channel_id=2, replica_groups=mesh['row'=16,'col'=16] {'row'}, dimensions={0}, use_global_device_ids=true | all-gather | bytes 974848 | tf_op jit(solution)/shard_map/all_gather | solution.py:442
  63.5 6.9 %factor_and_product.1 = (f32[128,128]{1,0:T(8,128)}, f32[128,128]{1,0:T(8,128)S(1)}, f32[16,72,128]{2,1,0:T(8,128)}) custom-call(f32[16,112,128]{2,1,0:T(8,128)S(1)} %bitcast.4, f32[1024,1024]{1,0:T(8,128)} %refs_4_.1), custom_call_target="tpu_custom_call" | custom-call | flops 805306368 | bytes 6000000 | tf_op jit(solution)/shard_map/factor_and_product/pallas_call | solution.py:232
  70.4 5.3 %all-to-all-start.1 = ((f32[16,72,128]{2,1,0:T(8,128)}), f32[16,72,128]{2,1,0:T(8,128)S(1)}, u32[]{:S(2)}, u32[]{:S(2)}) async-start(f32[16,72,128]{2,1,0:T(8,128)} %get-tuple-element.27), calls=%async_computation.1 | async-start | bytes 1179648 | tf_op jit(solution)/shard_map/all_to_all | solution.py:445
  75.7 0.5 basis_rows.1.refs_2_.turned_ref
  76.2 10.3 %all-to-all-done.1.refs_0_ = f32[16,72,128]{2,1,0:T(8,128)S(1)} async-done(((f32[16,72,128]{2,1,0:T(8,128)}), f32[16,72,128]{2,1,0:T(8,128)S(1)}, u32[]{:S(2)}, u32[]{:S(2)}) %all-to-all-start.1) | async-done | bytes 589856 | tf_op jit(solution)/shard_map/all_to_all | solution.py:445
  86.4 0.9 image_piece.1
  87.3 4.3 %all-to-all-start.2 = ((f32[16,64,128]{2,1,0:T(8,128)}), f32[16,64,128]{2,1,0:T(8,128)S(1)}, u32[]{:S(2)}, u32[]{:S(2)}) async-start(f32[16,64,128]{2,1,0:T(8,128)} %get-tuple-element.30), calls=%async_computation.2 | async-start | bytes 1048576 | tf_op jit(solution)/shard_map/all_to_all | solution.py:452
  91.6 5.0 %collective-permute-start.2 = (f32[64,128]{1,0:T(8,128)S(1)}, f32[64,128]{1,0:T(8,128)S(1)}, u32[]{:S(2)}, u32[]{:S(2)}) collective-permute-start(f32[64,128]{1,0:T(8,128)S(1)} %get-tuple-element.31), channel_id=1, source_target_pairs={{0,0},{1,16},{2,32},{3,48},{4,64},{5,80},{6,96},{7,112},{8,128},{9... | collective-permute-start | bytes 98312 | tf_op jit(solution)/shard_map/ppermute | solution.py:451
  96.6 2.9 %kernel.1 = (bf16[1024,256]{1,0:T(8,128)(2,1)S(1)}, bf16[1024,256]{1,0:T(8,128)(2,1)S(1)}) custom-call(f32[128,128]{1,0:T(8,128)S(1)} %get-tuple-element.28.inverse_ref.refs_0_, f32[128,128]{1,0:T(8,128)S(1)} %get-tuple-element.32.refs_1_, f32[128,1024]{1,0:T(8,128)S(1)} %basis_rows.1.refs_2_.turned_ref, f32[16,112,128]{2,1,0:T(8,128)S(1)} %bitcast.5), custom_call_target="tpu_custom_call" | custom-call | flops 300000000 | bytes 10000000 | tf_op jit(solution)/shard_map/kernel/pallas_call | solution.py:367
  99.6 2.0 %collective-permute-done.2.lone_ref = f32[64,128]{1,0:T(8,128)S(1)} collective-permute-done((f32[64,128]{1,0:T(8,128)S(1)}, f32[64,128]{1,0:T(8,128)S(1)}, u32[]{:S(2)}, u32[]{:S(2)}) %collective-permute-start.2) | collective-permute-done | bytes 32800 | tf_op jit(solution)/shard_map/ppermute | solution.py:451
  101.6 0.0 all-to-all-done.2
  101.6 0.0 copy-start
  101.6 0.7 inner_parts.1
  102.4 2.5 %collective-permute-start.3 = (f32[40,128]{1,0:T(8,128)S(1)}, f32[40,128]{1,0:T(8,128)S(1)}, u32[]{:S(2)}, u32[]{:S(2)}) collective-permute-start(f32[40,128]{1,0:T(8,128)S(1)} %get-tuple-element.38), channel_id=1, source_target_pairs={{0,16},{16,0},{32,48},{48,32},{64,80},{80,64},{96,112},{112,96},{1... | collective-permute-start | bytes 61448 | tf_op jit(solution)/shard_map/ppermute | solution.py:464
  104.9 0.8 collective-permute-done.3.came_ref
  105.7 19.7 %all-gather.1 = f32[1664,128]{1,0:T(8,128)S(1)} all-gather(f32[104,128]{1,0:T(8,128)S(1)} %join.1), channel_id=3, replica_groups=mesh['row'=16,'col'=16] {'row'}, dimensions={0}, use_global_device_ids=true | all-gather | bytes 905216 | tf_op jit(solution)/shard_map/all_gather | solution.py:465
  125.4 0.0 copy-done
  125.4 3.2 %update.1 = f32[1024,1024]{1,0:T(8,128)} custom-call(f32[16,104,128]{2,1,0:T(8,128)S(1)} %bitcast.8, f32[1024,128]{1,0:T(8,128)S(1)} %bitcast.7, bf16[1024,256]{1,0:T(8,128)(2,1)S(1)} %get-tuple-element.39.refs_2_, bf16[1024,256]{1,0:T(8,128)(2,1)S(1)} %get-tuple-element.40.refs_3_, f32[1024,1024]{1,0:T(8,128)S(1)} %copy-done), custom_call_target="tpu_custom_call" | custom-call | flops 1610612736 | bytes 9000000 | tf_op jit(solution)/shard_map/update/pallas_call | solution.py:408
  (3 shorter events, 0.0 us)
Async XLA Ops:
  17.8 17.9 %all-to-all-start = ((f32[16,64,128]{2,1,0:T(8,128)}), f32[16,64,128]{2,1,0:T(8,128)S(1)}, u32[]{:S(2)}, u32[]{:S(2)}) async-start(f32[16,64,128]{2,1,0:T(8,128)} %copies.1), calls=%async_computation | async-start | bytes 1048576 | tf_op jit(solution)/shard_map/all_to_all | solution.py:436
  25.4 7.2 %collective-permute-start = (f32[64,128]{1,0:T(8,128)}, f32[64,128]{1,0:T(8,128)S(1)}, u32[]{:S(2)}, u32[]{:S(2)}) collective-permute-start(f32[64,128]{1,0:T(8,128)} %rows_ref.1), channel_id=1, source_target_pairs={{0,0},{1,16},{2,32},{3,48},{4,64},{5,80},{6,96},{7,112},{8,128},{9... | collective-permute-start | bytes 98312 | tf_op jit(solution)/shard_map/ppermute | solution.py:435
  36.4 3.1 %collective-permute-start.1 = (f32[40,128]{1,0:T(8,128)S(1)}, f32[40,128]{1,0:T(8,128)S(1)}, u32[]{:S(2)}, u32[]{:S(2)}) collective-permute-start(f32[40,128]{1,0:T(8,128)S(1)} %get-tuple-element.25), channel_id=1, source_target_pairs={{0,16},{16,0},{32,48},{48,32},{64,80},{80,64},{96,112},{112,96},{1... | collective-permute-start | bytes 61448 | tf_op jit(solution)/shard_map/ppermute | solution.py:441
  70.4 16.0 %all-to-all-start.1 = ((f32[16,72,128]{2,1,0:T(8,128)}), f32[16,72,128]{2,1,0:T(8,128)S(1)}, u32[]{:S(2)}, u32[]{:S(2)}) async-start(f32[16,72,128]{2,1,0:T(8,128)} %get-tuple-element.27), calls=%async_computation.1 | async-start | bytes 1179648 | tf_op jit(solution)/shard_map/all_to_all | solution.py:445
  87.3 14.3 %all-to-all-start.2 = ((f32[16,64,128]{2,1,0:T(8,128)}), f32[16,64,128]{2,1,0:T(8,128)S(1)}, u32[]{:S(2)}, u32[]{:S(2)}) async-start(f32[16,64,128]{2,1,0:T(8,128)} %get-tuple-element.30), calls=%async_computation.2 | async-start | bytes 1048576 | tf_op jit(solution)/shard_map/all_to_all | solution.py:452
  91.6 10.0 %collective-permute-start.2 = (f32[64,128]{1,0:T(8,128)S(1)}, f32[64,128]{1,0:T(8,128)S(1)}, u32[]{:S(2)}, u32[]{:S(2)}) collective-permute-start(f32[64,128]{1,0:T(8,128)S(1)} %get-tuple-element.31), channel_id=1, source_target_pairs={{0,0},{1,16},{2,32},{3,48},{4,64},{5,80},{6,96},{7,112},{8,128},{9... | collective-permute-start | bytes 98312 | tf_op jit(solution)/shard_map/ppermute | solution.py:451
  101.6 23.8 %copy-start = (f32[1024,1024]{1,0:T(8,128)S(1)}, f32[1024,1024]{1,0:T(8,128)}, u32[]{:S(2)}) copy-start(f32[1024,1024]{1,0:T(8,128)} %refs_4_.1) | copy-start | bytes 12582916
  102.4 3.3 %collective-permute-start.3 = (f32[40,128]{1,0:T(8,128)S(1)}, f32[40,128]{1,0:T(8,128)S(1)}, u32[]{:S(2)}, u32[]{:S(2)}) collective-permute-start(f32[40,128]{1,0:T(8,128)S(1)} %get-tuple-element.38), channel_id=1, source_target_pairs={{0,16},{16,0},{32,48},{48,32},{64,80},{80,64},{96,112},{112,96},{1... | collective-permute-start | bytes 61448 | tf_op jit(solution)/shard_map/ppermute | solution.py:464

commit v9 on v8

--- a/solution.py
+++ b/solution.py
@@ -85,19 +85,19 @@
 
 
 def unpack(parts_ref, piece):
-    width = parts_ref.shape[2]
-    half = width // 4
-    stop = piece + half + STEP
-    sums = [parts_ref[h, piece:stop, :] for h in range(2)]
-    for i in range(2, parts_ref.shape[0]):
-        sums[i % 2] = sums[i % 2] + parts_ref[i, piece:stop, :]
+    half = parts_ref.shape[2] // 4
+    stop = piece + half
+    sums = [parts_ref[0, piece:stop, :], parts_ref[1, piece : stop + STEP, :]]
+    for i in range(2, parts_ref.shape[0], 2):
+        sums[0] = sums[0] + parts_ref[i, piece:stop, :]
+        sums[1] = sums[1] + parts_ref[i + 1, piece : stop + STEP, :]
     side = 2 * half
-    rows = jnp.concatenate([sums[0][:half], sums[1][:half]], 0)
+    rows = jnp.concatenate([sums[0], sums[1][:half]], 0)
     turned = rows.T
     row = lax.broadcasted_iota(jnp.int32, (side, side), 0)
     lane = lax.broadcasted_iota(jnp.int32, (side, side), 1)
     left, across = rows[:, :side], turned[:side]
-    last = sums[0][half : half + 1, :side]
+    last = sums[1][half : half + 1, :side]
     a = jnp.where(row >= lane, left, across)
     d = jnp.where(row == lane, last, jnp.where(row < lane, left, across))
     return jnp.concatenate(
@@ -254,24 +254,21 @@
     )(parts, mobility)
 
 
-def copy_kernel(rows_ref, out_ref, sems):
-    sends = []
-    for k in range(out_ref.shape[0]):
-        sends.append(pltpu.make_async_copy(rows_ref, out_ref.at[k], sems.at[k]))
-        sends[k].start()
-    for send in sends:
-        send.wait()
+def copy_kernel(rows_ref, out_ref, held, sem):
+    load = pltpu.make_async_copy(rows_ref, held, sem)
+    load.start()
+    load.wait()
+    out_ref[...] = jnp.broadcast_to(held[...][None], out_ref.shape)
 
 
 def copies(rows, count):
     hbm = pl.BlockSpec(memory_space=pltpu.HBM)
-    shape = (count,) + rows.shape
     return pl.pallas_call(
         copy_kernel,
         in_specs=[hbm],
-        out_specs=hbm,
-        out_shape=pltpu.HBM(shape, rows.dtype),
-        scratch_shapes=[pltpu.SemaphoreType.DMA((count,))],
+        out_specs=pl.BlockSpec(memory_space=pltpu.VMEM),
+        out_shape=jax.ShapeDtypeStruct((count,) + rows.shape, rows.dtype),
+        scratch_shapes=[pltpu.VMEM(rows.shape, rows.dtype), pltpu.SemaphoreType.DMA],
         cost_estimate=pl.CostEstimate(flops=0, bytes_accessed=600_000, transcendentals=0),
         compiler_params=pltpu.CompilerParams(vmem_limit_bytes=4 * MIB),
         name="copies",
@@ -439,7 +436,10 @@
         gram_kernel, (panel_rows,), [(share, width)], "gram_parts"
     )
     packed = keep + lax.ppermute(give, "row", swap)
-    panel_parts = lax.all_gather(jnp.concatenate([turned_panel, packed, top_part], 0), "row", axis=0)
+    even = lax.axis_index("row") % 2 == 0
+    tail = jnp.where(even, top_part, packed[-STEP:])
+    sent = jnp.concatenate([turned_panel, packed[:-STEP], tail], 0)
+    panel_parts = lax.all_gather(sent, "row", axis=0)
 
     panel_factor, inverse, sent = factor_and_product(panel_parts, mobility, piece, share)
     got = lax.all_to_all(sent, "col", 0, 0)

time: 129 us -> 114 us (0.88)
  Pallas kernels: 33 us -> 17.5 us
    pallas_call x1, Pallas kernels: 17.1 us -> 1.61 us  [copies(): pl.pallas_call(copy_kernel, in_specs=[hbm], out_specs=pl.BlockSpec(memory...]
where the time goes in v9:
time: 114 us; the launch traced here: 113 us
  blocking collectives  43.5 us (38%)
  starting transfers between devices  31.3 us (27%)
  waiting for transfers between devices  19.9 us (17%)
  Pallas kernels  17.5 us (15%)
    all_gather x1, blocking collectives, on_device(): panel_parts = lax.all_gather(sent, 'row', axis=0)  23.9 us
    all_gather x1, blocking collectives, on_device(): lax.all_gather(join(turned_image, keep, came, mobility), 'row', axis=0)  19.7 us
    all_to_all x1, waiting for transfers between devices, on_device(): got = lax.all_to_all(sent, 'col', 0, 0)  10.3 us
    all_to_all x1, starting transfers between devices, on_device(): lax.all_to_all(copies(panel, n_col), 'col', 0, 0).reshape(block_rows, width)  7.6 us
    pallas_call x1, Pallas kernels, factor_and_product(): pl.pallas_call(lambda *refs: product_kernel(piece, share, *refs), in_spec...  6.87 us
    all_to_all x1, starting transfers between devices, on_device(): got = lax.all_to_all(sent, 'col', 0, 0)  5.28 us
    ppermute x1, starting transfers between devices, on_device(): turned_image = lax.ppermute(image, BOTH, transposing)  5.03 us
    ppermute x1, starting transfers between devices, on_device(): turned_panel = lax.ppermute(panel, BOTH, transposing)  4.38 us
  transfers between devices with their start and end apart: 7, of which 6 were waited for; matrix products, arithmetic and copies ran while one was open for 0% of the time, Pallas kernels for 3%

profile of v9, /device:TPU:1, one launch (start us, length us, event | category | flops | bytes accessed | tf_op | source)
XLA Modules:
  0.0 112.9 jit_solution(7035376329256598660)
XLA Ops:
  0.6 1.6 %copies.1 = f32[16,64,128]{2,1,0:T(8,128)} custom-call(f32[64,128]{1,0:T(8,128)} %rows_ref.1), custom_call_target="tpu_custom_call" | custom-call | bytes 600000 | tf_op jit(solution)/shard_map/copies/pallas_call | solution.py:266
  2.2 7.6 %all-to-all-start = ((f32[16,64,128]{2,1,0:T(8,128)}), f32[16,64,128]{2,1,0:T(8,128)S(1)}, u32[]{:S(2)}, u32[]{:S(2)}) async-start(f32[16,64,128]{2,1,0:T(8,128)} %copies.1), calls=%async_computation | async-start | bytes 1048576 | tf_op jit(solution)/shard_map/all_to_all | solution.py:433
  9.9 4.4 %collective-permute-start = (f32[64,128]{1,0:T(8,128)}, f32[64,128]{1,0:T(8,128)S(1)}, u32[]{:S(2)}, u32[]{:S(2)}) collective-permute-start(f32[64,128]{1,0:T(8,128)} %rows_ref.1), channel_id=1, source_target_pairs={{0,0},{1,16},{2,32},{3,48},{4,64},{5,80},{6,96},{7,112},{8,128},{9... | collective-permute-start | bytes 98312 | tf_op jit(solution)/shard_map/ppermute | solution.py:432
  14.2 2.8 %collective-permute-done = f32[64,128]{1,0:T(8,128)S(1)} collective-permute-done((f32[64,128]{1,0:T(8,128)}, f32[64,128]{1,0:T(8,128)S(1)}, u32[]{:S(2)}, u32[]{:S(2)}) %collective-permute-start) | collective-permute-done | bytes 32800 | tf_op jit(solution)/shard_map/ppermute | solution.py:432
  17.0 3.1 %all-to-all-done = f32[16,64,128]{2,1,0:T(8,128)S(1)} async-done(((f32[16,64,128]{2,1,0:T(8,128)}), f32[16,64,128]{2,1,0:T(8,128)S(1)}, u32[]{:S(2)}, u32[]{:S(2)}) %all-to-all-start) | async-done | bytes 524320 | tf_op jit(solution)/shard_map/all_to_all | solution.py:433
  20.2 0.7 gram_parts.1
  20.9 2.2 %collective-permute-start.1 = (f32[40,128]{1,0:T(8,128)S(1)}, f32[40,128]{1,0:T(8,128)S(1)}, u32[]{:S(2)}, u32[]{:S(2)}) collective-permute-start(f32[40,128]{1,0:T(8,128)S(1)} %get-tuple-element.25), channel_id=1, source_target_pairs={{0,16},{16,0},{32,48},{48,32},{64,80},{80,64},{96,112},{112,96},{1... | collective-permute-start | bytes 61448 | tf_op jit(solution)/shard_map/ppermute | solution.py:438
  23.1 0.8 collective-permute-done.1
  24.0 23.9 %all-gather = f32[1664,128]{1,0:T(8,128)S(1)} all-gather(f32[104,128]{1,0:T(8,128)S(1)} %pad_maximum_fusion), channel_id=2, replica_groups=mesh['row'=16,'col'=16] {'row'}, dimensions={0}, use_global_device_ids=true | all-gather | bytes 905216 | tf_op jit(solution)/shard_map/all_gather | solution.py:442
  47.8 6.9 %factor_and_product.1 = (f32[128,128]{1,0:T(8,128)}, f32[128,128]{1,0:T(8,128)S(1)}, f32[16,72,128]{2,1,0:T(8,128)}) custom-call(f32[16,104,128]{2,1,0:T(8,128)S(1)} %bitcast.4, f32[1024,1024]{1,0:T(8,128)} %refs_4_.1), custom_call_target="tpu_custom_call" | custom-call | flops 805306368 | bytes 6000000 | tf_op jit(solution)/shard_map/factor_and_product/pallas_call | solution.py:232
  54.7 5.3 %all-to-all-start.1 = ((f32[16,72,128]{2,1,0:T(8,128)}), f32[16,72,128]{2,1,0:T(8,128)S(1)}, u32[]{:S(2)}, u32[]{:S(2)}) async-start(f32[16,72,128]{2,1,0:T(8,128)} %get-tuple-element.27), calls=%async_computation.1 | async-start | bytes 1179648 | tf_op jit(solution)/shard_map/all_to_all | solution.py:445
  60.0 0.5 basis_rows.1.refs_2_.turned_ref
  60.5 10.3 %all-to-all-done.1.refs_0_ = f32[16,72,128]{2,1,0:T(8,128)S(1)} async-done(((f32[16,72,128]{2,1,0:T(8,128)}), f32[16,72,128]{2,1,0:T(8,128)S(1)}, u32[]{:S(2)}, u32[]{:S(2)}) %all-to-all-start.1) | async-done | bytes 589856 | tf_op jit(solution)/shard_map/all_to_all | solution.py:445
  70.8 0.9 image_piece.1
  71.6 4.3 %all-to-all-start.2 = ((f32[16,64,128]{2,1,0:T(8,128)}), f32[16,64,128]{2,1,0:T(8,128)S(1)}, u32[]{:S(2)}, u32[]{:S(2)}) async-start(f32[16,64,128]{2,1,0:T(8,128)} %get-tuple-element.30), calls=%async_computation.2 | async-start | bytes 1048576 | tf_op jit(solution)/shard_map/all_to_all | solution.py:452
  75.9 5.0 %collective-permute-start.2 = (f32[64,128]{1,0:T(8,128)S(1)}, f32[64,128]{1,0:T(8,128)S(1)}, u32[]{:S(2)}, u32[]{:S(2)}) collective-permute-start(f32[64,128]{1,0:T(8,128)S(1)} %get-tuple-element.31), channel_id=1, source_target_pairs={{0,0},{1,16},{2,32},{3,48},{4,64},{5,80},{6,96},{7,112},{8,128},{9... | collective-permute-start | bytes 98312 | tf_op jit(solution)/shard_map/ppermute | solution.py:451
  81.0 2.9 %kernel.1 = (bf16[1024,256]{1,0:T(8,128)(2,1)S(1)}, bf16[1024,256]{1,0:T(8,128)(2,1)S(1)}) custom-call(f32[128,128]{1,0:T(8,128)S(1)} %get-tuple-element.28.inverse_ref.refs_0_, f32[128,128]{1,0:T(8,128)S(1)} %get-tuple-element.32.refs_1_, f32[128,1024]{1,0:T(8,128)S(1)} %basis_rows.1.refs_2_.turned_ref, f32[16,104,128]{2,1,0:T(8,128)S(1)} %bitcast.5), custom_call_target="tpu_custom_call" | custom-call | flops 300000000 | bytes 10000000 | tf_op jit(solution)/shard_map/kernel/pallas_call | solution.py:364
  83.9 2.0 %collective-permute-done.2.lone_ref = f32[64,128]{1,0:T(8,128)S(1)} collective-permute-done((f32[64,128]{1,0:T(8,128)S(1)}, f32[64,128]{1,0:T(8,128)S(1)}, u32[]{:S(2)}, u32[]{:S(2)}) %collective-permute-start.2) | collective-permute-done | bytes 32800 | tf_op jit(solution)/shard_map/ppermute | solution.py:451
  86.0 0.0 all-to-all-done.2
  86.0 0.0 copy-start
  86.0 0.7 inner_parts.1
  86.7 2.5 %collective-permute-start.3 = (f32[40,128]{1,0:T(8,128)S(1)}, f32[40,128]{1,0:T(8,128)S(1)}, u32[]{:S(2)}, u32[]{:S(2)}) collective-permute-start(f32[40,128]{1,0:T(8,128)S(1)} %get-tuple-element.38), channel_id=1, source_target_pairs={{0,16},{16,0},{32,48},{48,32},{64,80},{80,64},{96,112},{112,96},{1... | collective-permute-start | bytes 61448 | tf_op jit(solution)/shard_map/ppermute | solution.py:464
  89.2 0.8 collective-permute-done.3.came_ref
  90.0 19.7 %all-gather.1 = f32[1664,128]{1,0:T(8,128)S(1)} all-gather(f32[104,128]{1,0:T(8,128)S(1)} %join.1), channel_id=3, replica_groups=mesh['row'=16,'col'=16] {'row'}, dimensions={0}, use_global_device_ids=true | all-gather | bytes 905216 | tf_op jit(solution)/shard_map/all_gather | solution.py:465
  109.7 0.0 copy-done
  109.7 3.2 %update.1 = f32[1024,1024]{1,0:T(8,128)} custom-call(f32[16,104,128]{2,1,0:T(8,128)S(1)} %bitcast.8, f32[1024,128]{1,0:T(8,128)S(1)} %bitcast.7, bf16[1024,256]{1,0:T(8,128)(2,1)S(1)} %get-tuple-element.39.refs_2_, bf16[1024,256]{1,0:T(8,128)(2,1)S(1)} %get-tuple-element.40.refs_3_, f32[1024,1024]{1,0:T(8,128)S(1)} %copy-done), custom_call_target="tpu_custom_call" | custom-call | flops 1610612736 | bytes 9000000 | tf_op jit(solution)/shard_map/update/pallas_call | solution.py:405
  (5 shorter events, 0.0 us)
Async XLA Ops:
  2.2 17.9 %all-to-all-start = ((f32[16,64,128]{2,1,0:T(8,128)}), f32[16,64,128]{2,1,0:T(8,128)S(1)}, u32[]{:S(2)}, u32[]{:S(2)}) async-start(f32[16,64,128]{2,1,0:T(8,128)} %copies.1), calls=%async_computation | async-start | bytes 1048576 | tf_op jit(solution)/shard_map/all_to_all | solution.py:433
  9.9 7.2 %collective-permute-start = (f32[64,128]{1,0:T(8,128)}, f32[64,128]{1,0:T(8,128)S(1)}, u32[]{:S(2)}, u32[]{:S(2)}) collective-permute-start(f32[64,128]{1,0:T(8,128)} %rows_ref.1), channel_id=1, source_target_pairs={{0,0},{1,16},{2,32},{3,48},{4,64},{5,80},{6,96},{7,112},{8,128},{9... | collective-permute-start | bytes 98312 | tf_op jit(solution)/shard_map/ppermute | solution.py:432
  20.9 3.1 %collective-permute-start.1 = (f32[40,128]{1,0:T(8,128)S(1)}, f32[40,128]{1,0:T(8,128)S(1)}, u32[]{:S(2)}, u32[]{:S(2)}) collective-permute-start(f32[40,128]{1,0:T(8,128)S(1)} %get-tuple-element.25), channel_id=1, source_target_pairs={{0,16},{16,0},{32,48},{48,32},{64,80},{80,64},{96,112},{112,96},{1... | collective-permute-start | bytes 61448 | tf_op jit(solution)/shard_map/ppermute | solution.py:438
  54.7 16.0 %all-to-all-start.1 = ((f32[16,72,128]{2,1,0:T(8,128)}), f32[16,72,128]{2,1,0:T(8,128)S(1)}, u32[]{:S(2)}, u32[]{:S(2)}) async-start(f32[16,72,128]{2,1,0:T(8,128)} %get-tuple-element.27), calls=%async_computation.1 | async-start | bytes 1179648 | tf_op jit(solution)/shard_map/all_to_all | solution.py:445
  71.6 14.3 %all-to-all-start.2 = ((f32[16,64,128]{2,1,0:T(8,128)}), f32[16,64,128]{2,1,0:T(8,128)S(1)}, u32[]{:S(2)}, u32[]{:S(2)}) async-start(f32[16,64,128]{2,1,0:T(8,128)} %get-tuple-element.30), calls=%async_computation.2 | async-start | bytes 1048576 | tf_op jit(solution)/shard_map/all_to_all | solution.py:452
  75.9 10.0 %collective-permute-start.2 = (f32[64,128]{1,0:T(8,128)S(1)}, f32[64,128]{1,0:T(8,128)S(1)}, u32[]{:S(2)}, u32[]{:S(2)}) collective-permute-start(f32[64,128]{1,0:T(8,128)S(1)} %get-tuple-element.31), channel_id=1, source_target_pairs={{0,0},{1,16},{2,32},{3,48},{4,64},{5,80},{6,96},{7,112},{8,128},{9... | collective-permute-start | bytes 98312 | tf_op jit(solution)/shard_map/ppermute | solution.py:451
  86.0 23.8 %copy-start = (f32[1024,1024]{1,0:T(8,128)S(1)}, f32[1024,1024]{1,0:T(8,128)}, u32[]{:S(2)}) copy-start(f32[1024,1024]{1,0:T(8,128)} %refs_4_.1) | copy-start | bytes 12582916
  86.7 3.3 %collective-permute-start.3 = (f32[40,128]{1,0:T(8,128)S(1)}, f32[40,128]{1,0:T(8,128)S(1)}, u32[]{:S(2)}, u32[]{:S(2)}) collective-permute-start(f32[40,128]{1,0:T(8,128)S(1)} %get-tuple-element.38), channel_id=1, source_target_pairs={{0,16},{16,0},{32,48},{48,32},{64,80},{80,64},{96,112},{112,96},{1... | collective-permute-start | bytes 61448 | tf_op jit(solution)/shard_map/ppermute | solution.py:464

commit v10 on v9

--- a/solution.py
+++ b/solution.py
@@ -132,7 +132,7 @@
         out_specs=[vmem] * len(shapes),
         out_shape=[jax.ShapeDtypeStruct(shape, jnp.float32) for shape in shapes],
         cost_estimate=pl.CostEstimate(
-            flops=200_000_000, bytes_accessed=3_000_000, transcendentals=0
+            flops=1_000, bytes_accessed=1_000, transcendentals=0
         ),
         compiler_params=pltpu.CompilerParams(vmem_limit_bytes=8 * MIB),
         name=name,
@@ -431,10 +431,10 @@
 
     turned_panel = lax.ppermute(panel, BOTH, transposing)
     panel_rows = lax.all_to_all(copies(panel, n_col), "col", 0, 0).reshape(block_rows, width)
-    panel_rows, turned_panel = lax.optimization_barrier((panel_rows, turned_panel))
     keep, give, top_part = packed_parts(
         gram_kernel, (panel_rows,), [(share, width)], "gram_parts"
     )
+    give, turned_panel = lax.optimization_barrier((give, turned_panel))
     packed = keep + lax.ppermute(give, "row", swap)
     even = lax.axis_index("row") % 2 == 0
     tail = jnp.where(even, top_part, packed[-STEP:])
@@ -457,9 +457,7 @@
         [pltpu.VMEM((2 * width, width), jnp.float32)],
         "kernel",
     )
-    image_rows, turned_image, rows_left = lax.optimization_barrier(
-        (image_rows, turned_image, rows_left)
-    )
+    image_rows, rows_left = lax.optimization_barrier((image_rows, rows_left))
     keep, give = packed_parts(inner_kernel, (turned_rows, image_rows), [], "inner_parts")
     came = lax.ppermute(give, "row", swap)
     image_parts = lax.all_gather(join(turned_image, keep, came, mobility), "row", axis=0)

time: 114 us -> 112 us (0.982)
  blocking collectives: 43.5 us -> 42.1 us
    all_to_all x1, waiting for transfers between devices: 3.12 us -> 5.91 us  [on_device(): lax.all_to_all(copies(panel, n_col), 'col', 0, 0).reshape(block_rows, width)]
    ppermute x1, waiting for transfers between devices: 2.79 us -> 0.01 us  [on_device(): turned_panel = lax.ppermute(panel, BOTH, transposing)]
    ppermute x1, waiting for transfers between devices: 2.04 us -> 0.01 us  [on_device(): turned_image = lax.ppermute(image, BOTH, transposing)]
  transfers between devices with their start and end apart: 7 -> 7, of which waited for: 6 -> 5; matrix products, arithmetic and copies ran while one was open for 0% -> 0% of each run, Pallas kernels for 3% -> 4%
where the time goes in v10:
time: 112 us; the launch traced here: 111 us
  blocking collectives  42.1 us (38%)
  starting transfers between devices  32.2 us (29%)
  waiting for transfers between devices  18.8 us (17%)
  Pallas kernels  17.4 us (16%)
    all_gather x1, blocking collectives, on_device(): panel_parts = lax.all_gather(sent, 'row', axis=0)  23.2 us
    all_gather x1, blocking collectives, on_device(): lax.all_gather(join(turned_image, keep, came, mobility), 'row', axis=0)  18.9 us
    all_to_all x1, waiting for transfers between devices, on_device(): got = lax.all_to_all(sent, 'col', 0, 0)  10.3 us
    all_to_all x1, starting transfers between devices, on_device(): lax.all_to_all(copies(panel, n_col), 'col', 0, 0).reshape(block_rows, width)  7.6 us
    pallas_call x1, Pallas kernels, factor_and_product(): pl.pallas_call(lambda *refs: product_kernel(piece, share, *refs), in_spec...  6.86 us
    all_to_all x1, waiting for transfers between devices, on_device(): lax.all_to_all(copies(panel, n_col), 'col', 0, 0).reshape(block_rows, width)  5.91 us
    all_to_all x1, starting transfers between devices, on_device(): got = lax.all_to_all(sent, 'col', 0, 0)  5.11 us
    ppermute x1, starting transfers between devices, on_device(): turned_image = lax.ppermute(image, BOTH, transposing)  5.03 us
  transfers between devices with their start and end apart: 7, of which 5 were waited for; matrix products, arithmetic and copies ran while one was open for 0% of the time, Pallas kernels for 4%

profile of v10, /device:TPU:1, one launch (start us, length us, event | category | flops | bytes accessed | tf_op | source)
XLA Modules:
  0.0 111.4 jit_solution(5979298660198104052)
XLA Ops:
  0.6 1.6 %copies.1 = f32[16,64,128]{2,1,0:T(8,128)} custom-call(f32[64,128]{1,0:T(8,128)} %rows_ref.1), custom_call_target="tpu_custom_call" | custom-call | bytes 600000 | tf_op jit(solution)/shard_map/copies/pallas_call | solution.py:266
  2.2 7.6 %all-to-all-start = ((f32[16,64,128]{2,1,0:T(8,128)}), f32[16,64,128]{2,1,0:T(8,128)S(1)}, u32[]{:S(2)}, u32[]{:S(2)}) async-start(f32[16,64,128]{2,1,0:T(8,128)} %copies.1), calls=%async_computation | async-start | bytes 1048576 | tf_op jit(solution)/shard_map/all_to_all | solution.py:433
  9.9 4.4 %collective-permute-start = (f32[64,128]{1,0:T(8,128)}, f32[64,128]{1,0:T(8,128)S(1)}, u32[]{:S(2)}, u32[]{:S(2)}) collective-permute-start(f32[64,128]{1,0:T(8,128)} %rows_ref.1), channel_id=1, source_target_pairs={{0,0},{1,16},{2,32},{3,48},{4,64},{5,80},{6,96},{7,112},{8,128},{9... | collective-permute-start | bytes 98312 | tf_op jit(solution)/shard_map/ppermute | solution.py:432
  14.2 5.9 %all-to-all-done = f32[16,64,128]{2,1,0:T(8,128)S(1)} async-done(((f32[16,64,128]{2,1,0:T(8,128)}), f32[16,64,128]{2,1,0:T(8,128)S(1)}, u32[]{:S(2)}, u32[]{:S(2)}) %all-to-all-start) | async-done | bytes 524320 | tf_op jit(solution)/shard_map/all_to_all | solution.py:433
  20.2 0.7 gram_parts.1
  20.9 0.0 collective-permute-done
  20.9 2.2 %collective-permute-start.1 = (f32[40,128]{1,0:T(8,128)S(1)}, f32[40,128]{1,0:T(8,128)S(1)}, u32[]{:S(2)}, u32[]{:S(2)}) collective-permute-start(f32[40,128]{1,0:T(8,128)S(1)} %get-tuple-element.24), channel_id=1, source_target_pairs={{0,16},{16,0},{32,48},{48,32},{64,80},{80,64},{96,112},{112,96},{1... | collective-permute-start | bytes 61448 | tf_op jit(solution)/shard_map/ppermute | solution.py:438
  23.1 0.8 collective-permute-done.1
  24.0 23.2 %all-gather = f32[1664,128]{1,0:T(8,128)S(1)} all-gather(f32[104,128]{1,0:T(8,128)S(1)} %pad_maximum_fusion), channel_id=2, replica_groups=mesh['row'=16,'col'=16] {'row'}, dimensions={0}, use_global_device_ids=true | all-gather | bytes 905216 | tf_op jit(solution)/shard_map/all_gather | solution.py:442
  47.2 6.9 %factor_and_product.1 = (f32[128,128]{1,0:T(8,128)}, f32[128,128]{1,0:T(8,128)S(1)}, f32[16,72,128]{2,1,0:T(8,128)}) custom-call(f32[16,104,128]{2,1,0:T(8,128)S(1)} %bitcast.4, f32[1024,1024]{1,0:T(8,128)} %refs_4_.1), custom_call_target="tpu_custom_call" | custom-call | flops 805306368 | bytes 6000000 | tf_op jit(solution)/shard_map/factor_and_product/pallas_call | solution.py:232
  54.1 5.1 %all-to-all-start.1 = ((f32[16,72,128]{2,1,0:T(8,128)}), f32[16,72,128]{2,1,0:T(8,128)S(1)}, u32[]{:S(2)}, u32[]{:S(2)}) async-start(f32[16,72,128]{2,1,0:T(8,128)} %get-tuple-element.26), calls=%async_computation.1 | async-start | bytes 1179648 | tf_op jit(solution)/shard_map/all_to_all | solution.py:445
  59.2 0.5 basis_rows.1.refs_2_.turned_ref
  59.7 10.3 %all-to-all-done.1.refs_0_ = f32[16,72,128]{2,1,0:T(8,128)S(1)} async-done(((f32[16,72,128]{2,1,0:T(8,128)}), f32[16,72,128]{2,1,0:T(8,128)S(1)}, u32[]{:S(2)}, u32[]{:S(2)}) %all-to-all-start.1) | async-done | bytes 589856 | tf_op jit(solution)/shard_map/all_to_all | solution.py:445
  69.9 0.9 image_piece.1
  70.8 4.3 %all-to-all-start.2 = ((f32[16,64,128]{2,1,0:T(8,128)}), f32[16,64,128]{2,1,0:T(8,128)S(1)}, u32[]{:S(2)}, u32[]{:S(2)}) async-start(f32[16,64,128]{2,1,0:T(8,128)} %get-tuple-element.31), calls=%async_computation.2 | async-start | bytes 1048576 | tf_op jit(solution)/shard_map/all_to_all | solution.py:452
  75.1 5.0 %collective-permute-start.2 = (f32[64,128]{1,0:T(8,128)S(1)}, f32[64,128]{1,0:T(8,128)S(1)}, u32[]{:S(2)}, u32[]{:S(2)}) collective-permute-start(f32[64,128]{1,0:T(8,128)S(1)} %get-tuple-element.29), channel_id=1, source_target_pairs={{0,0},{1,16},{2,32},{3,48},{4,64},{5,80},{6,96},{7,112},{8,128},{9... | collective-permute-start | bytes 98312 | tf_op jit(solution)/shard_map/ppermute | solution.py:451
  80.1 2.9 %kernel.1 = (bf16[1024,256]{1,0:T(8,128)(2,1)S(1)}, bf16[1024,256]{1,0:T(8,128)(2,1)S(1)}) custom-call(f32[128,128]{1,0:T(8,128)S(1)} %get-tuple-element.27.inverse_ref.refs_0_, f32[128,128]{1,0:T(8,128)S(1)} %get-tuple-element.32.refs_1_, f32[128,1024]{1,0:T(8,128)S(1)} %basis_rows.1.refs_2_.turned_ref, f32[16,104,128]{2,1,0:T(8,128)S(1)} %bitcast.5), custom_call_target="tpu_custom_call" | custom-call | flops 300000000 | bytes 10000000 | tf_op jit(solution)/shard_map/kernel/pallas_call | solution.py:364
  83.1 1.0 all-to-all-done.2
  84.0 0.0 copy-start
  84.1 0.7 inner_parts.1
  84.8 3.6 %collective-permute-start.3 = (f32[40,128]{1,0:T(8,128)S(1)}, f32[40,128]{1,0:T(8,128)S(1)}, u32[]{:S(2)}, u32[]{:S(2)}) collective-permute-start(f32[40,128]{1,0:T(8,128)S(1)} %get-tuple-element.36), channel_id=1, source_target_pairs={{0,16},{16,0},{32,48},{48,32},{64,80},{80,64},{96,112},{112,96},{1... | collective-permute-start | bytes 61448 | tf_op jit(solution)/shard_map/ppermute | solution.py:462
  88.4 0.0 collective-permute-done.2.lone_ref
  88.4 0.8 collective-permute-done.3.came_ref
  89.2 18.9 %all-gather.1 = f32[1664,128]{1,0:T(8,128)S(1)} all-gather(f32[104,128]{1,0:T(8,128)S(1)} %join.1), channel_id=3, replica_groups=mesh['row'=16,'col'=16] {'row'}, dimensions={0}, use_global_device_ids=true | all-gather | bytes 905216 | tf_op jit(solution)/shard_map/all_gather | solution.py:463
  108.1 0.0 copy-done
  108.1 3.2 %update.1 = f32[1024,1024]{1,0:T(8,128)} custom-call(f32[16,104,128]{2,1,0:T(8,128)S(1)} %bitcast.10, f32[1024,128]{1,0:T(8,128)S(1)} %bitcast.9, bf16[1024,256]{1,0:T(8,128)(2,1)S(1)} %get-tuple-element.37.refs_2_, bf16[1024,256]{1,0:T(8,128)(2,1)S(1)} %get-tuple-element.38.refs_3_, f32[1024,1024]{1,0:T(8,128)S(1)} %copy-done), custom_call_target="tpu_custom_call" | custom-call | flops 1610612736 | bytes 9000000 | tf_op jit(solution)/shard_map/update/pallas_call | solution.py:405
  (5 shorter events, 0.0 us)
Async XLA Ops:
  2.2 17.9 %all-to-all-start = ((f32[16,64,128]{2,1,0:T(8,128)}), f32[16,64,128]{2,1,0:T(8,128)S(1)}, u32[]{:S(2)}, u32[]{:S(2)}) async-start(f32[16,64,128]{2,1,0:T(8,128)} %copies.1), calls=%async_computation | async-start | bytes 1048576 | tf_op jit(solution)/shard_map/all_to_all | solution.py:433
  9.9 11.0 %collective-permute-start = (f32[64,128]{1,0:T(8,128)}, f32[64,128]{1,0:T(8,128)S(1)}, u32[]{:S(2)}, u32[]{:S(2)}) collective-permute-start(f32[64,128]{1,0:T(8,128)} %rows_ref.1), channel_id=1, source_target_pairs={{0,0},{1,16},{2,32},{3,48},{4,64},{5,80},{6,96},{7,112},{8,128},{9... | collective-permute-start | bytes 98312 | tf_op jit(solution)/shard_map/ppermute | solution.py:432
  20.9 3.1 %collective-permute-start.1 = (f32[40,128]{1,0:T(8,128)S(1)}, f32[40,128]{1,0:T(8,128)S(1)}, u32[]{:S(2)}, u32[]{:S(2)}) collective-permute-start(f32[40,128]{1,0:T(8,128)S(1)} %get-tuple-element.24), channel_id=1, source_target_pairs={{0,16},{16,0},{32,48},{48,32},{64,80},{80,64},{96,112},{112,96},{1... | collective-permute-start | bytes 61448 | tf_op jit(solution)/shard_map/ppermute | solution.py:438
  54.1 15.9 %all-to-all-start.1 = ((f32[16,72,128]{2,1,0:T(8,128)}), f32[16,72,128]{2,1,0:T(8,128)S(1)}, u32[]{:S(2)}, u32[]{:S(2)}) async-start(f32[16,72,128]{2,1,0:T(8,128)} %get-tuple-element.26), calls=%async_computation.1 | async-start | bytes 1179648 | tf_op jit(solution)/shard_map/all_to_all | solution.py:445
  70.8 13.3 %all-to-all-start.2 = ((f32[16,64,128]{2,1,0:T(8,128)}), f32[16,64,128]{2,1,0:T(8,128)S(1)}, u32[]{:S(2)}, u32[]{:S(2)}) async-start(f32[16,64,128]{2,1,0:T(8,128)} %get-tuple-element.31), calls=%async_computation.2 | async-start | bytes 1048576 | tf_op jit(solution)/shard_map/all_to_all | solution.py:452
  75.1 13.3 %collective-permute-start.2 = (f32[64,128]{1,0:T(8,128)S(1)}, f32[64,128]{1,0:T(8,128)S(1)}, u32[]{:S(2)}, u32[]{:S(2)}) collective-permute-start(f32[64,128]{1,0:T(8,128)S(1)} %get-tuple-element.29), channel_id=1, source_target_pairs={{0,0},{1,16},{2,32},{3,48},{4,64},{5,80},{6,96},{7,112},{8,128},{9... | collective-permute-start | bytes 98312 | tf_op jit(solution)/shard_map/ppermute | solution.py:451
  84.0 24.1 %copy-start = (f32[1024,1024]{1,0:T(8,128)S(1)}, f32[1024,1024]{1,0:T(8,128)}, u32[]{:S(2)}) copy-start(f32[1024,1024]{1,0:T(8,128)} %refs_4_.1) | copy-start | bytes 12582916
  84.8 4.4 %collective-permute-start.3 = (f32[40,128]{1,0:T(8,128)S(1)}, f32[40,128]{1,0:T(8,128)S(1)}, u32[]{:S(2)}, u32[]{:S(2)}) collective-permute-start(f32[40,128]{1,0:T(8,128)S(1)} %get-tuple-element.36), channel_id=1, source_target_pairs={{0,16},{16,0},{32,48},{48,32},{64,80},{80,64},{96,112},{112,96},{1... | collective-permute-start | bytes 61448 | tf_op jit(solution)/shard_map/ppermute | solution.py:462

commit v11 on v10

--- a/solution.py
+++ b/solution.py
@@ -139,7 +139,7 @@
     )(*operands)
 
 
-def eliminate(gram, upper_ref, inverse_ref, work, other, beside):
+def eliminate(gram, upper_ref, inverse_ref, work, other, stash, beside):
     width = upper_ref.shape[0]
     full = (STEP, width)
     lane = lax.broadcasted_iota(jnp.int32, full, 1)
@@ -150,10 +150,12 @@
         a_rows = [jnp.broadcast_to(work[first + k : first + k + 1, :], full) for k in range(STEP)]
         x_rows = [jnp.broadcast_to(other[first + k : first + k + 1, :], full) for k in range(STEP)]
         entry, mult, inv = {}, {}, {}
+        pivot = work[first : first + STEP, :]
+        for k in range(STEP):
+            stash[k] = jnp.broadcast_to(pivot[:, first + k : first + k + 1], full)
         for i in range(STEP):
             for k in range(i + 1):
-                column = a_rows[i][:, first + k : first + k + 1]
-                entry[i, k] = jnp.broadcast_to(column, full)
+                entry[i, k] = jnp.broadcast_to(stash[k, i : i + 1, :], full)
         for k in range(STEP):
             inv[k] = 1.0 / entry[k, k]
             for i in range(k + 1, STEP):
@@ -191,7 +193,7 @@
 
 
 def product_kernel(piece, share, parts_ref, mob_ref, upper_ref, inverse_ref, out_ref, *refs):
-    work, other, rhs, held, found, sems = refs
+    work, other, stash, rhs, held, found, sems = refs
     width = parts_ref.shape[2]
     count = sems.shape[0]
     tile = held.shape[0] // count
@@ -217,7 +219,7 @@
         low_part = exact_dot(low, rhs[:, :width], NN)
         found[rows, :] = wide[:, :width] + wide[:, width:] + low_part
 
-    eliminate(unpack(parts_ref, piece), upper_ref, inverse_ref, work, other, beside)
+    eliminate(unpack(parts_ref, piece), upper_ref, inverse_ref, work, other, stash, beside)
     image = exact_dot(left_terms(found[...]), right_terms(inverse_ref[...]), NT)
     image = image + jnp.where(lax.axis_index("col") == 0, held[:, :width], 0.0)
     out_ref[:, :piece, :] = image.reshape(out_ref.shape[0], piece, width)
@@ -241,6 +243,7 @@
         scratch_shapes=[
             pltpu.VMEM((width, width), jnp.float32),
             pltpu.VMEM((width, width), jnp.float32),
+            pltpu.VMEM((STEP, STEP, width), jnp.float32),
             pltpu.VMEM((n_cols, 2 * width), jnp.bfloat16),
             pltpu.VMEM(mobility.shape, jnp.float32),
             pltpu.VMEM((n_rows, width), jnp.float32),

time: 112 us -> 111 us (level)
  Pallas kernels: 17.4 us -> 16 us
    pallas_call x1, Pallas kernels: 6.86 us -> 5.45 us  [factor_and_product(): pl.pallas_call(lambda *refs: product_kernel(piece, share, *refs), in_spec...]
where the time goes in v11:
time: 111 us; the launch traced here: 110 us
  blocking collectives  42.1 us (38%)
  starting transfers between devices  32.2 us (29%)
  waiting for transfers between devices  18.8 us (17%)
  Pallas kernels  16 us (14%)
    all_gather x1, blocking collectives, on_device(): panel_parts = lax.all_gather(sent, 'row', axis=0)  23.2 us
    all_gather x1, blocking collectives, on_device(): lax.all_gather(join(turned_image, keep, came, mobility), 'row', axis=0)  18.9 us
    all_to_all x1, waiting for transfers between devices, on_device(): got = lax.all_to_all(sent, 'col', 0, 0)  10.3 us
    all_to_all x1, starting transfers between devices, on_device(): lax.all_to_all(copies(panel, n_col), 'col', 0, 0).reshape(block_rows, width)  7.6 us
    all_to_all x1, waiting for transfers between devices, on_device(): lax.all_to_all(copies(panel, n_col), 'col', 0, 0).reshape(block_rows, width)  5.91 us
    pallas_call x1, Pallas kernels, factor_and_product(): pl.pallas_call(lambda *refs: product_kernel(piece, share, *refs), in_spec...  5.45 us
    all_to_all x1, starting transfers between devices, on_device(): got = lax.all_to_all(sent, 'col', 0, 0)  5.1 us
    ppermute x1, starting transfers between devices, on_device(): turned_image = lax.ppermute(image, BOTH, transposing)  5.03 us
  transfers between devices with their start and end apart: 7, of which 5 were waited for; matrix products, arithmetic and copies ran while one was open for 0% of the time, Pallas kernels for 4%

profile of v11, /device:TPU:1, one launch (start us, length us, event | category | flops | bytes accessed | tf_op | source)
XLA Modules:
  0.0 109.9 jit_solution(6070063394074856675)
XLA Ops:
  0.6 1.6 %copies.1 = f32[16,64,128]{2,1,0:T(8,128)} custom-call(f32[64,128]{1,0:T(8,128)} %rows_ref.1), custom_call_target="tpu_custom_call" | custom-call | bytes 600000 | tf_op jit(solution)/shard_map/copies/pallas_call | solution.py:269
  2.2 7.6 %all-to-all-start = ((f32[16,64,128]{2,1,0:T(8,128)}), f32[16,64,128]{2,1,0:T(8,128)S(1)}, u32[]{:S(2)}, u32[]{:S(2)}) async-start(f32[16,64,128]{2,1,0:T(8,128)} %copies.1), calls=%async_computation | async-start | bytes 1048576 | tf_op jit(solution)/shard_map/all_to_all | solution.py:436
  9.9 4.4 %collective-permute-start = (f32[64,128]{1,0:T(8,128)}, f32[64,128]{1,0:T(8,128)S(1)}, u32[]{:S(2)}, u32[]{:S(2)}) collective-permute-start(f32[64,128]{1,0:T(8,128)} %rows_ref.1), channel_id=1, source_target_pairs={{0,0},{1,16},{2,32},{3,48},{4,64},{5,80},{6,96},{7,112},{8,128},{9... | collective-permute-start | bytes 98312 | tf_op jit(solution)/shard_map/ppermute | solution.py:435
  14.2 5.9 %all-to-all-done = f32[16,64,128]{2,1,0:T(8,128)S(1)} async-done(((f32[16,64,128]{2,1,0:T(8,128)}), f32[16,64,128]{2,1,0:T(8,128)S(1)}, u32[]{:S(2)}, u32[]{:S(2)}) %all-to-all-start) | async-done | bytes 524320 | tf_op jit(solution)/shard_map/all_to_all | solution.py:436
  20.2 0.7 gram_parts.1
  20.9 0.0 collective-permute-done
  20.9 2.2 %collective-permute-start.1 = (f32[40,128]{1,0:T(8,128)S(1)}, f32[40,128]{1,0:T(8,128)S(1)}, u32[]{:S(2)}, u32[]{:S(2)}) collective-permute-start(f32[40,128]{1,0:T(8,128)S(1)} %get-tuple-element.24), channel_id=1, source_target_pairs={{0,16},{16,0},{32,48},{48,32},{64,80},{80,64},{96,112},{112,96},{1... | collective-permute-start | bytes 61448 | tf_op jit(solution)/shard_map/ppermute | solution.py:441
  23.1 0.8 collective-permute-done.1
  24.0 23.2 %all-gather = f32[1664,128]{1,0:T(8,128)S(1)} all-gather(f32[104,128]{1,0:T(8,128)S(1)} %pad_maximum_fusion), channel_id=2, replica_groups=mesh['row'=16,'col'=16] {'row'}, dimensions={0}, use_global_device_ids=true | all-gather | bytes 905216 | tf_op jit(solution)/shard_map/all_gather | solution.py:445
  47.2 5.4 %factor_and_product.1 = (f32[128,128]{1,0:T(8,128)}, f32[128,128]{1,0:T(8,128)S(1)}, f32[16,72,128]{2,1,0:T(8,128)}) custom-call(f32[16,104,128]{2,1,0:T(8,128)S(1)} %bitcast.4, f32[1024,1024]{1,0:T(8,128)} %refs_4_.1), custom_call_target="tpu_custom_call" | custom-call | flops 805306368 | bytes 6000000 | tf_op jit(solution)/shard_map/factor_and_product/pallas_call | solution.py:234
  52.6 5.1 %all-to-all-start.1 = ((f32[16,72,128]{2,1,0:T(8,128)}), f32[16,72,128]{2,1,0:T(8,128)S(1)}, u32[]{:S(2)}, u32[]{:S(2)}) async-start(f32[16,72,128]{2,1,0:T(8,128)} %get-tuple-element.26), calls=%async_computation.1 | async-start | bytes 1179648 | tf_op jit(solution)/shard_map/all_to_all | solution.py:448
  57.8 0.5 basis_rows.1.refs_2_.turned_ref
  58.2 10.3 %all-to-all-done.1.refs_0_ = f32[16,72,128]{2,1,0:T(8,128)S(1)} async-done(((f32[16,72,128]{2,1,0:T(8,128)}), f32[16,72,128]{2,1,0:T(8,128)S(1)}, u32[]{:S(2)}, u32[]{:S(2)}) %all-to-all-start.1) | async-done | bytes 589856 | tf_op jit(solution)/shard_map/all_to_all | solution.py:448
  68.5 0.9 image_piece.1
  69.4 4.3 %all-to-all-start.2 = ((f32[16,64,128]{2,1,0:T(8,128)}), f32[16,64,128]{2,1,0:T(8,128)S(1)}, u32[]{:S(2)}, u32[]{:S(2)}) async-start(f32[16,64,128]{2,1,0:T(8,128)} %get-tuple-element.31), calls=%async_computation.2 | async-start | bytes 1048576 | tf_op jit(solution)/shard_map/all_to_all | solution.py:455
  73.7 5.0 %collective-permute-start.2 = (f32[64,128]{1,0:T(8,128)S(1)}, f32[64,128]{1,0:T(8,128)S(1)}, u32[]{:S(2)}, u32[]{:S(2)}) collective-permute-start(f32[64,128]{1,0:T(8,128)S(1)} %get-tuple-element.29), channel_id=1, source_target_pairs={{0,0},{1,16},{2,32},{3,48},{4,64},{5,80},{6,96},{7,112},{8,128},{9... | collective-permute-start | bytes 98312 | tf_op jit(solution)/shard_map/ppermute | solution.py:454
  78.7 2.9 %kernel.1 = (bf16[1024,256]{1,0:T(8,128)(2,1)S(1)}, bf16[1024,256]{1,0:T(8,128)(2,1)S(1)}) custom-call(f32[128,128]{1,0:T(8,128)S(1)} %get-tuple-element.27.inverse_ref.refs_0_, f32[128,128]{1,0:T(8,128)S(1)} %get-tuple-element.32.refs_1_, f32[128,1024]{1,0:T(8,128)S(1)} %basis_rows.1.refs_2_.turned_ref, f32[16,104,128]{2,1,0:T(8,128)S(1)} %bitcast.5), custom_call_target="tpu_custom_call" | custom-call | flops 300000000 | bytes 10000000 | tf_op jit(solution)/shard_map/kernel/pallas_call | solution.py:367
  81.7 1.0 all-to-all-done.2
  82.6 0.0 copy-start
  82.6 0.7 inner_parts.1
  83.4 3.6 %collective-permute-start.3 = (f32[40,128]{1,0:T(8,128)S(1)}, f32[40,128]{1,0:T(8,128)S(1)}, u32[]{:S(2)}, u32[]{:S(2)}) collective-permute-start(f32[40,128]{1,0:T(8,128)S(1)} %get-tuple-element.36), channel_id=1, source_target_pairs={{0,16},{16,0},{32,48},{48,32},{64,80},{80,64},{96,112},{112,96},{1... | collective-permute-start | bytes 61448 | tf_op jit(solution)/shard_map/ppermute | solution.py:465
  86.9 0.0 collective-permute-done.2.lone_ref
  86.9 0.8 collective-permute-done.3.came_ref
  87.8 18.9 %all-gather.1 = f32[1664,128]{1,0:T(8,128)S(1)} all-gather(f32[104,128]{1,0:T(8,128)S(1)} %join.1), channel_id=3, replica_groups=mesh['row'=16,'col'=16] {'row'}, dimensions={0}, use_global_device_ids=true | all-gather | bytes 905216 | tf_op jit(solution)/shard_map/all_gather | solution.py:466
  106.7 0.0 copy-done
  106.7 3.2 %update.1 = f32[1024,1024]{1,0:T(8,128)} custom-call(f32[16,104,128]{2,1,0:T(8,128)S(1)} %bitcast.10, f32[1024,128]{1,0:T(8,128)S(1)} %bitcast.9, bf16[1024,256]{1,0:T(8,128)(2,1)S(1)} %get-tuple-element.37.refs_2_, bf16[1024,256]{1,0:T(8,128)(2,1)S(1)} %get-tuple-element.38.refs_3_, f32[1024,1024]{1,0:T(8,128)S(1)} %copy-done), custom_call_target="tpu_custom_call" | custom-call | flops 1610612736 | bytes 9000000 | tf_op jit(solution)/shard_map/update/pallas_call | solution.py:408
  (5 shorter events, 0.0 us)
Async XLA Ops:
  2.2 17.9 %all-to-all-start = ((f32[16,64,128]{2,1,0:T(8,128)}), f32[16,64,128]{2,1,0:T(8,128)S(1)}, u32[]{:S(2)}, u32[]{:S(2)}) async-start(f32[16,64,128]{2,1,0:T(8,128)} %copies.1), calls=%async_computation | async-start | bytes 1048576 | tf_op jit(solution)/shard_map/all_to_all | solution.py:436
  9.9 11.0 %collective-permute-start = (f32[64,128]{1,0:T(8,128)}, f32[64,128]{1,0:T(8,128)S(1)}, u32[]{:S(2)}, u32[]{:S(2)}) collective-permute-start(f32[64,128]{1,0:T(8,128)} %rows_ref.1), channel_id=1, source_target_pairs={{0,0},{1,16},{2,32},{3,48},{4,64},{5,80},{6,96},{7,112},{8,128},{9... | collective-permute-start | bytes 98312 | tf_op jit(solution)/shard_map/ppermute | solution.py:435
  20.9 3.1 %collective-permute-start.1 = (f32[40,128]{1,0:T(8,128)S(1)}, f32[40,128]{1,0:T(8,128)S(1)}, u32[]{:S(2)}, u32[]{:S(2)}) collective-permute-start(f32[40,128]{1,0:T(8,128)S(1)} %get-tuple-element.24), channel_id=1, source_target_pairs={{0,16},{16,0},{32,48},{48,32},{64,80},{80,64},{96,112},{112,96},{1... | collective-permute-start | bytes 61448 | tf_op jit(solution)/shard_map/ppermute | solution.py:441
  52.6 15.9 %all-to-all-start.1 = ((f32[16,72,128]{2,1,0:T(8,128)}), f32[16,72,128]{2,1,0:T(8,128)S(1)}, u32[]{:S(2)}, u32[]{:S(2)}) async-start(f32[16,72,128]{2,1,0:T(8,128)} %get-tuple-element.26), calls=%async_computation.1 | async-start | bytes 1179648 | tf_op jit(solution)/shard_map/all_to_all | solution.py:448
  69.4 13.2 %all-to-all-start.2 = ((f32[16,64,128]{2,1,0:T(8,128)}), f32[16,64,128]{2,1,0:T(8,128)S(1)}, u32[]{:S(2)}, u32[]{:S(2)}) async-start(f32[16,64,128]{2,1,0:T(8,128)} %get-tuple-element.31), calls=%async_computation.2 | async-start | bytes 1048576 | tf_op jit(solution)/shard_map/all_to_all | solution.py:455
  73.7 13.3 %collective-permute-start.2 = (f32[64,128]{1,0:T(8,128)S(1)}, f32[64,128]{1,0:T(8,128)S(1)}, u32[]{:S(2)}, u32[]{:S(2)}) collective-permute-start(f32[64,128]{1,0:T(8,128)S(1)} %get-tuple-element.29), channel_id=1, source_target_pairs={{0,0},{1,16},{2,32},{3,48},{4,64},{5,80},{6,96},{7,112},{8,128},{9... | collective-permute-start | bytes 98312 | tf_op jit(solution)/shard_map/ppermute | solution.py:454
  82.6 24.1 %copy-start = (f32[1024,1024]{1,0:T(8,128)S(1)}, f32[1024,1024]{1,0:T(8,128)}, u32[]{:S(2)}) copy-start(f32[1024,1024]{1,0:T(8,128)} %refs_4_.1) | copy-start | bytes 12582916
  83.4 4.4 %collective-permute-start.3 = (f32[40,128]{1,0:T(8,128)S(1)}, f32[40,128]{1,0:T(8,128)S(1)}, u32[]{:S(2)}, u32[]{:S(2)}) collective-permute-start(f32[40,128]{1,0:T(8,128)S(1)} %get-tuple-element.36), channel_id=1, source_target_pairs={{0,16},{16,0},{32,48},{48,32},{64,80},{80,64},{96,112},{112,96},{1... | collective-permute-start | bytes 61448 | tf_op jit(solution)/shard_map/ppermute | solution.py:465

commit v12 on v11

--- a/solution.py
+++ b/solution.py
@@ -437,7 +437,7 @@
     keep, give, top_part = packed_parts(
         gram_kernel, (panel_rows,), [(share, width)], "gram_parts"
     )
-    give, turned_panel = lax.optimization_barrier((give, turned_panel))
+    keep, turned_panel = lax.optimization_barrier((keep, turned_panel))
     packed = keep + lax.ppermute(give, "row", swap)
     even = lax.axis_index("row") % 2 == 0
     tail = jnp.where(even, top_part, packed[-STEP:])

time: 111 us -> 109 us (0.982)
    all_to_all x1, starting transfers between devices: 5.1 us -> 3.94 us  [on_device(): got = lax.all_to_all(sent, 'col', 0, 0)]
where the time goes in v12:
time: 109 us
  blocking collectives  42.1 us (39%)
  starting transfers between devices  31.1 us (29%)
  waiting for transfers between devices  18.8 us (17%)
  Pallas kernels  16 us (15%)
    all_gather x1, blocking collectives, on_device(): panel_parts = lax.all_gather(sent, 'row', axis=0)  23.2 us
    all_gather x1, blocking collectives, on_device(): lax.all_gather(join(turned_image, keep, came, mobility), 'row', axis=0)  18.9 us
    all_to_all x1, waiting for transfers between devices, on_device(): got = lax.all_to_all(sent, 'col', 0, 0)  10.3 us
    all_to_all x1, starting transfers between devices, on_device(): lax.all_to_all(copies(panel, n_col), 'col', 0, 0).reshape(block_rows, width)  7.6 us
    all_to_all x1, waiting for transfers between devices, on_device(): lax.all_to_all(copies(panel, n_col), 'col', 0, 0).reshape(block_rows, width)  5.91 us
    pallas_call x1, Pallas kernels, factor_and_product(): pl.pallas_call(lambda *refs: product_kernel(piece, share, *refs), in_spec...  5.45 us
    ppermute x1, starting transfers between devices, on_device(): turned_image = lax.ppermute(image, BOTH, transposing)  5.03 us
    ppermute x1, starting transfers between devices, on_device(): turned_panel = lax.ppermute(panel, BOTH, transposing)  4.38 us
  transfers between devices with their start and end apart: 7, of which 5 were waited for; matrix products, arithmetic and copies ran while one was open for 0% of the time, Pallas kernels for 4%

profile of v12, /device:TPU:1, one launch (start us, length us, event | category | flops | bytes accessed | tf_op | source)
XLA Modules:
  0.0 108.8 jit_solution(11738372391455241312)
XLA Ops:
  0.6 1.6 %copies.1 = f32[16,64,128]{2,1,0:T(8,128)} custom-call(f32[64,128]{1,0:T(8,128)} %rows_ref.1), custom_call_target="tpu_custom_call" | custom-call | bytes 600000 | tf_op jit(solution)/shard_map/copies/pallas_call | solution.py:269
  2.2 7.6 %all-to-all-start = ((f32[16,64,128]{2,1,0:T(8,128)}), f32[16,64,128]{2,1,0:T(8,128)S(1)}, u32[]{:S(2)}, u32[]{:S(2)}) async-start(f32[16,64,128]{2,1,0:T(8,128)} %copies.1), calls=%async_computation | async-start | bytes 1048576 | tf_op jit(solution)/shard_map/all_to_all | solution.py:436
  9.9 4.4 %collective-permute-start = (f32[64,128]{1,0:T(8,128)}, f32[64,128]{1,0:T(8,128)S(1)}, u32[]{:S(2)}, u32[]{:S(2)}) collective-permute-start(f32[64,128]{1,0:T(8,128)} %rows_ref.1), channel_id=1, source_target_pairs={{0,0},{1,16},{2,32},{3,48},{4,64},{5,80},{6,96},{7,112},{8,128},{9... | collective-permute-start | bytes 98312 | tf_op jit(solution)/shard_map/ppermute | solution.py:435
  14.2 5.9 %all-to-all-done = f32[16,64,128]{2,1,0:T(8,128)S(1)} async-done(((f32[16,64,128]{2,1,0:T(8,128)}), f32[16,64,128]{2,1,0:T(8,128)S(1)}, u32[]{:S(2)}, u32[]{:S(2)}) %all-to-all-start) | async-done | bytes 524320 | tf_op jit(solution)/shard_map/all_to_all | solution.py:436
  20.2 0.7 gram_parts.1
  20.9 2.2 %collective-permute-start.1 = (f32[40,128]{1,0:T(8,128)S(1)}, f32[40,128]{1,0:T(8,128)S(1)}, u32[]{:S(2)}, u32[]{:S(2)}) collective-permute-start(f32[40,128]{1,0:T(8,128)S(1)} %get-tuple-element.24), channel_id=1, source_target_pairs={{0,16},{16,0},{32,48},{48,32},{64,80},{80,64},{96,112},{112,96},{1... | collective-permute-start | bytes 61448 | tf_op jit(solution)/shard_map/ppermute | solution.py:441
  23.1 0.0 collective-permute-done
  23.1 0.8 collective-permute-done.1
  24.0 23.2 %all-gather = f32[1664,128]{1,0:T(8,128)S(1)} all-gather(f32[104,128]{1,0:T(8,128)S(1)} %pad_maximum_fusion), channel_id=2, replica_groups=mesh['row'=16,'col'=16] {'row'}, dimensions={0}, use_global_device_ids=true | all-gather | bytes 905216 | tf_op jit(solution)/shard_map/all_gather | solution.py:445
  47.2 5.5 %factor_and_product.1 = (f32[128,128]{1,0:T(8,128)}, f32[128,128]{1,0:T(8,128)S(1)}, f32[16,72,128]{2,1,0:T(8,128)}) custom-call(f32[16,104,128]{2,1,0:T(8,128)S(1)} %bitcast.4, f32[1024,1024]{1,0:T(8,128)} %refs_4_.1), custom_call_target="tpu_custom_call" | custom-call | flops 805306368 | bytes 6000000 | tf_op jit(solution)/shard_map/factor_and_product/pallas_call | solution.py:234
  52.6 3.9 %all-to-all-start.1 = ((f32[16,72,128]{2,1,0:T(8,128)}), f32[16,72,128]{2,1,0:T(8,128)S(1)}, u32[]{:S(2)}, u32[]{:S(2)}) async-start(f32[16,72,128]{2,1,0:T(8,128)} %get-tuple-element.26), calls=%async_computation.1 | async-start | bytes 1179648 | tf_op jit(solution)/shard_map/all_to_all | solution.py:448
  56.6 0.5 basis_rows.1.refs_2_.turned_ref
  57.1 10.3 %all-to-all-done.1.refs_0_ = f32[16,72,128]{2,1,0:T(8,128)S(1)} async-done(((f32[16,72,128]{2,1,0:T(8,128)}), f32[16,72,128]{2,1,0:T(8,128)S(1)}, u32[]{:S(2)}, u32[]{:S(2)}) %all-to-all-start.1) | async-done | bytes 589856 | tf_op jit(solution)/shard_map/all_to_all | solution.py:448
  67.3 0.9 image_piece.1
  68.2 4.3 %all-to-all-start.2 = ((f32[16,64,128]{2,1,0:T(8,128)}), f32[16,64,128]{2,1,0:T(8,128)S(1)}, u32[]{:S(2)}, u32[]{:S(2)}) async-start(f32[16,64,128]{2,1,0:T(8,128)} %get-tuple-element.31), calls=%async_computation.2 | async-start | bytes 1048576 | tf_op jit(solution)/shard_map/all_to_all | solution.py:455
  72.5 5.0 %collective-permute-start.2 = (f32[64,128]{1,0:T(8,128)S(1)}, f32[64,128]{1,0:T(8,128)S(1)}, u32[]{:S(2)}, u32[]{:S(2)}) collective-permute-start(f32[64,128]{1,0:T(8,128)S(1)} %get-tuple-element.29), channel_id=1, source_target_pairs={{0,0},{1,16},{2,32},{3,48},{4,64},{5,80},{6,96},{7,112},{8,128},{9... | collective-permute-start | bytes 98312 | tf_op jit(solution)/shard_map/ppermute | solution.py:454
  77.5 2.9 %kernel.1 = (bf16[1024,256]{1,0:T(8,128)(2,1)S(1)}, bf16[1024,256]{1,0:T(8,128)(2,1)S(1)}) custom-call(f32[128,128]{1,0:T(8,128)S(1)} %get-tuple-element.27.inverse_ref.refs_0_, f32[128,128]{1,0:T(8,128)S(1)} %get-tuple-element.32.refs_1_, f32[128,1024]{1,0:T(8,128)S(1)} %basis_rows.1.refs_2_.turned_ref, f32[16,104,128]{2,1,0:T(8,128)S(1)} %bitcast.5), custom_call_target="tpu_custom_call" | custom-call | flops 300000000 | bytes 10000000 | tf_op jit(solution)/shard_map/kernel/pallas_call | solution.py:367
  80.5 1.0 all-to-all-done.2
  81.5 0.0 copy-start
  81.5 0.7 inner_parts.1
  82.2 3.6 %collective-permute-start.3 = (f32[40,128]{1,0:T(8,128)S(1)}, f32[40,128]{1,0:T(8,128)S(1)}, u32[]{:S(2)}, u32[]{:S(2)}) collective-permute-start(f32[40,128]{1,0:T(8,128)S(1)} %get-tuple-element.36), channel_id=1, source_target_pairs={{0,16},{16,0},{32,48},{48,32},{64,80},{80,64},{96,112},{112,96},{1... | collective-permute-start | bytes 61448 | tf_op jit(solution)/shard_map/ppermute | solution.py:465
  85.8 0.0 collective-permute-done.2.lone_ref
  85.8 0.8 collective-permute-done.3.came_ref
  86.6 18.9 %all-gather.1 = f32[1664,128]{1,0:T(8,128)S(1)} all-gather(f32[104,128]{1,0:T(8,128)S(1)} %join.1), channel_id=3, replica_groups=mesh['row'=16,'col'=16] {'row'}, dimensions={0}, use_global_device_ids=true | all-gather | bytes 905216 | tf_op jit(solution)/shard_map/all_gather | solution.py:466
  105.6 0.0 copy-done
  105.6 3.2 %update.1 = f32[1024,1024]{1,0:T(8,128)} custom-call(f32[16,104,128]{2,1,0:T(8,128)S(1)} %bitcast.10, f32[1024,128]{1,0:T(8,128)S(1)} %bitcast.9, bf16[1024,256]{1,0:T(8,128)(2,1)S(1)} %get-tuple-element.37.refs_2_, bf16[1024,256]{1,0:T(8,128)(2,1)S(1)} %get-tuple-element.38.refs_3_, f32[1024,1024]{1,0:T(8,128)S(1)} %copy-done), custom_call_target="tpu_custom_call" | custom-call | flops 1610612736 | bytes 9000000 | tf_op jit(solution)/shard_map/update/pallas_call | solution.py:408
  (5 shorter events, 0.0 us)
Async XLA Ops:
  2.2 17.9 %all-to-all-start = ((f32[16,64,128]{2,1,0:T(8,128)}), f32[16,64,128]{2,1,0:T(8,128)S(1)}, u32[]{:S(2)}, u32[]{:S(2)}) async-start(f32[16,64,128]{2,1,0:T(8,128)} %copies.1), calls=%async_computation | async-start | bytes 1048576 | tf_op jit(solution)/shard_map/all_to_all | solution.py:436
  9.9 13.3 %collective-permute-start = (f32[64,128]{1,0:T(8,128)}, f32[64,128]{1,0:T(8,128)S(1)}, u32[]{:S(2)}, u32[]{:S(2)}) collective-permute-start(f32[64,128]{1,0:T(8,128)} %rows_ref.1), channel_id=1, source_target_pairs={{0,0},{1,16},{2,32},{3,48},{4,64},{5,80},{6,96},{7,112},{8,128},{9... | collective-permute-start | bytes 98312 | tf_op jit(solution)/shard_map/ppermute | solution.py:435
  20.9 3.1 %collective-permute-start.1 = (f32[40,128]{1,0:T(8,128)S(1)}, f32[40,128]{1,0:T(8,128)S(1)}, u32[]{:S(2)}, u32[]{:S(2)}) collective-permute-start(f32[40,128]{1,0:T(8,128)S(1)} %get-tuple-element.24), channel_id=1, source_target_pairs={{0,16},{16,0},{32,48},{48,32},{64,80},{80,64},{96,112},{112,96},{1... | collective-permute-start | bytes 61448 | tf_op jit(solution)/shard_map/ppermute | solution.py:441
  52.6 14.7 %all-to-all-start.1 = ((f32[16,72,128]{2,1,0:T(8,128)}), f32[16,72,128]{2,1,0:T(8,128)S(1)}, u32[]{:S(2)}, u32[]{:S(2)}) async-start(f32[16,72,128]{2,1,0:T(8,128)} %get-tuple-element.26), calls=%async_computation.1 | async-start | bytes 1179648 | tf_op jit(solution)/shard_map/all_to_all | solution.py:448
  68.2 13.2 %all-to-all-start.2 = ((f32[16,64,128]{2,1,0:T(8,128)}), f32[16,64,128]{2,1,0:T(8,128)S(1)}, u32[]{:S(2)}, u32[]{:S(2)}) async-start(f32[16,64,128]{2,1,0:T(8,128)} %get-tuple-element.31), calls=%async_computation.2 | async-start | bytes 1048576 | tf_op jit(solution)/shard_map/all_to_all | solution.py:455
  72.5 13.3 %collective-permute-start.2 = (f32[64,128]{1,0:T(8,128)S(1)}, f32[64,128]{1,0:T(8,128)S(1)}, u32[]{:S(2)}, u32[]{:S(2)}) collective-permute-start(f32[64,128]{1,0:T(8,128)S(1)} %get-tuple-element.29), channel_id=1, source_target_pairs={{0,0},{1,16},{2,32},{3,48},{4,64},{5,80},{6,96},{7,112},{8,128},{9... | collective-permute-start | bytes 98312 | tf_op jit(solution)/shard_map/ppermute | solution.py:454
  81.5 24.1 %copy-start = (f32[1024,1024]{1,0:T(8,128)S(1)}, f32[1024,1024]{1,0:T(8,128)}, u32[]{:S(2)}) copy-start(f32[1024,1024]{1,0:T(8,128)} %refs_4_.1) | copy-start | bytes 12582916
  82.2 4.4 %collective-permute-start.3 = (f32[40,128]{1,0:T(8,128)S(1)}, f32[40,128]{1,0:T(8,128)S(1)}, u32[]{:S(2)}, u32[]{:S(2)}) collective-permute-start(f32[40,128]{1,0:T(8,128)S(1)} %get-tuple-element.36), channel_id=1, source_target_pairs={{0,16},{16,0},{32,48},{48,32},{64,80},{80,64},{96,112},{112,96},{1... | collective-permute-start | bytes 61448 | tf_op jit(solution)/shard_map/ppermute | solution.py:465

commit v13 on v12

--- a/solution.py
+++ b/solution.py
@@ -209,8 +209,8 @@
     )
 
     def beside(index):
-        k = index // 3 - 1
-        if index % 3 or not 0 <= k < count:
+        k = index // 2 - 4
+        if index % 2 or not 0 <= k < count:
             return
         loads[k].wait()
         rows = slice(k * tile, (k + 1) * tile)

time: 109 us -> 109 us (level)
  transfers between devices with their start and end apart: 7 -> 7, of which waited for: 5 -> 5; matrix products, arithmetic and copies ran while one was open for 0% -> 0% of each run, Pallas kernels for 4% -> 5%
where the time goes in v13:
time: 109 us; the launch traced here: 108 us
  blocking collectives  42.1 us (39%)
  starting transfers between devices  31.1 us (29%)
  waiting for transfers between devices  18.8 us (17%)
  Pallas kernels  15.5 us (14%)
    all_gather x1, blocking collectives, on_device(): panel_parts = lax.all_gather(sent, 'row', axis=0)  23.2 us
    all_gather x1, blocking collectives, on_device(): lax.all_gather(join(turned_image, keep, came, mobility), 'row', axis=0)  18.9 us
    all_to_all x1, waiting for transfers between devices, on_device(): got = lax.all_to_all(sent, 'col', 0, 0)  10.3 us
    all_to_all x1, starting transfers between devices, on_device(): lax.all_to_all(copies(panel, n_col), 'col', 0, 0).reshape(block_rows, width)  7.6 us
    all_to_all x1, waiting for transfers between devices, on_device(): lax.all_to_all(copies(panel, n_col), 'col', 0, 0).reshape(block_rows, width)  5.91 us
    ppermute x1, starting transfers between devices, on_device(): turned_image = lax.ppermute(image, BOTH, transposing)  5.03 us
    pallas_call x1, Pallas kernels, factor_and_product(): pl.pallas_call(lambda *refs: product_kernel(piece, share, *refs), in_spec...  4.9 us
    ppermute x1, starting transfers between devices, on_device(): turned_panel = lax.ppermute(panel, BOTH, transposing)  4.38 us
  transfers between devices with their start and end apart: 7, of which 5 were waited for; matrix products, arithmetic and copies ran while one was open for 0% of the time, Pallas kernels for 5%

profile of v13, /device:TPU:1, one launch (start us, length us, event | category | flops | bytes accessed | tf_op | source)
XLA Modules:
  0.0 108.2 jit_solution(7406946294011207552)
XLA Ops:
  0.6 1.6 %copies.1 = f32[16,64,128]{2,1,0:T(8,128)} custom-call(f32[64,128]{1,0:T(8,128)} %rows_ref.1), custom_call_target="tpu_custom_call" | custom-call | bytes 600000 | tf_op jit(solution)/shard_map/copies/pallas_call | solution.py:269
  2.2 7.6 %all-to-all-start = ((f32[16,64,128]{2,1,0:T(8,128)}), f32[16,64,128]{2,1,0:T(8,128)S(1)}, u32[]{:S(2)}, u32[]{:S(2)}) async-start(f32[16,64,128]{2,1,0:T(8,128)} %copies.1), calls=%async_computation | async-start | bytes 1048576 | tf_op jit(solution)/shard_map/all_to_all | solution.py:436
  9.9 4.4 %collective-permute-start = (f32[64,128]{1,0:T(8,128)}, f32[64,128]{1,0:T(8,128)S(1)}, u32[]{:S(2)}, u32[]{:S(2)}) collective-permute-start(f32[64,128]{1,0:T(8,128)} %rows_ref.1), channel_id=1, source_target_pairs={{0,0},{1,16},{2,32},{3,48},{4,64},{5,80},{6,96},{7,112},{8,128},{9... | collective-permute-start | bytes 98312 | tf_op jit(solution)/shard_map/ppermute | solution.py:435
  14.2 5.9 %all-to-all-done = f32[16,64,128]{2,1,0:T(8,128)S(1)} async-done(((f32[16,64,128]{2,1,0:T(8,128)}), f32[16,64,128]{2,1,0:T(8,128)S(1)}, u32[]{:S(2)}, u32[]{:S(2)}) %all-to-all-start) | async-done | bytes 524320 | tf_op jit(solution)/shard_map/all_to_all | solution.py:436
  20.2 0.7 gram_parts.1
  20.9 2.2 %collective-permute-start.1 = (f32[40,128]{1,0:T(8,128)S(1)}, f32[40,128]{1,0:T(8,128)S(1)}, u32[]{:S(2)}, u32[]{:S(2)}) collective-permute-start(f32[40,128]{1,0:T(8,128)S(1)} %get-tuple-element.24), channel_id=1, source_target_pairs={{0,16},{16,0},{32,48},{48,32},{64,80},{80,64},{96,112},{112,96},{1... | collective-permute-start | bytes 61448 | tf_op jit(solution)/shard_map/ppermute | solution.py:441
  23.1 0.0 collective-permute-done
  23.1 0.8 collective-permute-done.1
  24.0 23.2 %all-gather = f32[1664,128]{1,0:T(8,128)S(1)} all-gather(f32[104,128]{1,0:T(8,128)S(1)} %pad_maximum_fusion), channel_id=2, replica_groups=mesh['row'=16,'col'=16] {'row'}, dimensions={0}, use_global_device_ids=true | all-gather | bytes 905216 | tf_op jit(solution)/shard_map/all_gather | solution.py:445
  47.2 4.9 %factor_and_product.1 = (f32[128,128]{1,0:T(8,128)}, f32[128,128]{1,0:T(8,128)S(1)}, f32[16,72,128]{2,1,0:T(8,128)}) custom-call(f32[16,104,128]{2,1,0:T(8,128)S(1)} %bitcast.4, f32[1024,1024]{1,0:T(8,128)} %refs_4_.1), custom_call_target="tpu_custom_call" | custom-call | flops 805306368 | bytes 6000000 | tf_op jit(solution)/shard_map/factor_and_product/pallas_call | solution.py:234
  52.1 3.9 %all-to-all-start.1 = ((f32[16,72,128]{2,1,0:T(8,128)}), f32[16,72,128]{2,1,0:T(8,128)S(1)}, u32[]{:S(2)}, u32[]{:S(2)}) async-start(f32[16,72,128]{2,1,0:T(8,128)} %get-tuple-element.26), calls=%async_computation.1 | async-start | bytes 1179648 | tf_op jit(solution)/shard_map/all_to_all | solution.py:448
  56.0 0.5 basis_rows.1.refs_2_.turned_ref
  56.5 10.3 %all-to-all-done.1.refs_0_ = f32[16,72,128]{2,1,0:T(8,128)S(1)} async-done(((f32[16,72,128]{2,1,0:T(8,128)}), f32[16,72,128]{2,1,0:T(8,128)S(1)}, u32[]{:S(2)}, u32[]{:S(2)}) %all-to-all-start.1) | async-done | bytes 589856 | tf_op jit(solution)/shard_map/all_to_all | solution.py:448
  66.8 0.9 image_piece.1
  67.7 4.3 %all-to-all-start.2 = ((f32[16,64,128]{2,1,0:T(8,128)}), f32[16,64,128]{2,1,0:T(8,128)S(1)}, u32[]{:S(2)}, u32[]{:S(2)}) async-start(f32[16,64,128]{2,1,0:T(8,128)} %get-tuple-element.31), calls=%async_computation.2 | async-start | bytes 1048576 | tf_op jit(solution)/shard_map/all_to_all | solution.py:455
  72.0 5.0 %collective-permute-start.2 = (f32[64,128]{1,0:T(8,128)S(1)}, f32[64,128]{1,0:T(8,128)S(1)}, u32[]{:S(2)}, u32[]{:S(2)}) collective-permute-start(f32[64,128]{1,0:T(8,128)S(1)} %get-tuple-element.29), channel_id=1, source_target_pairs={{0,0},{1,16},{2,32},{3,48},{4,64},{5,80},{6,96},{7,112},{8,128},{9... | collective-permute-start | bytes 98312 | tf_op jit(solution)/shard_map/ppermute | solution.py:454
  77.0 2.9 %kernel.1 = (bf16[1024,256]{1,0:T(8,128)(2,1)S(1)}, bf16[1024,256]{1,0:T(8,128)(2,1)S(1)}) custom-call(f32[128,128]{1,0:T(8,128)S(1)} %get-tuple-element.27.inverse_ref.refs_0_, f32[128,128]{1,0:T(8,128)S(1)} %get-tuple-element.32.refs_1_, f32[128,1024]{1,0:T(8,128)S(1)} %basis_rows.1.refs_2_.turned_ref, f32[16,104,128]{2,1,0:T(8,128)S(1)} %bitcast.5), custom_call_target="tpu_custom_call" | custom-call | flops 300000000 | bytes 10000000 | tf_op jit(solution)/shard_map/kernel/pallas_call | solution.py:367
  79.9 1.0 all-to-all-done.2
  80.9 0.0 copy-start
  80.9 0.7 inner_parts.1
  81.6 3.6 %collective-permute-start.3 = (f32[40,128]{1,0:T(8,128)S(1)}, f32[40,128]{1,0:T(8,128)S(1)}, u32[]{:S(2)}, u32[]{:S(2)}) collective-permute-start(f32[40,128]{1,0:T(8,128)S(1)} %get-tuple-element.36), channel_id=1, source_target_pairs={{0,16},{16,0},{32,48},{48,32},{64,80},{80,64},{96,112},{112,96},{1... | collective-permute-start | bytes 61448 | tf_op jit(solution)/shard_map/ppermute | solution.py:465
  85.2 0.0 collective-permute-done.2.lone_ref
  85.2 0.8 collective-permute-done.3.came_ref
  86.1 18.9 %all-gather.1 = f32[1664,128]{1,0:T(8,128)S(1)} all-gather(f32[104,128]{1,0:T(8,128)S(1)} %join.1), channel_id=3, replica_groups=mesh['row'=16,'col'=16] {'row'}, dimensions={0}, use_global_device_ids=true | all-gather | bytes 905216 | tf_op jit(solution)/shard_map/all_gather | solution.py:466
  105.0 0.0 copy-done
  105.0 3.2 %update.1 = f32[1024,1024]{1,0:T(8,128)} custom-call(f32[16,104,128]{2,1,0:T(8,128)S(1)} %bitcast.10, f32[1024,128]{1,0:T(8,128)S(1)} %bitcast.9, bf16[1024,256]{1,0:T(8,128)(2,1)S(1)} %get-tuple-element.37.refs_2_, bf16[1024,256]{1,0:T(8,128)(2,1)S(1)} %get-tuple-element.38.refs_3_, f32[1024,1024]{1,0:T(8,128)S(1)} %copy-done), custom_call_target="tpu_custom_call" | custom-call | flops 1610612736 | bytes 9000000 | tf_op jit(solution)/shard_map/update/pallas_call | solution.py:408
  (5 shorter events, 0.0 us)
Async XLA Ops:
  2.2 17.9 %all-to-all-start = ((f32[16,64,128]{2,1,0:T(8,128)}), f32[16,64,128]{2,1,0:T(8,128)S(1)}, u32[]{:S(2)}, u32[]{:S(2)}) async-start(f32[16,64,128]{2,1,0:T(8,128)} %copies.1), calls=%async_computation | async-start | bytes 1048576 | tf_op jit(solution)/shard_map/all_to_all | solution.py:436
  9.9 13.3 %collective-permute-start = (f32[64,128]{1,0:T(8,128)}, f32[64,128]{1,0:T(8,128)S(1)}, u32[]{:S(2)}, u32[]{:S(2)}) collective-permute-start(f32[64,128]{1,0:T(8,128)} %rows_ref.1), channel_id=1, source_target_pairs={{0,0},{1,16},{2,32},{3,48},{4,64},{5,80},{6,96},{7,112},{8,128},{9... | collective-permute-start | bytes 98312 | tf_op jit(solution)/shard_map/ppermute | solution.py:435
  20.9 3.1 %collective-permute-start.1 = (f32[40,128]{1,0:T(8,128)S(1)}, f32[40,128]{1,0:T(8,128)S(1)}, u32[]{:S(2)}, u32[]{:S(2)}) collective-permute-start(f32[40,128]{1,0:T(8,128)S(1)} %get-tuple-element.24), channel_id=1, source_target_pairs={{0,16},{16,0},{32,48},{48,32},{64,80},{80,64},{96,112},{112,96},{1... | collective-permute-start | bytes 61448 | tf_op jit(solution)/shard_map/ppermute | solution.py:441
  52.1 14.7 %all-to-all-start.1 = ((f32[16,72,128]{2,1,0:T(8,128)}), f32[16,72,128]{2,1,0:T(8,128)S(1)}, u32[]{:S(2)}, u32[]{:S(2)}) async-start(f32[16,72,128]{2,1,0:T(8,128)} %get-tuple-element.26), calls=%async_computation.1 | async-start | bytes 1179648 | tf_op jit(solution)/shard_map/all_to_all | solution.py:448
  67.7 13.2 %all-to-all-start.2 = ((f32[16,64,128]{2,1,0:T(8,128)}), f32[16,64,128]{2,1,0:T(8,128)S(1)}, u32[]{:S(2)}, u32[]{:S(2)}) async-start(f32[16,64,128]{2,1,0:T(8,128)} %get-tuple-element.31), calls=%async_computation.2 | async-start | bytes 1048576 | tf_op jit(solution)/shard_map/all_to_all | solution.py:455
  72.0 13.3 %collective-permute-start.2 = (f32[64,128]{1,0:T(8,128)S(1)}, f32[64,128]{1,0:T(8,128)S(1)}, u32[]{:S(2)}, u32[]{:S(2)}) collective-permute-start(f32[64,128]{1,0:T(8,128)S(1)} %get-tuple-element.29), channel_id=1, source_target_pairs={{0,0},{1,16},{2,32},{3,48},{4,64},{5,80},{6,96},{7,112},{8,128},{9... | collective-permute-start | bytes 98312 | tf_op jit(solution)/shard_map/ppermute | solution.py:454
  80.9 24.1 %copy-start = (f32[1024,1024]{1,0:T(8,128)S(1)}, f32[1024,1024]{1,0:T(8,128)}, u32[]{:S(2)}) copy-start(f32[1024,1024]{1,0:T(8,128)} %refs_4_.1) | copy-start | bytes 12582916
  81.6 4.4 %collective-permute-start.3 = (f32[40,128]{1,0:T(8,128)S(1)}, f32[40,128]{1,0:T(8,128)S(1)}, u32[]{:S(2)}, u32[]{:S(2)}) collective-permute-start(f32[40,128]{1,0:T(8,128)S(1)} %get-tuple-element.36), channel_id=1, source_target_pairs={{0,16},{16,0},{32,48},{48,32},{64,80},{80,64},{96,112},{112,96},{1... | collective-permute-start | bytes 61448 | tf_op jit(solution)/shard_map/ppermute | solution.py:465
